TPU v7x, 512 devices: a whole 4x8x8 slice. The times are simulated.
512 devices in a mesh: row: 16 (over z, core), col: 32 (over y, x).
Axes of the slice: x: 4, y: 8, z: 8, core: 2. Of those that a mesh axis runs over, the one named last changes fastest.
Arguments:
- tokens: bfloat16 [4096, 2560], P('row', 'col'), may hold values from -6 to 6
- w_down: bfloat16 [2560, 1056], P('col'), may hold values from -0.125 to 0.125
- q_gain: float32 [768], replicated, may hold values from 0.1 to 1.9
- kv_gain: float32 [256], replicated, may hold values from 0.1 to 1.9
- w_q_up: bfloat16 [768, 3072], P(None, 'col'), may hold values from -8.8767604 to 8.8767604
- w_kv_up: bfloat16 [256, 4096], replicated, may hold values from -0.375 to 0.375
- w_out: bfloat16 [2048, 2560], P('col'), may hold values from -0.75 to 0.75
- latent_cache: bfloat16 [16, 8192, 288], P('row', 'col'), may hold values from -6 to 6
- cache_len: int32 [16], replicated, may hold values from 1 to 8192, as said below
- new_len: int32 [16], replicated, may hold values from 1 to 256, as said below
- page_table: int32 [16, 128], replicated, may hold values from 0 to 127, each once within a row
- home_slot: int32 [16], replicated, may hold values from 0 to 15, each once
Outputs:
- output: bfloat16 [4096, 2560], P('row', 'col')
Inputs may be any that keep to these rules, and one draw needn't show every extreme that they name: `cache_len`: some slot has exactly 8192 cached tokens; about half the slots hold at most 1024, the others at least 7168. `new_len`: some request has exactly 256 real new tokens.
All inputs are finite; a program needn't handle non-finite values.
Results may differ from a plain program's by a relative error of at most 0.023.
Values may be sent and summed in bfloat16 or wider, within the bound.
A program may use at most 64 MiB of HBM per device.

v0:
```python
import math

import jax
import jax.numpy as jnp
from jax import lax
from jax.sharding import PartitionSpec as P

NOPE = 64
ROPE = 32
VDIM = 64


epsilon = 1e-05


def rms_scale(values, gain):
    return values * lax.rsqrt(jnp.mean(values * values, axis=-1, keepdims=True) + epsilon) * gain


def angle_tables(positions, width):
    half_dim = width // 2
    frequency = 10000.0 ** (-2.0 * jnp.arange(half_dim, dtype=jnp.float32) / width)
    angles = positions.astype(jnp.float32)[:, None] * frequency[None, :]
    return (jnp.cos(angles), jnp.sin(angles))


def rotary(values, cosine, sine_table):
    half_dim = values.shape[-1] // 2
    first_half = values[..., :half_dim]
    second_half = values[..., half_dim:]
    return jnp.concatenate(
        [
            first_half * cosine - second_half * sine_table,
            second_half * cosine + first_half * sine_table,
        ],
        -1,
    )


def body(
    tokens,
    w_down,
    q_gain,
    kv_gain,
    w_q_up,
    w_kv_up,
    w_out,
    latent_cache,
    cache_len,
    new_len,
    page_table,
    home_slot,
):
    columns = lax.axis_size("col")
    column_id = lax.axis_index("col")
    row_id = lax.axis_index("row")
    group_rows = tokens.shape[0]
    own_rows = group_rows // columns
    q_width = q_gain.shape[0]
    kv_width = kv_gain.shape[0]
    slot_index = home_slot[row_id]
    cached_count = cache_len[slot_index]
    live_count = new_len[row_id]
    combined = lax.psum_scatter(
        jnp.dot(tokens, w_down, preferred_element_type=jnp.float32),
        "col",
        scatter_dimension=0,
        tiled=True,
    )
    own_position = cached_count + column_id * own_rows + jnp.arange(own_rows, dtype=jnp.int32)
    own_cos, own_sin = angle_tables(own_position, ROPE)
    query_latent = rms_scale(combined[:, :q_width], q_gain).astype(jnp.bfloat16)
    new_latent = rms_scale(combined[:, q_width : q_width + kv_width], kv_gain).astype(jnp.bfloat16)
    new_rope = rotary(combined[:, q_width + kv_width :], own_cos, own_sin).astype(jnp.bfloat16)
    new_rows = jnp.concatenate([new_latent, new_rope], 1)
    projected = jnp.dot(
        lax.all_gather(query_latent, "col", axis=0, tiled=True),
        w_q_up,
        preferred_element_type=jnp.float32,
    )
    query_cos, query_sin = angle_tables(
        cached_count + jnp.arange(group_rows, dtype=jnp.int32), ROPE
    )
    queries = jnp.concatenate(
        [projected[:, :NOPE], rotary(projected[:, NOPE:], query_cos, query_sin)], 1
    ).astype(jnp.bfloat16)
    segment = lax.all_gather(latent_cache, "row", axis=0, tiled=True)
    matches = jnp.arange(segment.shape[0], dtype=jnp.int32) == slot_index
    own_cache = jnp.sum(
        jnp.where(matches[:, None, None], segment.astype(jnp.float32), 0.0), 0
    ).astype(jnp.bfloat16)
    head_width = NOPE + VDIM
    head_weight = lax.dynamic_slice_in_dim(w_kv_up, column_id * head_width, head_width, 1)

    def expand(latents):
        lifted = jnp.dot(
            latents[:, :kv_width], head_weight, preferred_element_type=jnp.float32
        ).astype(jnp.bfloat16)
        return (jnp.concatenate([lifted[:, :NOPE], latents[:, kv_width:]], 1), lifted[:, NOPE:])

    cache_latents, fresh_latents = (
        lax.all_gather(own_cache, "col", axis=0, tiled=True),
        lax.all_gather(new_rows, "col", axis=0, tiled=True),
    )
    cache_keys, cache_values = expand(cache_latents)
    fresh_keys, fresh_values = expand(fresh_latents)
    key_total = cache_keys.shape[0]
    page_row = page_table[slot_index]
    page_count = page_row.shape[0]
    page_size = key_total // page_count
    block_size = min(512, key_total)
    offsets = jnp.arange(page_size, dtype=jnp.int32)
    page_ids = jnp.arange(page_count, dtype=jnp.int32)
    logical_page = jnp.sum(
        page_ids[:, None] * (page_row[:, None] == page_ids[None, :]).astype(jnp.int32), 0
    )
    cached_visible = (logical_page[:, None] * page_size + offsets[None, :]).reshape(
        key_total
    ) < cached_count
    block_limit = key_total // block_size
    score_scale = 1.0 / math.sqrt(NOPE + ROPE)
    query_index = jnp.arange(group_rows, dtype=jnp.int32)[:, None]
    key_index = jnp.arange(group_rows, dtype=jnp.int32)[None, :]
    fresh_visible = (key_index <= query_index) & (key_index < live_count)
    fresh_scores = (
        jnp.einsum("qd,kd->qk", queries, fresh_keys, preferred_element_type=jnp.float32)
        * score_scale
    )
    fresh_scores = jnp.where(fresh_visible, fresh_scores, -jnp.inf)
    first_peak = jnp.max(fresh_scores, 1)
    fresh_exponent = jnp.exp(fresh_scores - first_peak[:, None])
    start_state = (
        first_peak,
        jnp.sum(fresh_exponent, 1),
        jnp.dot(
            fresh_exponent.astype(jnp.bfloat16), fresh_values, preferred_element_type=jnp.float32
        ),
    )

    def accumulate(block_id, running):
        row_peak, row_total, summed = running
        key_block = lax.dynamic_slice_in_dim(cache_keys, block_id * block_size, block_size, 0)
        mask_block = lax.dynamic_slice_in_dim(cached_visible, block_id * block_size, block_size, 0)
        value_block = lax.dynamic_slice_in_dim(cache_values, block_id * block_size, block_size, 0)
        raw_scores = (
            jnp.einsum("qd,kd->qk", queries, key_block, preferred_element_type=jnp.float32)
            * score_scale
        )
        raw_scores = jnp.where(mask_block[None, :], raw_scores, -jnp.inf)
        next_peak = jnp.maximum(row_peak, jnp.max(raw_scores, 1))
        factor = jnp.exp(row_peak - next_peak)
        exponent = jnp.exp(raw_scores - next_peak[:, None])
        next_total = row_total * factor + jnp.sum(exponent, 1)
        next_summed = summed * factor[:, None] + jnp.dot(
            exponent.astype(jnp.bfloat16), value_block, preferred_element_type=jnp.float32
        )
        return (next_peak, next_total, next_summed)

    row_peak, row_total, summed = lax.fori_loop(0, block_limit, accumulate, start_state)
    attended = (summed / row_total[:, None]).astype(jnp.bfloat16)
    live_rows = jnp.arange(group_rows, dtype=jnp.int32) < live_count
    attended = jnp.where(live_rows[:, None], attended, jnp.zeros_like(attended))
    summed_out = lax.psum_scatter(
        lax.dot_general(
            w_out, attended, (((0,), (1,)), ((), ())), preferred_element_type=jnp.float32
        ).astype(jnp.bfloat16),
        "col",
        scatter_dimension=0,
        tiled=True,
    ).astype(jnp.float32)
    result = summed_out.T.astype(jnp.bfloat16)
    return result


def solution(mesh):
    return jax.shard_map(
        body,
        mesh=mesh,
        in_specs=(
            P("row", "col"),
            P("col", None),
            P(),
            P(),
            P(None, "col"),
            P(),
            P("col", None),
            P("row", "col", None),
            P(),
            P(),
            P(),
            P(),
        ),
        out_specs=P("row", "col"),
        check_vma=False,
    )
```

profile of v0, /device:TPU:6, one launch (start us, length us, event | category | flops | bytes accessed | tf_op | source)
XLA Modules:
  0.0 534.6 jit_solution(15060410855748943424)
XLA Ops:
  7.4 0.7 all-gather.3.cloned.1.call-update
  8.1 2.3 fusion.51
  10.6 0.7 dynamic_slice.37
  11.2 0.7 iota_compare_fusion.3
  11.9 46.4 %all-gather.3.cloned.1.call-done = bf16[16,256,288]{1,2,0:T(8,128)(2,1)} async-done(((bf16[1,256,288]{1,2,0:T(8,128)(2,1)}), bf16[16,256,288]{1,2,0:T(8,128)(2,1)}) %all-gather.3.cloned.1.call-update) | async-done | bytes 2359312 | tf_op jit(solution)/shard_map/all_gather | solution.py:87
  58.3 2.9 select_reduce_fusion
  62.6 0.6 dynamic_slice.36
  63.9 0.7 dynamic_slice.38
  65.3 0.7 dynamic-slice_bitcast_fusion
  66.1 0.8 add_compare_fusion
  67.0 1.3 dynamic-slice
  68.9 0.6 iota_compare_fusion.2
  69.5 0.7 add_convert_fusion
  70.2 105.4 %all-reduce.3.cloned.1.call-done = f32[256,1056]{1,0:T(8,128)} async-done(((f32[256,1056]{1,0:T(8,128)}), f32[256,1056]{1,0:T(8,128)}) %all-reduce.3.cloned.1.call-update) | async-done | bytes 1081360
  175.6 0.9 multiply_reduce_fusion.1
  176.5 0.9 fusion.41
  177.3 0.8 multiply_convert_fusion.1
  178.2 45.1 %all_gather.13 = bf16[256,288]{1,0:T(8,128)(2,1)S(1)} all-gather(bf16[8,288]{1,0:T(8,128)(2,1)S(1)} %pad_maximum_fusion.2), channel_id=1, replica_groups=mesh['row'=16,'col'=32] {'col'}, dimensions={0}, use_global_device_ids=true | all-gather | bytes 152064 | tf_op jit(solution)/shard_map/all_gather | solution.py:103
  223.4 0.2 convolution_convert_fusion.2
  223.7 0.9 multiply_reduce_fusion
  224.5 0.8 multiply_convert_fusion
  225.3 47.5 %all_gather.12 = bf16[256,768]{1,0:T(8,128)(2,1)S(1)} all-gather(bf16[8,768]{1,0:T(8,128)(2,1)S(1)} %multiply_convert_fusion), channel_id=1, replica_groups=mesh['row'=16,'col'=32] {'col'}, dimensions={0}, use_global_device_ids=true | all-gather | bytes 405504 | tf_op jit(solution)/shard_map/all_gather | solution.py:77
  272.8 0.3 fusion.52
  273.4 0.3 fusion.50
  273.7 0.2 fusion.15
  273.9 3.0 convolution_convert_fusion
  277.0 0.9 slice-done
  277.9 1.3 pad_maximum_fusion
  279.1 26.9 %while.17 = (s32[]{:T(128)}, f32[256]{0:T(256)S(1)}, f32[256]{0:T(256)S(1)}, f32[256,64]{0,1:T(8,128)S(1)}, pred[8192]{0:T(1024)(128)(4,1)S(1)}, /*index=5*/bf16...) while((s32[]{:T(128)}, f32[256]{0:T(256)S(1)}, ...), condition=%wide.region_10.11_spmd, body=%wide.region_7.10_spmd.sunk | while | flops 42893828 | bytes 1935023 | solution.py:159
  279.2 1.2 fusion.67
  280.6 0.2 convolution_add_fusion.2
  280.9 1.2 fusion.67
  282.2 0.2 convolution_add_fusion.2
  282.6 1.2 fusion.67
  283.9 0.2 convolution_add_fusion.2
  284.3 1.2 fusion.67
  285.6 0.2 convolution_add_fusion.2
  286.0 1.2 fusion.67
  287.3 0.2 convolution_add_fusion.2
  287.6 1.2 fusion.67
  289.0 0.2 convolution_add_fusion.2
  289.3 1.2 fusion.67
  290.7 0.2 convolution_add_fusion.2
  291.0 1.2 fusion.67
  292.3 0.2 convolution_add_fusion.2
  292.7 1.2 fusion.67
  294.0 0.2 convolution_add_fusion.2
  294.4 1.2 fusion.67
  295.7 0.2 convolution_add_fusion.2
  296.1 1.2 fusion.67
  297.4 0.2 convolution_add_fusion.2
  297.8 1.2 fusion.67
  299.1 0.2 convolution_add_fusion.2
  299.4 1.2 fusion.67
  300.8 0.2 convolution_add_fusion.2
  301.1 1.2 fusion.67
  302.5 0.2 convolution_add_fusion.2
  302.8 1.2 fusion.67
  304.1 0.2 convolution_add_fusion.2
  304.5 1.2 fusion.67
  305.8 0.2 convolution_add_fusion.2
  306.1 1.5 fusion.10
  307.6 1.5 copy.43
  309.1 217.9 %reduce-scatter.4.cloned.1.call-done = bf16[80,256]{1,0:T(8,128)(2,1)} async-done(((bf16[2560,256]{1,0:T(8,128)(2,1)}), bf16[80,256]{1,0:T(8,128)(2,1)}) %reduce-scatter.4.cloned.1.call-update) | async-done | bytes 40976
  (120 shorter events, 4.8 us)
Async XLA Ops:
  7.4 216.0 %copy-start = (bf16[256,4096]{1,0:T(8,128)(2,1)S(1)}, bf16[256,4096]{1,0:T(8,128)(2,1)}, u32[]{:S(2)}) copy-start(bf16[256,4096]{1,0:T(8,128)(2,1)} %param.19) | copy-start | bytes 6291460
  7.4 3.2 copy-start.4
  7.4 50.9 %all-gather.3.cloned.1.call-start = ((), (), s32[]{:S(2)}) async-start(), calls=%async_computation.1 | async-start | bytes 2506752 | tf_op jit(solution)/shard_map/all_gather | solution.py:87
  8.1 167.5 %all-reduce.3.cloned.1.call-start = ((), (), s32[]{:S(2)}) async-start(), calls=%async_computation.4 | async-start | bytes 2359296
  10.5 52.2 %copy-start.5 = (s32[16]{0:T(128)S(1)}, s32[16]{0:T(128)}, u32[]{:S(2)}) copy-start(s32[16]{0:T(128)} %param.23) | copy-start | bytes 196
  10.5 53.5 %copy-start.6 = (s32[16]{0:T(128)S(1)}, s32[16]{0:T(128)}, u32[]{:S(2)}) copy-start(s32[16]{0:T(128)} %param.22) | copy-start | bytes 196
  10.5 166.9 %copy-start.3 = (f32[256]{0:T(256)S(1)}, f32[256]{0:T(256)}, u32[]{:S(2)}) copy-start(f32[256]{0:T(256)} %param.17) | copy-start | bytes 3076
  10.5 214.0 %copy-start.2 = (f32[768]{0:T(1024)S(1)}, f32[768]{0:T(1024)}, u32[]{:S(2)}) copy-start(f32[768]{0:T(1024)} %param.16) | copy-start | bytes 9220
  10.5 262.3 %copy-start.1 = (bf16[768,96]{0,1:T(8,128)(2,1)S(1)}, bf16[768,96]{0,1:T(8,128)(2,1)}, u32[]{:S(2)}) copy-start(bf16[768,96]{0,1:T(8,128)(2,1)} %param.18) | copy-start | bytes 442372
  10.5 263.4 %all-gather.5.cloned.1.call-start = ((), (), s32[]{:S(2)}) async-start(), calls=%async_computation.2 | async-start | bytes 4866048 | tf_op jit(solution)/shard_map/all_gather | solution.py:102
  61.2 465.8 %reduce-scatter.4.cloned.1.call-start = ((), (), s32[]{:S(2)}) async-start(), calls=%async_computation.3 | async-start | bytes 1351680
  276.8 1.0 slice-start
Sparse Core Ops, SparseCore 0:
  10.3 47.9 all-gather.2
Sparse Core Ops, SparseCore 1:
  12.0 163.5 all-reduce.2
  178.5 92.0 all-gather.4
  309.2 217.8 reduce-scatter.3
where the time goes:
time: 536 us; the launch traced here: 535 us
  waiting for transfers between devices  370 us (69%)
  blocking collectives  92.6 us (17%)
  matrix products  30.2 us (6%)
  between operations  18.6 us (3%)
  other arithmetic  13.9 us (3%)
  local copies, waits for them, and re-layouts  8.05 us (2%)
    unnamed x6, waiting for transfers between devices  324 us
    all_gather x1, blocking collectives, body(): lax.all_gather(query_latent, 'col', axis=0, tiled=True)  47.5 us
    all_gather x1, waiting for transfers between devices, body(): segment = lax.all_gather(latent_cache, 'row', axis=0, tiled=True)  46.4 us
    all_gather x1, blocking collectives, body(): lax.all_gather(new_rows, 'col', axis=0, tiled=True)  45.1 us
    dot_general x16, matrix products, accumulate(): jnp.einsum('qd,kd->qk', queries, key_block, preferred_element_type=jnp.fl...  18.8 us
  transfers between devices with their start and end apart: 4, of which 3 were waited for; matrix products, arithmetic and copies ran while one was open for 3% of the time, Pallas kernels for 0%

commit v1 on v0

--- a/solution.py
+++ b/solution.py
@@ -61,26 +61,17 @@
     slot_index = home_slot[row_id]
     cached_count = cache_len[slot_index]
     live_count = new_len[row_id]
-    combined = lax.psum_scatter(
-        jnp.dot(tokens, w_down, preferred_element_type=jnp.float32),
-        "col",
-        scatter_dimension=0,
-        tiled=True,
-    )
-    own_position = cached_count + column_id * own_rows + jnp.arange(own_rows, dtype=jnp.int32)
-    own_cos, own_sin = angle_tables(own_position, ROPE)
-    query_latent = rms_scale(combined[:, :q_width], q_gain).astype(jnp.bfloat16)
-    new_latent = rms_scale(combined[:, q_width : q_width + kv_width], kv_gain).astype(jnp.bfloat16)
-    new_rope = rotary(combined[:, q_width + kv_width :], own_cos, own_sin).astype(jnp.bfloat16)
-    new_rows = jnp.concatenate([new_latent, new_rope], 1)
-    projected = jnp.dot(
-        lax.all_gather(query_latent, "col", axis=0, tiled=True),
-        w_q_up,
-        preferred_element_type=jnp.float32,
+    combined = lax.psum(
+        jnp.dot(tokens, w_down, preferred_element_type=jnp.float32), "col"
     )
     query_cos, query_sin = angle_tables(
         cached_count + jnp.arange(group_rows, dtype=jnp.int32), ROPE
     )
+    query_latent = rms_scale(combined[:, :q_width], q_gain).astype(jnp.bfloat16)
+    new_latent = rms_scale(combined[:, q_width : q_width + kv_width], kv_gain).astype(jnp.bfloat16)
+    new_rope = rotary(combined[:, q_width + kv_width :], query_cos, query_sin).astype(jnp.bfloat16)
+    fresh_latents = jnp.concatenate([new_latent, new_rope], 1)
+    projected = jnp.dot(query_latent, w_q_up, preferred_element_type=jnp.float32)
     queries = jnp.concatenate(
         [projected[:, :NOPE], rotary(projected[:, NOPE:], query_cos, query_sin)], 1
     ).astype(jnp.bfloat16)
@@ -98,10 +89,7 @@
         ).astype(jnp.bfloat16)
         return (jnp.concatenate([lifted[:, :NOPE], latents[:, kv_width:]], 1), lifted[:, NOPE:])
 
-    cache_latents, fresh_latents = (
-        lax.all_gather(own_cache, "col", axis=0, tiled=True),
-        lax.all_gather(new_rows, "col", axis=0, tiled=True),
-    )
+    cache_latents = lax.all_gather(own_cache, "col", axis=0, tiled=True)
     cache_keys, cache_values = expand(cache_latents)
     fresh_keys, fresh_values = expand(fresh_latents)
     key_total = cache_keys.shape[0]

time: 536 us -> 533 us (level)
  blocking collectives: 92.6 us -> 0 us
  waiting for transfers between devices: 370 us -> 462 us
    psum x0 -> x1, waiting for transfers between devices: none -> 108 us  [body(): lax.psum(jnp.dot(tokens, w_down, preferred_element_type=jnp.float32), 'col')]
    unnamed x6 -> x5, waiting for transfers between devices: 324 us -> 220 us
    all_gather x2 -> x0, blocking collectives: 92.6 us -> none  [the longest x1 47.5 us: body(): lax.all_gather(query_latent, 'col', axis=0, tiled=True)]
    all_gather x1, waiting for transfers between devices: 0.01 us -> 87.4 us  [body(): cache_latents = lax.all_gather(own_cache, 'col', axis=0, tiled=True)]
  transfers between devices with their start and end apart: 4 -> 4, of which waited for: 3 -> 4; matrix products, arithmetic and copies ran while one was open for 3% -> 3% of each run, Pallas kernels for 0% -> 0%
where the time goes in v1:
time: 533 us; the launch traced here: 531 us
  waiting for transfers between devices  462 us (87%)
  matrix products  32.4 us (6%)
  between operations  17.1 us (3%)
  other arithmetic  12.4 us (2%)
  local copies, waits for them, and re-layouts  6.62 us (1%)
    unnamed x5, waiting for transfers between devices  220 us
    psum x1, waiting for transfers between devices, body(): lax.psum(jnp.dot(tokens, w_down, preferred_element_type=jnp.float32), 'col')  108 us
    all_gather x1, waiting for transfers between devices, body(): cache_latents = lax.all_gather(own_cache, 'col', axis=0, tiled=True)  87.4 us
    all_gather x1, waiting for transfers between devices, body(): segment = lax.all_gather(latent_cache, 'row', axis=0, tiled=True)  46.5 us
    dot_general x16, matrix products, accumulate(): jnp.einsum('qd,kd->qk', queries, key_block, preferred_element_type=jnp.fl...  18.8 us
  transfers between devices with their start and end apart: 4, of which 4 were waited for; matrix products, arithmetic and copies ran while one was open for 3% of the time, Pallas kernels for 0%

profile of v1, /device:TPU:6, one launch (start us, length us, event | category | flops | bytes accessed | tf_op | source)
XLA Modules:
  0.0 531.3 jit_solution(8802280258935113749)
XLA Ops:
  7.4 0.7 all-gather.3.cloned.1.call-update
  8.1 2.3 fusion.57
  10.6 0.6 dynamic_slice.37
  11.2 0.6 iota_compare_fusion.3
  11.8 46.5 %all-gather.3.cloned.1.call-done = bf16[16,256,288]{1,2,0:T(8,128)(2,1)} async-done(((bf16[1,256,288]{1,2,0:T(8,128)(2,1)}), bf16[16,256,288]{1,2,0:T(8,128)(2,1)}) %all-gather.3.cloned.1.call-update) | async-done | bytes 2359312 | tf_op jit(solution)/shard_map/all_gather | solution.py:78
  58.3 2.9 select_reduce_fusion
  62.5 0.6 dynamic_slice.36
  63.8 0.6 dynamic_slice.38
  64.4 0.7 dynamic-slice_bitcast_fusion
  65.2 0.7 add_compare_fusion
  66.1 0.6 iota_compare_fusion.2
  66.7 0.6 add_convert_fusion
  67.4 107.9 %all-reduce.2.cloned.1.call-done = f32[256,1056]{0,1:T(8,128)} async-done(((f32[256,1056]{0,1:T(8,128)}), f32[256,1056]{0,1:T(8,128)}) %all-reduce.2.cloned.1.call-update) | async-done | bytes 1081360 | tf_op jit(solution)/shard_map/psum | solution.py:64
  175.2 1.0 multiply_reduce_fusion.1
  176.3 1.2 convolution_convert_fusion.2
  177.5 1.3 multiply_reduce_fusion
  178.8 1.4 fusion.12
  180.2 0.9 fusion.42
  181.2 0.3 fusion.56
  181.6 0.2 fusion.18
  181.7 87.4 %all-gather.5.cloned.1.call-done = bf16[8192,288]{0,1:T(8,128)(2,1)} async-done(((bf16[256,288]{0,1:T(8,128)(2,1)}), bf16[8192,288]{0,1:T(8,128)(2,1)}) %all-gather.5.cloned.1.call-update) | async-done | bytes 4718608 | tf_op jit(solution)/shard_map/all_gather | solution.py:92
  269.1 3.0 convolution_convert_fusion
  272.1 0.1 fusion.55
  272.3 0.9 slice-done
  273.1 1.3 pad_maximum_fusion
  274.4 26.9 %while.17 = (s32[]{:T(128)}, f32[256]{0:T(256)S(1)}, f32[256]{0:T(256)S(1)}, f32[256,64]{0,1:T(8,128)S(1)}, pred[8192]{0:T(1024)(128)(4,1)S(1)}, /*index=5*/bf16...) while((s32[]{:T(128)}, f32[256]{0:T(256)S(1)}, ...), condition=%wide.region_10.11_spmd, body=%wide.region_7.10_spmd.sunk | while | flops 42893828 | bytes 1935023 | solution.py:147
  274.5 1.2 fusion.71
  275.7 0.1 fusion.72
  275.8 0.2 convolution_add_fusion.2
  276.2 1.2 fusion.71
  277.5 0.2 convolution_add_fusion.2
  277.8 1.2 fusion.71
  279.2 0.2 convolution_add_fusion.2
  279.5 1.2 fusion.71
  280.9 0.2 convolution_add_fusion.2
  281.2 1.2 fusion.71
  282.5 0.2 convolution_add_fusion.2
  282.9 1.2 fusion.71
  284.2 0.2 convolution_add_fusion.2
  284.6 1.2 fusion.71
  285.9 0.2 convolution_add_fusion.2
  286.3 1.2 fusion.71
  287.6 0.2 convolution_add_fusion.2
  288.0 1.2 fusion.71
  289.3 0.2 convolution_add_fusion.2
  289.6 1.2 fusion.71
  291.0 0.2 convolution_add_fusion.2
  291.3 1.2 fusion.71
  292.7 0.2 convolution_add_fusion.2
  293.0 1.2 fusion.71
  294.2 0.1 fusion.72
  294.3 0.2 convolution_add_fusion.2
  294.7 1.2 fusion.71
  296.0 0.2 convolution_add_fusion.2
  296.4 1.2 fusion.71
  297.6 0.1 fusion.72
  297.7 0.2 convolution_add_fusion.2
  298.1 1.2 fusion.71
  299.4 0.2 convolution_add_fusion.2
  299.7 1.2 fusion.71
  301.1 0.2 convolution_add_fusion.2
  301.3 1.5 fusion.10
  302.8 1.5 copy.29
  304.3 219.4 %reduce-scatter.4.cloned.1.call-done = bf16[80,256]{1,0:T(8,128)(2,1)} async-done(((bf16[2560,256]{1,0:T(8,128)(2,1)}), bf16[80,256]{1,0:T(8,128)(2,1)}) %reduce-scatter.4.cloned.1.call-update) | async-done | bytes 40976
  (110 shorter events, 3.9 us)
Async XLA Ops:
  7.4 168.9 %copy-start = (bf16[256,4096]{1,0:T(8,128)(2,1)S(1)}, bf16[256,4096]{1,0:T(8,128)(2,1)}, u32[]{:S(2)}) copy-start(bf16[256,4096]{1,0:T(8,128)(2,1)} %param.19) | copy-start | bytes 6291460
  7.4 3.2 copy-start.4
  7.4 50.9 %all-gather.3.cloned.1.call-start = ((), (), s32[]{:S(2)}) async-start(), calls=%async_computation.2 | async-start | bytes 2506752 | tf_op jit(solution)/shard_map/all_gather | solution.py:78
  8.1 167.1 %all-reduce.2.cloned.1.call-start = ((), (), s32[]{:S(2)}) async-start(), calls=%async_computation.1 | async-start | bytes 2162688 | tf_op jit(solution)/shard_map/psum | solution.py:64
  10.5 52.1 %copy-start.5 = (s32[16]{0:T(128)S(1)}, s32[16]{0:T(128)}, u32[]{:S(2)}) copy-start(s32[16]{0:T(128)} %param.23) | copy-start | bytes 196
  10.5 53.4 %copy-start.6 = (s32[16]{0:T(128)S(1)}, s32[16]{0:T(128)}, u32[]{:S(2)}) copy-start(s32[16]{0:T(128)} %param.22) | copy-start | bytes 196
  10.5 165.8 %copy-start.3 = (f32[256]{0:T(256)S(1)}, f32[256]{0:T(256)}, u32[]{:S(2)}) copy-start(f32[256]{0:T(256)} %param.17) | copy-start | bytes 3076
  10.5 258.7 %all-gather.5.cloned.1.call-start = ((), (), s32[]{:S(2)}) async-start(), calls=%async_computation.3 | async-start | bytes 4866048 | tf_op jit(solution)/shard_map/all_gather | solution.py:92
  11.8 166.9 %copy-start.1 = (bf16[768,96]{0,1:T(8,128)(2,1)S(1)}, bf16[768,96]{0,1:T(8,128)(2,1)}, u32[]{:S(2)}) copy-start(bf16[768,96]{0,1:T(8,128)(2,1)} %param.18) | copy-start | bytes 442372
  11.8 166.9 %copy-start.2 = (f32[768]{0:T(1024)S(1)}, f32[768]{0:T(1024)}, u32[]{:S(2)}) copy-start(f32[768]{0:T(1024)} %param.16) | copy-start | bytes 9220
  61.2 462.5 %reduce-scatter.4.cloned.1.call-start = ((), (), s32[]{:S(2)}) async-start(), calls=%async_computation.4 | async-start | bytes 1351680
  272.1 1.0 slice-start
Sparse Core Ops, SparseCore 0:
  10.3 47.9 all-gather.2
Sparse Core Ops, SparseCore 1:
  12.0 163.2 all-reduce.1
  178.2 90.9 all-gather.4
  304.4 219.2 reduce-scatter.3

commit v2 on v1

--- a/solution.py
+++ b/solution.py
@@ -1,9 +1,14 @@
+import functools
 import math
 
 import jax
 import jax.numpy as jnp
 from jax import lax
+from jax.experimental import pallas as pl
+from jax.experimental.pallas import tpu as pltpu
 from jax.sharding import PartitionSpec as P
+
+MESH = pl.DeviceIdType.MESH
 
 NOPE = 64
 ROPE = 32
@@ -35,6 +40,58 @@
         ],
         -1,
     )
+
+
+def _exchange_kernel(n, axis, gather, x_ref, y_ref, send_sem, recv_sem):
+    me = lax.axis_index(axis)
+    barrier = pltpu.get_barrier_semaphore()
+    for k in range(1, n):
+        pl.semaphore_signal(
+            barrier, inc=1, device_id={axis: lax.rem(me + k, n)}, device_id_type=MESH
+        )
+    pl.semaphore_wait(barrier, n - 1)
+    sends = []
+    for k in range(1, n):
+        peer = lax.rem(me + k, n)
+        copy = pltpu.make_async_remote_copy(
+            src_ref=x_ref if gather else x_ref.at[peer],
+            dst_ref=y_ref.at[me],
+            send_sem=send_sem.at[k],
+            recv_sem=recv_sem.at[k],
+            device_id={axis: peer},
+            device_id_type=MESH,
+        )
+        copy.start()
+        sends.append(copy)
+    if gather:
+        y_ref[me] = x_ref[...]
+    else:
+        y_ref[me] = x_ref[me]
+    for copy in sends:
+        copy.wait_send()
+    for k in range(1, n):
+        source = lax.rem(me + n - k, n)
+        pltpu.make_async_remote_copy(
+            src_ref=x_ref if gather else x_ref.at[source],
+            dst_ref=y_ref.at[source],
+            send_sem=send_sem.at[k],
+            recv_sem=recv_sem.at[k],
+            device_id={axis: source},
+            device_id_type=MESH,
+        ).wait_recv()
+
+
+def exchange(x, axis, gather, collective_id):
+    n = lax.axis_size(axis)
+    shape = ((n,) + x.shape) if gather else x.shape
+    return pl.pallas_call(
+        functools.partial(_exchange_kernel, n, axis, gather),
+        out_shape=jax.ShapeDtypeStruct(shape, x.dtype),
+        in_specs=[pl.BlockSpec(memory_space=pltpu.VMEM)],
+        out_specs=pl.BlockSpec(memory_space=pltpu.VMEM),
+        scratch_shapes=[pltpu.SemaphoreType.DMA((n,)), pltpu.SemaphoreType.DMA((n,))],
+        compiler_params=pltpu.CompilerParams(collective_id=collective_id, has_side_effects=True),
+    )(x)
 
 
 def body(
@@ -61,16 +118,21 @@
     slot_index = home_slot[row_id]
     cached_count = cache_len[slot_index]
     live_count = new_len[row_id]
-    combined = lax.psum(
-        jnp.dot(tokens, w_down, preferred_element_type=jnp.float32), "col"
-    )
+    partial_sums = jnp.dot(tokens, w_down, preferred_element_type=jnp.float32)
+    pieces = exchange(partial_sums.reshape(columns, own_rows, -1), "col", False, 0)
+    combined = jnp.sum(pieces, 0)
+    own_position = cached_count + column_id * own_rows + jnp.arange(own_rows, dtype=jnp.int32)
+    own_cos, own_sin = angle_tables(own_position, ROPE)
+    own_query = rms_scale(combined[:, :q_width], q_gain).astype(jnp.bfloat16)
+    own_latent = rms_scale(combined[:, q_width : q_width + kv_width], kv_gain).astype(jnp.bfloat16)
+    own_rope = rotary(combined[:, q_width + kv_width :], own_cos, own_sin).astype(jnp.bfloat16)
+    own_rows_all = jnp.concatenate([own_query, own_latent, own_rope], 1)
+    all_rows = exchange(own_rows_all, "col", True, 1).reshape(group_rows, -1)
+    query_latent = all_rows[:, :q_width]
+    fresh_latents = all_rows[:, q_width:]
     query_cos, query_sin = angle_tables(
         cached_count + jnp.arange(group_rows, dtype=jnp.int32), ROPE
     )
-    query_latent = rms_scale(combined[:, :q_width], q_gain).astype(jnp.bfloat16)
-    new_latent = rms_scale(combined[:, q_width : q_width + kv_width], kv_gain).astype(jnp.bfloat16)
-    new_rope = rotary(combined[:, q_width + kv_width :], query_cos, query_sin).astype(jnp.bfloat16)
-    fresh_latents = jnp.concatenate([new_latent, new_rope], 1)
     projected = jnp.dot(query_latent, w_q_up, preferred_element_type=jnp.float32)
     queries = jnp.concatenate(
         [projected[:, :NOPE], rotary(projected[:, NOPE:], query_cos, query_sin)], 1
@@ -89,7 +151,7 @@
         ).astype(jnp.bfloat16)
         return (jnp.concatenate([lifted[:, :NOPE], latents[:, kv_width:]], 1), lifted[:, NOPE:])
 
-    cache_latents = lax.all_gather(own_cache, "col", axis=0, tiled=True)
+    cache_latents = exchange(own_cache, "col", True, 2).reshape(-1, own_cache.shape[-1])
     cache_keys, cache_values = expand(cache_latents)
     fresh_keys, fresh_values = expand(fresh_latents)
     key_total = cache_keys.shape[0]
@@ -148,14 +210,11 @@
     attended = (summed / row_total[:, None]).astype(jnp.bfloat16)
     live_rows = jnp.arange(group_rows, dtype=jnp.int32) < live_count
     attended = jnp.where(live_rows[:, None], attended, jnp.zeros_like(attended))
-    summed_out = lax.psum_scatter(
-        lax.dot_general(
-            w_out, attended, (((0,), (1,)), ((), ())), preferred_element_type=jnp.float32
-        ).astype(jnp.bfloat16),
-        "col",
-        scatter_dimension=0,
-        tiled=True,
-    ).astype(jnp.float32)
+    out_parts = lax.dot_general(
+        w_out, attended, (((0,), (1,)), ((), ())), preferred_element_type=jnp.float32
+    ).astype(jnp.bfloat16)
+    out_pieces = exchange(out_parts.reshape(columns, -1, group_rows), "col", False, 3)
+    summed_out = jnp.sum(out_pieces.astype(jnp.float32), 0)
     result = summed_out.T.astype(jnp.bfloat16)
     return result
 

time: 533 us -> 361 us (0.68)
  waiting for transfers between devices: 462 us -> 0.71 us
  Pallas kernels: 0 us -> 266 us
  matrix products: 32.4 us -> 47.6 us
  local copies, waits for them, and re-layouts: 6.62 us -> 16.1 us
    pallas_call x0 -> x4, Pallas kernels: none -> 266 us  [exchange(): pl.pallas_call(functools.partial(_exchange_kernel, n, axis, gather), out_...]
    unnamed x5 -> x1, waiting for transfers between devices: 220 us -> 0.71 us
    psum x1 -> x0, waiting for transfers between devices: 108 us -> none  [body(): lax.psum(jnp.dot(tokens, w_down, preferred_element_type=jnp.float32), 'col')]
    all_gather x1 -> x0, waiting for transfers between devices: 87.4 us -> none  [body(): cache_latents = lax.all_gather(own_cache, 'col', axis=0, tiled=True)]
    all_gather x1, waiting for transfers between devices: 46.5 us -> 0.01 us  [body(): segment = lax.all_gather(latent_cache, 'row', axis=0, tiled=True)]
    dot_general x16, matrix products: 3.75 us -> 17.2 us  [accumulate(): jnp.dot(exponent.astype(jnp.bfloat16), value_block, preferred_element_typ...]
  transfers between devices with their start and end apart: 4 -> 1, of which waited for: 4 -> 0; matrix products, arithmetic and copies ran while one was open for 3% -> 4% of each run, Pallas kernels for 0% -> 17%
where the time goes in v2:
time: 361 us; the launch traced here: 359 us
  Pallas kernels  266 us (74%)
  matrix products  47.6 us (13%)
  local copies, waits for them, and re-layouts  16.1 us (4%)
  between operations  15.9 us (4%)
  other arithmetic  12.6 us (3%)
    pallas_call x4, Pallas kernels, exchange(): pl.pallas_call(functools.partial(_exchange_kernel, n, axis, gather), out_...  266 us
    dot_general x16, matrix products, accumulate(): jnp.einsum('qd,kd->qk', queries, key_block, preferred_element_type=jnp.fl...  18.7 us
    dot_general x16, matrix products, accumulate(): jnp.dot(exponent.astype(jnp.bfloat16), value_block, preferred_element_typ...  17.2 us
  transfers between devices with their start and end apart: 1, of which 0 were waited for; matrix products, arithmetic and copies ran while one was open for 4% of the time, Pallas kernels for 17%

profile of v2, /device:TPU:6, one launch (start us, length us, event | category | flops | bytes accessed | tf_op | source)
XLA Modules:
  0.0 359.2 jit_solution(17266184011337135933)
XLA Ops:
  6.5 0.7 all-gather.2.cloned.1.call-update
  7.3 1.2 dynamic_slice.37
  9.6 2.3 convolution_bitcast_fusion.x_ref
  11.9 38.7 %shard_map.118 = f32[32,8,1056]{2,1,0:T(8,128)} custom-call(f32[32,8,1056]{2,1,0:T(8,128)} %convolution_bitcast_fusion.x_ref), custom_call_target="tpu_custom_call" | custom-call | tf_op jit(solution)/shard_map/pallas_call | solution.py:87
  50.6 1.3 reduce_sum.79
  52.5 0.6 dynamic_slice.38
  54.2 0.7 concatenate.16.x_ref
  54.9 22.4 %shard_map.119 = bf16[32,8,1056]{2,1,0:T(8,128)(2,1)} custom-call(bf16[8,1056]{1,0:T(8,128)(2,1)} %concatenate.16.x_ref), custom_call_target="tpu_custom_call" | custom-call | tf_op jit(solution)/shard_map/pallas_call | solution.py:87
  77.3 0.8 slice.84
  78.3 1.1 convolution_convert_fusion.2
  79.4 1.3 fusion.12
  80.7 0.6 dynamic_slice.36
  81.3 0.7 dynamic-slice_bitcast_fusion
  82.1 0.7 add_compare_fusion
  82.9 0.6 add_convert_fusion
  83.7 0.6 iota_compare_fusion.3
  84.3 0.7 iota_compare_fusion.2
  84.9 0.3 fusion.52
  85.3 0.2 fusion.17
  85.4 2.2 select_reduce_fusion
  87.6 0.8 copy.45.x_ref
  88.5 153.3 %shard_map.120 = bf16[32,256,288]{2,1,0:T(8,128)(2,1)} custom-call(bf16[256,288]{1,0:T(8,128)(2,1)} %copy.45.x_ref), custom_call_target="tpu_custom_call" | custom-call | tf_op jit(solution)/shard_map/pallas_call | solution.py:87
  241.8 3.1 slice.88
  244.9 5.0 %convolution_convert_fusion = bf16[8192,128]{0,1:T(8,128)(2,1)} fusion(bf16[8192,288]{1,0:T(8,128)(2,1)} %bitcast.21, bf16[256,4096]{1,0:T(8,128)(2,1)S(1)} %copy-done, s32[]{:T(128)S(6)} %select_n.43), kind=kOutput, calls=%fused_computation.13 | convolution fusion | flops 537919488 | bytes 6356996 | tf_op jit(solution)/shard_map/dot_general | solution.py:149
  249.9 1.9 copy.54
  251.8 2.7 fusion.51
  254.4 1.3 pad_maximum_fusion
  255.7 40.3 %while.17 = (s32[]{:T(128)}, f32[256]{0:T(256)S(1)}, f32[256]{0:T(256)S(1)}, f32[256,64]{0,1:T(8,128)S(1)}, pred[8192]{0:T(1024)(128)(4,1)S(1)}, /*index=5*/bf16...) while((s32[]{:T(128)}, f32[256]{0:T(256)S(1)}, ...), condition=%wide.region_10.11_spmd, body=%wide.region_7.10_spmd.sunk | while | flops 42893828 | bytes 1935031 | solution.py:209
  255.8 1.2 fusion.66
  257.1 1.1 convolution_add_fusion.2
  258.3 1.2 fusion.66
  259.6 1.1 convolution_add_fusion.2
  260.8 1.2 fusion.66
  262.1 1.1 convolution_add_fusion.2
  263.3 1.2 fusion.66
  264.7 1.1 convolution_add_fusion.2
  265.8 1.2 fusion.66
  267.2 1.1 convolution_add_fusion.2
  268.4 1.2 fusion.66
  269.7 1.1 convolution_add_fusion.2
  270.9 1.2 fusion.66
  272.2 1.1 convolution_add_fusion.2
  273.4 1.2 fusion.66
  274.7 1.1 convolution_add_fusion.2
  275.9 1.2 fusion.66
  277.2 1.1 convolution_add_fusion.2
  278.4 1.2 fusion.66
  279.8 1.1 convolution_add_fusion.2
  281.0 1.2 fusion.66
  282.3 1.1 convolution_add_fusion.2
  283.5 1.2 fusion.66
  284.8 1.1 convolution_add_fusion.2
  286.0 1.2 fusion.66
  287.3 1.1 convolution_add_fusion.2
  288.5 1.2 fusion.66
  289.8 1.1 convolution_add_fusion.2
  291.0 1.2 fusion.66
  292.4 1.1 convolution_add_fusion.2
  293.5 1.2 fusion.66
  294.9 1.1 convolution_add_fusion.2
  296.0 1.5 fusion.10
  297.5 1.5 copy.50
  298.9 51.3 %shard_map.121 = bf16[32,80,256]{2,1,0:T(8,128)(2,1)} custom-call(bf16[32,80,256]{2,1,0:T(8,128)(2,1)} %bitcast.22), custom_call_target="tpu_custom_call" | custom-call | tf_op jit(solution)/shard_map/pallas_call | solution.py:87
  350.2 2.1 reduce_sum.85
  (113 shorter events, 4.8 us)
Async XLA Ops:
  6.5 71.7 %copy-start = (bf16[256,4096]{1,0:T(8,128)(2,1)S(1)}, bf16[256,4096]{1,0:T(8,128)(2,1)}, u32[]{:S(2)}) copy-start(bf16[256,4096]{1,0:T(8,128)(2,1)} %param.19) | copy-start | bytes 6291460
  6.5 78.9 %all-gather.2.cloned.1.call-start = ((), (), s32[]{:S(2)}) async-start(), calls=%async_computation | async-start | bytes 2506752 | tf_op jit(solution)/shard_map/all_gather | solution.py:140
  11.9 40.6 %copy-start.4 = (s32[16]{0:T(128)S(1)}, s32[16]{0:T(128)}, u32[]{:S(2)}) copy-start(s32[16]{0:T(128)} %param.22) | copy-start | bytes 196
  11.9 42.2 %copy-start.2 = (f32[256]{0:T(256)S(1)}, f32[256]{0:T(256)}, u32[]{:S(2)}) copy-start(f32[256]{0:T(256)} %param.17) | copy-start | bytes 3076
  11.9 42.3 %copy-start.1 = (f32[768]{0:T(1024)S(1)}, f32[768]{0:T(1024)}, u32[]{:S(2)}) copy-start(f32[768]{0:T(1024)} %param.16) | copy-start | bytes 9220
  11.9 67.5 %copy-start.3 = (bf16[768,96]{0,1:T(8,128)(2,1)S(1)}, bf16[768,96]{0,1:T(8,128)(2,1)}, u32[]{:S(2)}) copy-start(bf16[768,96]{0,1:T(8,128)(2,1)} %param.18) | copy-start | bytes 442372
  50.6 30.1 %copy-start.5 = (s32[16]{0:T(128)S(1)}, s32[16]{0:T(128)}, u32[]{:S(2)}) copy-start(s32[16]{0:T(128)} %param.23) | copy-start | bytes 196
Sparse Core Ops, SparseCore 0:
  9.5 47.9 all-gather.1

commit v3 on v2

v3 whole, which is shorter than its diff:
```python
import functools
import math

import jax
import jax.numpy as jnp
from jax import lax
from jax.experimental import pallas as pl
from jax.experimental.pallas import tpu as pltpu
from jax.sharding import PartitionSpec as P

MESH = pl.DeviceIdType.MESH

NOPE = 64
ROPE = 32
VDIM = 64


epsilon = 1e-05


def rms_scale(values, gain):
    return values * lax.rsqrt(jnp.mean(values * values, axis=-1, keepdims=True) + epsilon) * gain


def angle_tables(positions, width):
    half_dim = width // 2
    frequency = 10000.0 ** (-2.0 * jnp.arange(half_dim, dtype=jnp.float32) / width)
    angles = positions.astype(jnp.float32)[:, None] * frequency[None, :]
    return (jnp.cos(angles), jnp.sin(angles))


def rotary(values, cosine, sine_table):
    half_dim = values.shape[-1] // 2
    first_half = values[..., :half_dim]
    second_half = values[..., half_dim:]
    return jnp.concatenate(
        [
            first_half * cosine - second_half * sine_table,
            second_half * cosine + first_half * sine_table,
        ],
        -1,
    )


def _exchange_kernel(n, axis, modes, *refs):
    count = len(modes)
    sources, targets = refs[:count], refs[count : 2 * count]
    send_sem, recv_sem = refs[2 * count :]
    me = lax.axis_index(axis)
    barrier = pltpu.get_barrier_semaphore()
    for k in range(1, n):
        pl.semaphore_signal(
            barrier, inc=1, device_id={axis: lax.rem(me + k, n)}, device_id_type=MESH
        )
    pl.semaphore_wait(barrier, n - 1)

    def remote(a, k, peer, landing):
        x_ref = sources[a]
        return pltpu.make_async_remote_copy(
            src_ref=x_ref if modes[a] else x_ref.at[peer],
            dst_ref=targets[a].at[landing],
            send_sem=send_sem.at[a, k],
            recv_sem=recv_sem.at[a, k],
            device_id={axis: peer},
            device_id_type=MESH,
        )

    sends = []
    for k in range(1, n):
        for a in range(count):
            copy = remote(a, k, lax.rem(me + k, n), me)
            copy.start()
            sends.append(copy)
    for a in range(count):
        if modes[a]:
            targets[a][me] = sources[a][...]
        else:
            targets[a][me] = sources[a][me]
    for copy in sends:
        copy.wait_send()
    for k in range(1, n):
        source = lax.rem(me + n - k, n)
        for a in range(count):
            remote(a, k, source, source).wait_recv()


def exchange(arrays, modes, axis, collective_id):
    n = lax.axis_size(axis)
    shapes = [
        jax.ShapeDtypeStruct(((n,) + x.shape) if gather else x.shape, x.dtype)
        for x, gather in zip(arrays, modes)
    ]
    return pl.pallas_call(
        functools.partial(_exchange_kernel, n, axis, tuple(modes)),
        out_shape=shapes,
        in_specs=[pl.BlockSpec(memory_space=pltpu.VMEM)] * len(arrays),
        out_specs=[pl.BlockSpec(memory_space=pltpu.VMEM)] * len(arrays),
        scratch_shapes=[
            pltpu.SemaphoreType.DMA((len(arrays), n)),
            pltpu.SemaphoreType.DMA((len(arrays), n)),
        ],
        compiler_params=pltpu.CompilerParams(collective_id=collective_id, has_side_effects=True),
    )(*arrays)


def body(
    tokens,
    w_down,
    q_gain,
    kv_gain,
    w_q_up,
    w_kv_up,
    w_out,
    latent_cache,
    cache_len,
    new_len,
    page_table,
    home_slot,
):
    columns = lax.axis_size("col")
    column_id = lax.axis_index("col")
    row_id = lax.axis_index("row")
    group_rows = tokens.shape[0]
    own_rows = group_rows // columns
    q_width = q_gain.shape[0]
    kv_width = kv_gain.shape[0]
    slot_index = home_slot[row_id]
    cached_count = cache_len[slot_index]
    live_count = new_len[row_id]
    partial_sums = jnp.dot(tokens, w_down, preferred_element_type=jnp.float32)
    (pieces,) = exchange([partial_sums.reshape(columns, own_rows, -1)], [False], "col", 0)
    combined = jnp.sum(pieces, 0)
    own_position = cached_count + column_id * own_rows + jnp.arange(own_rows, dtype=jnp.int32)
    own_cos, own_sin = angle_tables(own_position, ROPE)
    own_query = rms_scale(combined[:, :q_width], q_gain).astype(jnp.bfloat16)
    own_latent = rms_scale(combined[:, q_width : q_width + kv_width], kv_gain).astype(jnp.bfloat16)
    own_rope = rotary(combined[:, q_width + kv_width :], own_cos, own_sin).astype(jnp.bfloat16)
    own_rows_all = jnp.concatenate([own_query, own_latent, own_rope], 1)
    (all_rows,) = exchange([own_rows_all], [True], "col", 1)
    all_rows = all_rows.reshape(group_rows, -1)
    query_latent = all_rows[:, :q_width]
    fresh_latents = all_rows[:, q_width:]
    query_cos, query_sin = angle_tables(
        cached_count + jnp.arange(group_rows, dtype=jnp.int32), ROPE
    )
    projected = jnp.dot(query_latent, w_q_up, preferred_element_type=jnp.float32)
    queries = jnp.concatenate(
        [projected[:, :NOPE], rotary(projected[:, NOPE:], query_cos, query_sin)], 1
    ).astype(jnp.bfloat16)
    segment = lax.all_gather(latent_cache, "row", axis=0, tiled=True)
    matches = jnp.arange(segment.shape[0], dtype=jnp.int32) == slot_index
    own_cache = jnp.sum(
        jnp.where(matches[:, None, None], segment.astype(jnp.float32), 0.0), 0
    ).astype(jnp.bfloat16)
    head_width = NOPE + VDIM
    head_weight = lax.dynamic_slice_in_dim(w_kv_up, column_id * head_width, head_width, 1)
    chunk = own_cache.shape[0]
    own_lifted = (
        jnp.dot(own_cache[:, :kv_width], w_kv_up, preferred_element_type=jnp.float32)
        .astype(jnp.bfloat16)
        .reshape(chunk, columns, head_width)
        .transpose(1, 0, 2)
    )
    lifted_parts, rope_parts = exchange(
        [own_lifted, own_cache[:, kv_width:].T], [False, True], "col", 2
    )
    key_total = columns * chunk
    lifted_parts = lifted_parts.reshape(key_total, head_width)
    fresh_lifted = jnp.dot(
        fresh_latents[:, :kv_width], head_weight, preferred_element_type=jnp.float32
    ).astype(jnp.bfloat16)
    all_keys = jnp.concatenate(
        [
            jnp.concatenate(
                [lifted_parts[:, :NOPE], rope_parts.transpose(0, 2, 1).reshape(key_total, ROPE)], 1
            ),
            jnp.concatenate([fresh_lifted[:, :NOPE], fresh_latents[:, kv_width:]], 1),
        ],
        0,
    )
    all_values = jnp.concatenate([lifted_parts[:, NOPE:], fresh_lifted[:, NOPE:]], 0)
    page_row = page_table[slot_index]
    page_count = page_row.shape[0]
    page_size = key_total // page_count
    offsets = jnp.arange(page_size, dtype=jnp.int32)
    page_ids = jnp.arange(page_count, dtype=jnp.int32)
    logical_page = jnp.sum(
        page_ids[:, None] * (page_row[:, None] == page_ids[None, :]).astype(jnp.int32), 0
    )
    cached_visible = (logical_page[:, None] * page_size + offsets[None, :]).reshape(
        key_total
    ) < cached_count
    score_scale = 1.0 / math.sqrt(NOPE + ROPE)
    query_index = jnp.arange(group_rows, dtype=jnp.int32)[:, None]
    key_index = jnp.arange(group_rows, dtype=jnp.int32)[None, :]
    fresh_visible = (key_index <= query_index) & (key_index < live_count)
    visible = jnp.concatenate(
        [jnp.broadcast_to(cached_visible[None, :], (group_rows, key_total)), fresh_visible], 1
    )
    scores = (
        jnp.einsum("qd,kd->qk", queries, all_keys, preferred_element_type=jnp.float32)
        * score_scale
    )
    scores = jnp.where(visible, scores, -jnp.inf)
    row_peak = jnp.max(scores, 1, keepdims=True)
    exponent = jnp.exp(scores - row_peak)
    row_total = jnp.sum(exponent, 1)
    summed = jnp.dot(
        exponent.astype(jnp.bfloat16), all_values, preferred_element_type=jnp.float32
    )
    attended = (summed / row_total[:, None]).astype(jnp.bfloat16)
    live_rows = jnp.arange(group_rows, dtype=jnp.int32) < live_count
    attended = jnp.where(live_rows[:, None], attended, jnp.zeros_like(attended))
    out_parts = lax.dot_general(
        w_out, attended, (((0,), (1,)), ((), ())), preferred_element_type=jnp.float32
    ).astype(jnp.bfloat16)
    (out_pieces,) = exchange([out_parts.reshape(columns, -1, group_rows)], [False], "col", 3)
    summed_out = jnp.sum(out_pieces.astype(jnp.float32), 0)
    result = summed_out.T.astype(jnp.bfloat16)
    return result


def solution(mesh):
    return jax.shard_map(
        body,
        mesh=mesh,
        in_specs=(
            P("row", "col"),
            P("col", None),
            P(),
            P(),
            P(None, "col"),
            P(),
            P("col", None),
            P("row", "col", None),
            P(),
            P(),
            P(),
            P(),
        ),
        out_specs=P("row", "col"),
        check_vma=False,
    )
```

time: 361 us -> 244 us (0.68)
  Pallas kernels: 266 us -> 170 us
  matrix products: 47.6 us -> 21.1 us
  local copies, waits for them, and re-layouts: 16.1 us -> 24 us
    pallas_call x4, Pallas kernels: 266 us -> 170 us  [exchange(): pl.pallas_call(functools.partial(_exchange_kernel, n, axis, tuple(modes))...]
    dot_general x36 -> x3, matrix products: 42.6 us -> 10.7 us  [the longest x1 7.55 us: body(): jnp.einsum('qd,kd->qk', queries, all_keys, preferred_element_type=jnp.flo...]
    reshape x0 -> x2, local copies, waits for them, and re-layouts: none -> 5.86 us  [the longest x1 4.08 us: body(): own_lifted = jnp.dot(own_cache[:, :kv_width], w_kv_up, preferred_element_...]
    dot_general x1, matrix products: 1.5 us -> 6.81 us  [body(): lax.dot_general(w_out, attended, (((0,), (1,)), ((), ())), preferred_elem...]
  transfers between devices with their start and end apart: 1 -> 1, of which waited for: 0 -> 0; matrix products, arithmetic and copies ran while one was open for 4% -> 6% of each run, Pallas kernels for 17% -> 25%
where the time goes in v3:
time: 244 us; the launch traced here: 242 us
  Pallas kernels  170 us (70%)
  local copies, waits for them, and re-layouts  24 us (10%)
  matrix products  21.1 us (9%)
  between operations  15.9 us (7%)
  other arithmetic  10.3 us (4%)
    pallas_call x4, Pallas kernels, exchange(): pl.pallas_call(functools.partial(_exchange_kernel, n, axis, tuple(modes))...  170 us
    dot_general x1, matrix products, body(): jnp.einsum('qd,kd->qk', queries, all_keys, preferred_element_type=jnp.flo...  7.55 us
    dot_general x1, matrix products, body(): lax.dot_general(w_out, attended, (((0,), (1,)), ((), ())), preferred_elem...  6.81 us
    slice x1, local copies, waits for them, and re-layouts, body(): lifted_parts[:, :NOPE]  5.04 us
  transfers between devices with their start and end apart: 1, of which 0 were waited for; matrix products, arithmetic and copies ran while one was open for 6% of the time, Pallas kernels for 25%

profile of v3, /device:TPU:6, one launch (start us, length us, event | category | flops | bytes accessed | tf_op | source)
XLA Modules:
  0.0 242.2 jit_solution(2042163854242849064)
XLA Ops:
  6.5 0.0 copy-start
  6.5 0.0 copy-start.6
  6.5 0.0 all-gather.2.cloned.1.call-start
  6.5 0.7 all-gather.2.cloned.1.call-update
  7.3 1.2 dynamic_slice.16
  9.6 2.3 convolution_bitcast_fusion.refs_0_
  11.9 0.0 copy-start.4
  11.9 0.0 copy-start.3
  11.9 0.0 copy-start.5
  11.9 38.7 %shard_map.118 = f32[32,8,1056]{2,1,0:T(8,128)} custom-call(f32[32,8,1056]{2,1,0:T(8,128)} %convolution_bitcast_fusion.refs_0_), custom_call_target="tpu_custom_call" | custom-call | tf_op jit(solution)/shard_map/pallas_call | solution.py:93
  50.6 0.0 copy-start.7
  51.1 0.0 copy-done.6
  51.2 0.6 dynamic_slice.18
  52.3 1.4 reduce_sum.67
  53.7 0.1 multiply_reduce_fusion.1
  53.8 0.1 multiply_reduce_fusion
  54.0 0.1 fusion.63
  54.1 0.0 copy-done.4
  54.1 0.1 multiply_convert_fusion.1
  54.2 0.0 copy-done.3
  54.2 0.1 multiply_convert_fusion
  54.2 0.7 concatenate.26.refs_0_
  54.9 22.4 %shard_map.119 = bf16[32,8,1056]{2,1,0:T(8,128)(2,1)} custom-call(bf16[8,1056]{1,0:T(8,128)(2,1)} %concatenate.26.refs_0_), custom_call_target="tpu_custom_call" | custom-call | tf_op jit(solution)/shard_map/pallas_call | solution.py:93
  77.3 0.8 slice.87
  78.2 0.1 copy.48
  78.2 0.0 copy-done
  78.2 1.1 convolution_convert_fusion.2
  79.4 0.1 copy.42
  79.5 0.0 copy-done.5
  79.5 1.3 fusion.34
  80.8 0.7 dynamic-slice_bitcast_fusion
  81.5 0.1 select_reduce_fusion.1
  81.6 0.7 add_compare_fusion
  82.3 0.1 reshape.93
  82.4 0.0 copy-done.7
  82.4 0.6 dynamic_slice.15
  83.0 0.1 copy.43
  83.1 0.6 iota_compare_fusion.3
  83.7 0.7 iota_compare_fusion.2
  84.3 0.6 add_convert_fusion
  84.9 0.1 fusion.52
  85.1 0.0 all-gather.2.cloned.1.call-done
  85.1 2.2 select_reduce_fusion
  87.3 2.0 convolution_convert_fusion
  89.3 0.6 slice_bitcast_fusion.refs_1_
  90.0 4.1 %copy.37 = bf16[256,4096]{0,1:T(8,128)(2,1)} copy(bf16[256,4096]{1,0:T(8,128)(2,1)} %convolution_convert_fusion) | data formatting | bytes 4194304 | tf_op jit(solution)/shard_map/convert_element_type | solution.py:160
  94.1 4.1 %copy.38 = bf16[256,32,128]{2,0,1:T(8,128)(2,1)} copy(bf16[256,32,128]{0,2,1:T(8,128)(2,1)} %bitcast.26) | data formatting | bytes 4194304 | tf_op jit(solution)/shard_map/reshape | solution.py:161
  98.1 70.4 %shard_map.120 = (bf16[32,256,128]{2,1,0:T(8,128)(2,1)}, bf16[32,32,256]{2,1,0:T(8,128)(2,1)}) custom-call(bf16[32,256,128]{2,1,0:T(8,128)(2,1)} %bitcast.25, bf16[32,256]{1,0:T(8,128)(2,1)} %slice_bitcast_fusion.refs_1_), custom_call_target="tpu_custom_call" | custom-call | tf_op jit(solution)/shard_map/pallas_call | solution.py:93
  168.5 0.0 copy-start.2
  168.5 5.0 %fusion.69 = (bf16[8192,64]{1,0:T(8,128)(2,1)}, bf16[8192,64]{1,0:T(8,128)(2,1)}) fusion(bf16[8192,128]{1,0:T(8,128)(2,1)} %bitcast.24), kind=kLoop, calls=%fused_computation.82 | loop fusion | bytes 4194304 | tf_op jit(solution)/shard_map/slice | solution.py:175
  173.6 0.0 copy-done.2
  173.6 1.8 copy.46
  175.4 7.6 %fusion.71 = (f32[256]{0:T(256)S(1)}, f32[256,8448]{1,0:T(8,128)S(1)}) fusion(bf16[256,96]{1,0:T(8,128)(2,1)S(1)} %copy.42, bf16[8192,32]{1,0:T(8,128)(2,1)} %bitcast.28, bf16[8192,64]{1,0:T(8,128)(2,1)} %get-tuple-element.9, bf16[256,16]{0,1:T(8,128)(2,1)S(1)} %get-tuple-element.12, bf16[256,16]{0,1:T(8,128)(2,1)S(1)} %get-tuple-element.11, ...), kind=kOutput, calls=%fused_computation.84 | convolution fusion | flops 428900096 | bytes 10396928 | tf_op jit(solution)/shard_map/qd,kd->qk/dot_general | solution.py:201
  182.9 0.0 copy-start.1
  182.9 1.4 fusion.1
  184.3 1.9 copy-done.1
  186.2 6.8 %fusion.6 = bf16[2560,256]{0,1:T(8,128)(2,1)S(1)} fusion(bf16[64,2560]{1,0:T(8,128)(2,1)} %param.18, bf16[256,64]{1,0:T(8,128)(2,1)S(1)} %copy.43, bf16[8192,64]{1,0:T(8,128)(2,1)} %get-tuple-element.10, f32[256,8448]{1,0:T(8,128)} %copy-done.1, f32[256]{0:T(256)S(1)} %get-tuple-element.17, f32[256]{0:T(256)S(1)} %fusion.1, ...), kind=kOutput, calls=%fused_computation.10 | convolution fusion | flops 367902720 | bytes 11372800 | tf_op jit(solution)/shard_map/dot_general | solution.py:214
  193.0 1.5 copy.44
  194.5 38.7 %shard_map.121 = bf16[32,80,256]{2,1,0:T(8,128)(2,1)} custom-call(bf16[32,80,256]{2,1,0:T(8,128)(2,1)} %bitcast.27), custom_call_target="tpu_custom_call" | custom-call | tf_op jit(solution)/shard_map/pallas_call | solution.py:93
  233.2 2.1 reduce_sum.72
  (10 shorter events, 0.1 us)
Async XLA Ops:
  6.5 71.7 %copy-start = (bf16[256,4096]{1,0:T(8,128)(2,1)S(1)}, bf16[256,4096]{1,0:T(8,128)(2,1)}, u32[]{:S(2)}) copy-start(bf16[256,4096]{1,0:T(8,128)(2,1)} %param.17) | copy-start | bytes 6291460
  6.5 44.6 %copy-start.6 = (s32[16]{0:T(128)S(1)}, s32[16]{0:T(128)}, u32[]{:S(2)}) copy-start(s32[16]{0:T(128)} %param.20) | copy-start | bytes 196
  6.5 78.6 %all-gather.2.cloned.1.call-start = ((), (), s32[]{:S(2)}) async-start(), calls=%async_computation | async-start | bytes 2506752 | tf_op jit(solution)/shard_map/all_gather | solution.py:150
  11.9 42.2 %copy-start.4 = (f32[256]{0:T(256)S(1)}, f32[256]{0:T(256)}, u32[]{:S(2)}) copy-start(f32[256]{0:T(256)} %param.15) | copy-start | bytes 3076
  11.9 42.3 %copy-start.3 = (f32[768]{0:T(1024)S(1)}, f32[768]{0:T(1024)}, u32[]{:S(2)}) copy-start(f32[768]{0:T(1024)} %param.14) | copy-start | bytes 9220
  11.9 67.6 %copy-start.5 = (bf16[768,96]{0,1:T(8,128)(2,1)S(1)}, bf16[768,96]{0,1:T(8,128)(2,1)}, u32[]{:S(2)}) copy-start(bf16[768,96]{0,1:T(8,128)(2,1)} %param.16) | copy-start | bytes 442372
  50.6 31.8 %copy-start.7 = (s32[16]{0:T(128)S(1)}, s32[16]{0:T(128)}, u32[]{:S(2)}) copy-start(s32[16]{0:T(128)} %param.21) | copy-start | bytes 196
  168.5 5.1 %copy-start.2 = (bf16[32,32,256]{2,1,0:T(8,128)(2,1)S(1)}, bf16[32,32,256]{2,1,0:T(8,128)(2,1)}, u32[]{:S(2)}) copy-start(bf16[32,32,256]{2,1,0:T(8,128)(2,1)} %get-tuple-element.8) | copy-start | bytes 1572868
  182.9 3.3 %copy-start.1 = (f32[256,8448]{1,0:T(8,128)}, f32[256,8448]{1,0:T(8,128)S(1)}, u32[]{:S(2)}) copy-start(f32[256,8448]{1,0:T(8,128)S(1)} %get-tuple-element.18) | copy-start | bytes 25952260
Sparse Core Ops, SparseCore 0:
  9.5 47.9 all-gather.1

commit v4 on v3

--- a/solution.py
+++ b/solution.py
@@ -136,17 +136,6 @@
     own_latent = rms_scale(combined[:, q_width : q_width + kv_width], kv_gain).astype(jnp.bfloat16)
     own_rope = rotary(combined[:, q_width + kv_width :], own_cos, own_sin).astype(jnp.bfloat16)
     own_rows_all = jnp.concatenate([own_query, own_latent, own_rope], 1)
-    (all_rows,) = exchange([own_rows_all], [True], "col", 1)
-    all_rows = all_rows.reshape(group_rows, -1)
-    query_latent = all_rows[:, :q_width]
-    fresh_latents = all_rows[:, q_width:]
-    query_cos, query_sin = angle_tables(
-        cached_count + jnp.arange(group_rows, dtype=jnp.int32), ROPE
-    )
-    projected = jnp.dot(query_latent, w_q_up, preferred_element_type=jnp.float32)
-    queries = jnp.concatenate(
-        [projected[:, :NOPE], rotary(projected[:, NOPE:], query_cos, query_sin)], 1
-    ).astype(jnp.bfloat16)
     segment = lax.all_gather(latent_cache, "row", axis=0, tiled=True)
     matches = jnp.arange(segment.shape[0], dtype=jnp.int32) == slot_index
     own_cache = jnp.sum(
@@ -161,9 +150,19 @@
         .reshape(chunk, columns, head_width)
         .transpose(1, 0, 2)
     )
-    lifted_parts, rope_parts = exchange(
-        [own_lifted, own_cache[:, kv_width:].T], [False, True], "col", 2
-    )
+    lifted_parts, rope_parts, all_rows = exchange(
+        [own_lifted, own_cache[:, kv_width:].T, own_rows_all], [False, True, True], "col", 2
+    )
+    all_rows = all_rows.reshape(group_rows, -1)
+    query_latent = all_rows[:, :q_width]
+    fresh_latents = all_rows[:, q_width:]
+    query_cos, query_sin = angle_tables(
+        cached_count + jnp.arange(group_rows, dtype=jnp.int32), ROPE
+    )
+    projected = jnp.dot(query_latent, w_q_up, preferred_element_type=jnp.float32)
+    queries = jnp.concatenate(
+        [projected[:, :NOPE], rotary(projected[:, NOPE:], query_cos, query_sin)], 1
+    ).astype(jnp.bfloat16)
     key_total = columns * chunk
     lifted_parts = lifted_parts.reshape(key_total, head_width)
     fresh_lifted = jnp.dot(

time: 244 us -> 239 us (0.980)
  Pallas kernels: 170 us -> 165 us
    pallas_call x4 -> x3, Pallas kernels: 170 us -> 165 us  [exchange(): pl.pallas_call(functools.partial(_exchange_kernel, n, axis, tuple(modes))...]
  transfers between devices with their start and end apart: 1 -> 1, of which waited for: 0 -> 0; matrix products, arithmetic and copies ran while one was open for 6% -> 4% of each run, Pallas kernels for 25% -> 16%
where the time goes in v4:
time: 239 us; the launch traced here: 237 us
  Pallas kernels  165 us (69%)
  local copies, waits for them, and re-layouts  24 us (10%)
  matrix products  21 us (9%)
  between operations  15.9 us (7%)
  other arithmetic  10.2 us (4%)
    pallas_call x3, Pallas kernels, exchange(): pl.pallas_call(functools.partial(_exchange_kernel, n, axis, tuple(modes))...  165 us
    dot_general x1, matrix products, body(): jnp.einsum('qd,kd->qk', queries, all_keys, preferred_element_type=jnp.flo...  7.58 us
    dot_general x1, matrix products, body(): lax.dot_general(w_out, attended, (((0,), (1,)), ((), ())), preferred_elem...  6.81 us
    slice x1, local copies, waits for them, and re-layouts, body(): lifted_parts[:, :NOPE]  5.04 us
  transfers between devices with their start and end apart: 1, of which 0 were waited for; matrix products, arithmetic and copies ran while one was open for 4% of the time, Pallas kernels for 16%

profile of v4, /device:TPU:6, one launch (start us, length us, event | category | flops | bytes accessed | tf_op | source)
XLA Modules:
  0.0 237.2 jit_solution(7278837847142294765)
XLA Ops:
  6.5 0.0 copy-start
  6.5 0.0 copy-start.6
  6.5 0.0 copy-start.7
  6.5 0.0 all-gather.2.cloned.1.call-start
  6.5 0.7 all-gather.2.cloned.1.call-update
  7.3 1.2 dynamic_slice.16
  9.6 2.3 convolution_bitcast_fusion.refs_0_
  11.9 0.0 copy-start.5
  11.9 0.0 copy-start.4
  11.9 38.7 %shard_map.118 = f32[32,8,1056]{2,1,0:T(8,128)} custom-call(f32[32,8,1056]{2,1,0:T(8,128)} %convolution_bitcast_fusion.refs_0_), custom_call_target="tpu_custom_call" | custom-call | tf_op jit(solution)/shard_map/pallas_call | solution.py:93
  51.1 0.0 copy-done.6
  51.1 0.6 dynamic_slice.18
  52.3 0.7 dynamic-slice_bitcast_fusion
  53.0 0.1 select_reduce_fusion.1
  53.1 0.7 add_compare_fusion
  53.8 0.1 reshape.93
  53.8 0.0 copy-done.7
  53.9 0.6 dynamic_slice.15
  54.4 1.3 reduce_sum.68
  55.8 0.1 multiply_reduce_fusion.1
  55.9 0.1 multiply_reduce_fusion
  56.1 0.1 fusion.63
  56.2 0.0 copy-done.5
  56.2 0.1 multiply_convert_fusion.1
  56.3 0.0 copy-done.4
  56.3 0.1 multiply_convert_fusion
  56.3 0.7 concatenate.26.refs_2_
  57.0 0.5 iota_compare_fusion.3
  57.6 0.6 iota_compare_fusion.2
  58.2 0.6 add_convert_fusion
  58.8 0.0 all-gather.2.cloned.1.call-done
  58.8 2.2 select_reduce_fusion
  61.0 0.6 slice_bitcast_fusion.refs_1_
  61.6 0.0 copy-done
  61.6 2.0 convolution_convert_fusion
  63.6 4.1 %copy.36 = bf16[256,4096]{0,1:T(8,128)(2,1)} copy(bf16[256,4096]{1,0:T(8,128)(2,1)} %convolution_convert_fusion) | data formatting | bytes 4194304 | tf_op jit(solution)/shard_map/convert_element_type | solution.py:149
  67.7 4.1 %copy.37 = bf16[256,32,128]{2,0,1:T(8,128)(2,1)} copy(bf16[256,32,128]{0,2,1:T(8,128)(2,1)} %bitcast.26) | data formatting | bytes 4194304 | tf_op jit(solution)/shard_map/reshape | solution.py:150
  71.8 86.1 %shard_map.119 = (bf16[32,256,128]{2,1,0:T(8,128)(2,1)}, bf16[32,32,256]{2,1,0:T(8,128)(2,1)}, bf16[32,8,1056]{2,1,0:T(8,128)(2,1)}) custom-call(bf16[32,256,128]{2,1,0:T(8,128)(2,1)} %bitcast.25, bf16[32,256]{1,0:T(8,128)(2,1)} %slice_bitcast_fusion.refs_1_, bf16[8,1056]{1,0:T(8,128)(2,1)} %concatenate.26.refs_2_), custom_call_target="tpu_custom_call" | custom-call | tf_op jit(solution)/shard_map/pallas_call | solution.py:93
  158.0 0.8 slice.87
  158.8 1.1 convolution_convert_fusion.2
  160.0 0.1 copy.48
  160.0 0.1 copy.42
  160.2 0.0 copy-start.2
  160.2 5.0 %fusion.69 = (bf16[8192,64]{1,0:T(8,128)(2,1)}, bf16[8192,64]{1,0:T(8,128)(2,1)}) fusion(bf16[8192,128]{1,0:T(8,128)(2,1)} %bitcast.24), kind=kLoop, calls=%fused_computation.82 | loop fusion | bytes 4194304 | tf_op jit(solution)/shard_map/slice | solution.py:174
  165.2 0.0 copy-start.3
  165.2 0.0 copy-done.2
  165.2 1.8 copy.46
  167.0 0.0 copy-done.3
  167.0 1.2 fusion.34
  168.2 0.1 fusion.52
  168.4 0.1 copy.43
  168.5 7.6 %fusion.71 = (f32[256]{0:T(256)S(1)}, f32[256,8448]{1,0:T(8,128)S(1)}) fusion(bf16[256,96]{1,0:T(8,128)(2,1)S(1)} %copy.42, bf16[8192,32]{1,0:T(8,128)(2,1)} %bitcast.28, bf16[8192,64]{1,0:T(8,128)(2,1)} %get-tuple-element.11, bf16[256,16]{0,1:T(8,128)(2,1)S(1)} %get-tuple-element.14, bf16[256,16]{0,1:T(8,128)(2,1)S(1)} %get-tuple-element.13, ...), kind=kOutput, calls=%fused_computation.84 | convolution fusion | flops 428900096 | bytes 10396928 | tf_op jit(solution)/shard_map/qd,kd->qk/dot_general | solution.py:200
  176.1 0.0 copy-start.1
  176.1 1.4 fusion.1
  177.5 1.9 copy-done.1
  179.4 6.8 %fusion.6 = bf16[2560,256]{0,1:T(8,128)(2,1)S(1)} fusion(bf16[64,2560]{1,0:T(8,128)(2,1)} %param.18, bf16[256,64]{1,0:T(8,128)(2,1)S(1)} %copy.43, bf16[8192,64]{1,0:T(8,128)(2,1)} %get-tuple-element.12, f32[256,8448]{1,0:T(8,128)} %copy-done.1, f32[256]{0:T(256)S(1)} %get-tuple-element.19, f32[256]{0:T(256)S(1)} %fusion.1, ...), kind=kOutput, calls=%fused_computation.10 | convolution fusion | flops 367902720 | bytes 11372800 | tf_op jit(solution)/shard_map/dot_general | solution.py:213
  186.2 1.5 copy.44
  187.6 40.5 %shard_map.120 = bf16[32,80,256]{2,1,0:T(8,128)(2,1)} custom-call(bf16[32,80,256]{2,1,0:T(8,128)(2,1)} %bitcast.27), custom_call_target="tpu_custom_call" | custom-call | tf_op jit(solution)/shard_map/pallas_call | solution.py:93
  228.2 2.1 reduce_sum.72
  (10 shorter events, 0.1 us)
Async XLA Ops:
  6.5 55.1 %copy-start = (bf16[256,4096]{1,0:T(8,128)(2,1)S(1)}, bf16[256,4096]{1,0:T(8,128)(2,1)}, u32[]{:S(2)}) copy-start(bf16[256,4096]{1,0:T(8,128)(2,1)} %param.17) | copy-start | bytes 6291460
  6.5 44.6 %copy-start.6 = (s32[16]{0:T(128)S(1)}, s32[16]{0:T(128)}, u32[]{:S(2)}) copy-start(s32[16]{0:T(128)} %param.20) | copy-start | bytes 196
  6.5 47.3 %copy-start.7 = (s32[16]{0:T(128)S(1)}, s32[16]{0:T(128)}, u32[]{:S(2)}) copy-start(s32[16]{0:T(128)} %param.21) | copy-start | bytes 196
  6.5 52.3 %all-gather.2.cloned.1.call-start = ((), (), s32[]{:S(2)}) async-start(), calls=%async_computation | async-start | bytes 2506752 | tf_op jit(solution)/shard_map/all_gather | solution.py:139
  11.9 44.3 %copy-start.5 = (f32[256]{0:T(256)S(1)}, f32[256]{0:T(256)}, u32[]{:S(2)}) copy-start(f32[256]{0:T(256)} %param.15) | copy-start | bytes 3076
  11.9 44.4 %copy-start.4 = (f32[768]{0:T(1024)S(1)}, f32[768]{0:T(1024)}, u32[]{:S(2)}) copy-start(f32[768]{0:T(1024)} %param.14) | copy-start | bytes 9220
  160.2 5.1 %copy-start.2 = (bf16[32,32,256]{2,1,0:T(8,128)(2,1)S(1)}, bf16[32,32,256]{2,1,0:T(8,128)(2,1)}, u32[]{:S(2)}) copy-start(bf16[32,32,256]{2,1,0:T(8,128)(2,1)} %get-tuple-element.10) | copy-start | bytes 1572868
  165.2 1.8 copy-start.3
  176.1 3.3 %copy-start.1 = (f32[256,8448]{1,0:T(8,128)}, f32[256,8448]{1,0:T(8,128)S(1)}, u32[]{:S(2)}) copy-start(f32[256,8448]{1,0:T(8,128)S(1)} %get-tuple-element.20) | copy-start | bytes 25952260
Sparse Core Ops, SparseCore 0:
  9.5 47.9 all-gather.1

commit v5 on v4

--- a/solution.py
+++ b/solution.py
@@ -128,8 +128,10 @@
     cached_count = cache_len[slot_index]
     live_count = new_len[row_id]
     partial_sums = jnp.dot(tokens, w_down, preferred_element_type=jnp.float32)
-    (pieces,) = exchange([partial_sums.reshape(columns, own_rows, -1)], [False], "col", 0)
-    combined = jnp.sum(pieces, 0)
+    (pieces,) = exchange(
+        [partial_sums.astype(jnp.bfloat16).reshape(columns, -1, 128)], [False], "col", 0
+    )
+    combined = jnp.sum(pieces.astype(jnp.float32), 0).reshape(own_rows, -1)
     own_position = cached_count + column_id * own_rows + jnp.arange(own_rows, dtype=jnp.int32)
     own_cos, own_sin = angle_tables(own_position, ROPE)
     own_query = rms_scale(combined[:, :q_width], q_gain).astype(jnp.bfloat16)

time: 239 us -> 239 us (level)
  Pallas kernels: 165 us -> 154 us
  waiting for transfers between devices: 0.73 us -> 11.7 us
    pallas_call x3, Pallas kernels: 165 us -> 154 us  [exchange(): pl.pallas_call(functools.partial(_exchange_kernel, n, axis, tuple(modes))...]
    all_gather x1, waiting for transfers between devices: 0.02 us -> 11 us  [body(): segment = lax.all_gather(latent_cache, 'row', axis=0, tiled=True)]
  transfers between devices with their start and end apart: 1 -> 1, of which waited for: 0 -> 1; matrix products, arithmetic and copies ran while one was open for 4% -> 5% of each run, Pallas kernels for 16% -> 11%
where the time goes in v5:
time: 239 us; the launch traced here: 238 us
  Pallas kernels  154 us (64%)
  local copies, waits for them, and re-layouts  26 us (11%)
  matrix products  20 us (8%)
  between operations  15.9 us (7%)
  waiting for transfers between devices  11.7 us (5%)
  other arithmetic  10.1 us (4%)
    pallas_call x3, Pallas kernels, exchange(): pl.pallas_call(functools.partial(_exchange_kernel, n, axis, tuple(modes))...  154 us
    all_gather x1, waiting for transfers between devices, body(): segment = lax.all_gather(latent_cache, 'row', axis=0, tiled=True)  11 us
    dot_general x1, matrix products, body(): jnp.einsum('qd,kd->qk', queries, all_keys, preferred_element_type=jnp.flo...  7.58 us
    dot_general x1, matrix products, body(): lax.dot_general(w_out, attended, (((0,), (1,)), ((), ())), preferred_elem...  6.81 us
    slice x1, local copies, waits for them, and re-layouts, body(): lifted_parts[:, :NOPE]  5.04 us
  transfers between devices with their start and end apart: 1, of which 1 were waited for; matrix products, arithmetic and copies ran while one was open for 5% of the time, Pallas kernels for 11%

profile of v5, /device:TPU:6, one launch (start us, length us, event | category | flops | bytes accessed | tf_op | source)
XLA Modules:
  0.0 238.0 jit_solution(6346958490622216910)
XLA Ops:
  6.5 0.0 copy-start
  6.5 0.0 all-gather.2.cloned.1.call-start
  6.5 0.7 all-gather.2.cloned.1.call-update
  7.3 1.2 dynamic_slice.16
  9.6 1.3 convolution_convert_fusion.2
  10.9 0.0 copy-start.6
  11.0 0.0 copy-start.7
  11.0 0.0 copy-start.5
  11.0 0.0 copy-start.4
  11.0 0.3 copy.38
  11.3 1.6 reshape.91.refs_0_
  12.9 25.3 %shard_map.118 = bf16[32,66,128]{2,1,0:T(8,128)(2,1)} custom-call(bf16[32,66,128]{2,1,0:T(8,128)(2,1)} %reshape.91.refs_0_), custom_call_target="tpu_custom_call" | custom-call | tf_op jit(solution)/shard_map/pallas_call | solution.py:93
  38.2 1.2 convert_reduce_fusion
  39.4 0.1 reshape.92
  40.0 0.0 copy-done.6
  40.0 0.6 dynamic_slice.18
  41.2 0.7 dynamic-slice_bitcast_fusion
  41.9 0.1 select_reduce_fusion.1
  42.0 0.6 add_compare_fusion
  42.6 0.1 reshape.97
  42.7 0.0 copy-done.7
  42.7 0.6 dynamic_slice.15
  43.4 0.1 multiply_reduce_fusion.1
  43.5 0.1 multiply_reduce_fusion
  43.6 0.1 fusion.63
  43.7 0.0 copy-done.5
  43.8 0.1 multiply_convert_fusion.1
  43.8 0.0 copy-done.4
  43.8 0.1 multiply_convert_fusion
  43.9 0.7 concatenate.26.refs_2_
  44.6 0.6 iota_compare_fusion.3
  45.2 0.6 iota_compare_fusion.2
  45.8 0.6 add_convert_fusion
  46.4 11.0 %all-gather.2.cloned.1.call-done = bf16[16,256,288]{1,2,0:T(8,128)(2,1)} async-done(((bf16[1,256,288]{1,2,0:T(8,128)(2,1)}), bf16[16,256,288]{1,2,0:T(8,128)(2,1)}) %all-gather.2.cloned.1.call-update) | async-done | bytes 2359312 | tf_op jit(solution)/shard_map/all_gather | solution.py:141
  57.4 2.2 select_reduce_fusion
  59.6 0.6 slice_bitcast_fusion.refs_1_
  60.2 0.0 copy-done
  60.2 2.0 convolution_convert_fusion
  62.2 4.1 %copy.36 = bf16[256,4096]{0,1:T(8,128)(2,1)} copy(bf16[256,4096]{1,0:T(8,128)(2,1)} %convolution_convert_fusion) | data formatting | bytes 4194304 | tf_op jit(solution)/shard_map/convert_element_type | solution.py:151
  66.3 4.1 %copy.37 = bf16[256,32,128]{2,0,1:T(8,128)(2,1)} copy(bf16[256,32,128]{0,2,1:T(8,128)(2,1)} %bitcast.24) | data formatting | bytes 4194304 | tf_op jit(solution)/shard_map/reshape | solution.py:152
  70.4 88.1 %shard_map.119 = (bf16[32,256,128]{2,1,0:T(8,128)(2,1)}, bf16[32,32,256]{2,1,0:T(8,128)(2,1)}, bf16[32,8,1056]{2,1,0:T(8,128)(2,1)}) custom-call(bf16[32,256,128]{2,1,0:T(8,128)(2,1)} %bitcast.23, bf16[32,256]{1,0:T(8,128)(2,1)} %slice_bitcast_fusion.refs_1_, bf16[8,1056]{1,0:T(8,128)(2,1)} %concatenate.26.refs_2_), custom_call_target="tpu_custom_call" | custom-call | tf_op jit(solution)/shard_map/pallas_call | solution.py:93
  158.5 0.8 slice.87
  159.4 1.1 convolution_convert_fusion.3
  160.5 0.1 copy.47
  160.6 0.1 copy.42
  160.7 0.0 copy-start.2
  160.7 5.0 %fusion.69 = (bf16[8192,64]{1,0:T(8,128)(2,1)}, bf16[8192,64]{1,0:T(8,128)(2,1)}) fusion(bf16[8192,128]{1,0:T(8,128)(2,1)} %bitcast.22), kind=kLoop, calls=%fused_computation.83 | loop fusion | bytes 4194304 | tf_op jit(solution)/shard_map/slice | solution.py:176
  165.8 0.0 copy-start.3
  165.8 0.0 copy-done.2
  165.8 1.8 copy.45
  167.6 0.0 copy-done.3
  167.6 1.2 fusion.34
  168.8 0.1 fusion.52
  168.9 0.1 copy.43
  169.0 7.6 %fusion.71 = (f32[256]{0:T(256)S(1)}, f32[256,8448]{1,0:T(8,128)S(1)}) fusion(bf16[256,96]{1,0:T(8,128)(2,1)S(1)} %copy.42, bf16[8192,32]{1,0:T(8,128)(2,1)} %bitcast.26, bf16[8192,64]{1,0:T(8,128)(2,1)} %get-tuple-element.11, bf16[256,16]{0,1:T(8,128)(2,1)S(1)} %get-tuple-element.14, bf16[256,16]{0,1:T(8,128)(2,1)S(1)} %get-tuple-element.13, ...), kind=kOutput, calls=%fused_computation.85 | convolution fusion | flops 428900096 | bytes 10396928 | tf_op jit(solution)/shard_map/qd,kd->qk/dot_general | solution.py:202
  176.6 0.0 copy-start.1
  176.6 1.4 fusion.1
  178.0 1.9 copy-done.1
  179.9 6.8 %fusion.6 = bf16[2560,256]{0,1:T(8,128)(2,1)S(1)} fusion(bf16[64,2560]{1,0:T(8,128)(2,1)} %param.18, bf16[256,64]{1,0:T(8,128)(2,1)S(1)} %copy.43, bf16[8192,64]{1,0:T(8,128)(2,1)} %get-tuple-element.12, f32[256,8448]{1,0:T(8,128)} %copy-done.1, f32[256]{0:T(256)S(1)} %get-tuple-element.19, f32[256]{0:T(256)S(1)} %fusion.1, ...), kind=kOutput, calls=%fused_computation.10 | convolution fusion | flops 367902720 | bytes 11372800 | tf_op jit(solution)/shard_map/dot_general | solution.py:215
  186.8 1.5 copy.44
  188.2 40.8 %shard_map.120 = bf16[32,80,256]{2,1,0:T(8,128)(2,1)} custom-call(bf16[32,80,256]{2,1,0:T(8,128)(2,1)} %bitcast.25), custom_call_target="tpu_custom_call" | custom-call | tf_op jit(solution)/shard_map/pallas_call | solution.py:93
  229.1 2.1 reduce_sum.72
  (10 shorter events, 0.1 us)
Async XLA Ops:
  6.5 53.7 %copy-start = (bf16[256,4096]{1,0:T(8,128)(2,1)S(1)}, bf16[256,4096]{1,0:T(8,128)(2,1)}, u32[]{:S(2)}) copy-start(bf16[256,4096]{1,0:T(8,128)(2,1)} %param.17) | copy-start | bytes 6291460
  6.5 50.9 %all-gather.2.cloned.1.call-start = ((), (), s32[]{:S(2)}) async-start(), calls=%async_computation | async-start | bytes 2506752 | tf_op jit(solution)/shard_map/all_gather | solution.py:141
  10.9 29.1 %copy-start.6 = (s32[16]{0:T(128)S(1)}, s32[16]{0:T(128)}, u32[]{:S(2)}) copy-start(s32[16]{0:T(128)} %param.20) | copy-start | bytes 196
  11.0 31.8 %copy-start.7 = (s32[16]{0:T(128)S(1)}, s32[16]{0:T(128)}, u32[]{:S(2)}) copy-start(s32[16]{0:T(128)} %param.21) | copy-start | bytes 196
  11.0 32.8 %copy-start.5 = (f32[256]{0:T(256)S(1)}, f32[256]{0:T(256)}, u32[]{:S(2)}) copy-start(f32[256]{0:T(256)} %param.15) | copy-start | bytes 3076
  11.0 32.9 %copy-start.4 = (f32[768]{0:T(1024)S(1)}, f32[768]{0:T(1024)}, u32[]{:S(2)}) copy-start(f32[768]{0:T(1024)} %param.14) | copy-start | bytes 9220
  160.7 5.1 %copy-start.2 = (bf16[32,32,256]{2,1,0:T(8,128)(2,1)S(1)}, bf16[32,32,256]{2,1,0:T(8,128)(2,1)}, u32[]{:S(2)}) copy-start(bf16[32,32,256]{2,1,0:T(8,128)(2,1)} %get-tuple-element.10) | copy-start | bytes 1572868
  165.8 1.8 copy-start.3
  176.6 3.3 %copy-start.1 = (f32[256,8448]{1,0:T(8,128)}, f32[256,8448]{1,0:T(8,128)S(1)}, u32[]{:S(2)}) copy-start(f32[256,8448]{1,0:T(8,128)S(1)} %get-tuple-element.20) | copy-start | bytes 25952260
Sparse Core Ops, SparseCore 0:
  9.5 47.8 all-gather.1

commit v6 on v5

--- a/solution.py
+++ b/solution.py
@@ -101,6 +101,74 @@
         ],
         compiler_params=pltpu.CompilerParams(collective_id=collective_id, has_side_effects=True),
     )(*arrays)
+
+
+def _attention_kernel(
+    scale, q_nope_ref, q_rope_ref, lifted_ref, rope_ref, bias_ref, fresh_keys_ref,
+    fresh_values_ref, fresh_bias_ref, out_ref, scores_ref,
+):
+    blocks, _, width = rope_ref.shape
+    q_nope = q_nope_ref[...]
+    q_rope = q_rope_ref[...]
+    transposed = (((1,), (1,)), ((), ()))
+    fresh = (
+        lax.dot_general(
+            jnp.concatenate([q_nope, q_rope], 1), fresh_keys_ref[...], transposed,
+            preferred_element_type=jnp.float32,
+        )
+        * scale
+        + fresh_bias_ref[...]
+    )
+
+    def score(j, peak):
+        rows = pl.ds(pl.multiple_of(j * width, width), width)
+        block = (
+            lax.dot_general(
+                q_nope, lifted_ref[rows, pl.ds(0, NOPE)], transposed,
+                preferred_element_type=jnp.float32,
+            )
+            + jnp.dot(q_rope, rope_ref[j], preferred_element_type=jnp.float32)
+        ) * scale + bias_ref[pl.ds(j, 1), :]
+        scores_ref[:, rows] = block
+        return jnp.maximum(peak, jnp.max(block, axis=1, keepdims=True))
+
+    peak = lax.fori_loop(0, blocks, score, jnp.max(fresh, axis=1, keepdims=True))
+    fresh_exp = jnp.exp(fresh - peak)
+    start = (
+        jnp.sum(fresh_exp, axis=1, keepdims=True),
+        jnp.dot(
+            fresh_exp.astype(jnp.bfloat16), fresh_values_ref[...],
+            preferred_element_type=jnp.float32,
+        ),
+    )
+
+    def accumulate(j, carry):
+        total, summed = carry
+        rows = pl.ds(pl.multiple_of(j * width, width), width)
+        exponent = jnp.exp(scores_ref[:, rows] - peak)
+        return (
+            total + jnp.sum(exponent, axis=1, keepdims=True),
+            summed
+            + jnp.dot(
+                exponent.astype(jnp.bfloat16), lifted_ref[rows, pl.ds(NOPE, VDIM)],
+                preferred_element_type=jnp.float32,
+            ),
+        )
+
+    total, summed = lax.fori_loop(0, blocks, accumulate, start)
+    out_ref[...] = (summed / total).astype(out_ref.dtype)
+
+
+def attention(q_nope, q_rope, lifted, rope, bias, fresh_keys, fresh_values, fresh_bias):
+    rows = q_nope.shape[0]
+    vmem = pl.BlockSpec(memory_space=pltpu.VMEM)
+    return pl.pallas_call(
+        functools.partial(_attention_kernel, 1.0 / math.sqrt(NOPE + ROPE)),
+        out_shape=jax.ShapeDtypeStruct((rows, VDIM), jnp.bfloat16),
+        in_specs=[vmem] * 8,
+        out_specs=vmem,
+        scratch_shapes=[pltpu.VMEM((rows, lifted.shape[0]), jnp.float32)],
+    )(q_nope, q_rope, lifted, rope, bias, fresh_keys, fresh_values, fresh_bias)
 
 
 def body(
@@ -170,16 +238,6 @@
     fresh_lifted = jnp.dot(
         fresh_latents[:, :kv_width], head_weight, preferred_element_type=jnp.float32
     ).astype(jnp.bfloat16)
-    all_keys = jnp.concatenate(
-        [
-            jnp.concatenate(
-                [lifted_parts[:, :NOPE], rope_parts.transpose(0, 2, 1).reshape(key_total, ROPE)], 1
-            ),
-            jnp.concatenate([fresh_lifted[:, :NOPE], fresh_latents[:, kv_width:]], 1),
-        ],
-        0,
-    )
-    all_values = jnp.concatenate([lifted_parts[:, NOPE:], fresh_lifted[:, NOPE:]], 0)
     page_row = page_table[slot_index]
     page_count = page_row.shape[0]
     page_size = key_total // page_count
@@ -195,21 +253,18 @@
     query_index = jnp.arange(group_rows, dtype=jnp.int32)[:, None]
     key_index = jnp.arange(group_rows, dtype=jnp.int32)[None, :]
     fresh_visible = (key_index <= query_index) & (key_index < live_count)
-    visible = jnp.concatenate(
-        [jnp.broadcast_to(cached_visible[None, :], (group_rows, key_total)), fresh_visible], 1
-    )
-    scores = (
-        jnp.einsum("qd,kd->qk", queries, all_keys, preferred_element_type=jnp.float32)
-        * score_scale
-    )
-    scores = jnp.where(visible, scores, -jnp.inf)
-    row_peak = jnp.max(scores, 1, keepdims=True)
-    exponent = jnp.exp(scores - row_peak)
-    row_total = jnp.sum(exponent, 1)
-    summed = jnp.dot(
-        exponent.astype(jnp.bfloat16), all_values, preferred_element_type=jnp.float32
-    )
-    attended = (summed / row_total[:, None]).astype(jnp.bfloat16)
+    fresh_bias = jnp.where(fresh_visible, 0.0, -jnp.inf).astype(jnp.float32)
+    cached_bias = jnp.where(cached_visible, 0.0, -jnp.inf).astype(jnp.float32)
+    attended = attention(
+        queries[:, :NOPE],
+        queries[:, NOPE:],
+        lifted_parts,
+        rope_parts,
+        cached_bias.reshape(columns, chunk),
+        jnp.concatenate([fresh_lifted[:, :NOPE], fresh_latents[:, kv_width:]], 1),
+        fresh_lifted[:, NOPE:],
+        fresh_bias,
+    )
     live_rows = jnp.arange(group_rows, dtype=jnp.int32) < live_count
     attended = jnp.where(live_rows[:, None], attended, jnp.zeros_like(attended))
     out_parts = lax.dot_general(

time: 239 us -> 239 us (level)
  Pallas kernels: 154 us -> 175 us
  matrix products: 20 us -> 7.22 us
  local copies, waits for them, and re-layouts: 26 us -> 19.4 us
    pallas_call x0 -> x1, Pallas kernels: none -> 20.5 us  [attention(): pl.pallas_call(functools.partial(_attention_kernel, 1.0 / math.sqrt(NOPE...]
    dot_general x1 -> x0, matrix products: 7.58 us -> none  [body(): jnp.einsum('qd,kd->qk', queries, all_keys, preferred_element_type=jnp.flo...]
    dot_general x1, matrix products: 6.81 us -> 1.55 us  [body(): lax.dot_general(w_out, attended, (((0,), (1,)), ((), ())), preferred_elem...]
    slice x2 -> x0, local copies, waits for them, and re-layouts: 5.05 us -> none  [the longest x1 5.04 us: body(): lifted_parts[:, :NOPE]]
where the time goes in v6:
time: 239 us; the launch traced here: 238 us
  Pallas kernels  175 us (73%)
  local copies, waits for them, and re-layouts  19.4 us (8%)
  between operations  16.1 us (7%)
  other arithmetic  10.7 us (4%)
  waiting for transfers between devices  9.85 us (4%)
  matrix products  7.22 us (3%)
    pallas_call x3, Pallas kernels, exchange(): pl.pallas_call(functools.partial(_exchange_kernel, n, axis, tuple(modes))...  154 us
    pallas_call x1, Pallas kernels, attention(): pl.pallas_call(functools.partial(_attention_kernel, 1.0 / math.sqrt(NOPE...  20.5 us
    all_gather x1, waiting for transfers between devices, body(): segment = lax.all_gather(latent_cache, 'row', axis=0, tiled=True)  9.14 us
  transfers between devices with their start and end apart: 1, of which 1 were waited for; matrix products, arithmetic and copies ran while one was open for 5% of the time, Pallas kernels for 11%

profile of v6, /device:TPU:6, one launch (start us, length us, event | category | flops | bytes accessed | tf_op | source)
XLA Modules:
  0.0 238.1 jit_solution(14155761503954336116)
XLA Ops:
  6.5 0.0 copy-start
  6.5 0.0 all-gather.2.cloned.1.call-start
  6.5 0.7 all-gather.2.cloned.1.call-update
  7.3 1.2 dynamic_slice.16
  9.8 1.3 convolution_convert_fusion.2
  11.1 0.0 copy-start.4
  11.1 0.0 copy-start.5
  11.1 0.0 copy-start.2
  11.2 0.0 copy-start.1
  11.2 0.3 copy.43
  11.5 1.6 reshape.83.refs_0_
  13.0 25.3 %shard_map.118 = bf16[32,66,128]{2,1,0:T(8,128)(2,1)} custom-call(bf16[32,66,128]{2,1,0:T(8,128)(2,1)} %reshape.83.refs_0_), custom_call_target="tpu_custom_call" | custom-call | tf_op jit(solution)/shard_map/pallas_call | solution.py:93
  38.4 1.2 convert_reduce_fusion
  39.5 0.1 reshape.84
  40.3 0.0 copy-done.4
  40.3 0.6 dynamic_slice.17
  40.9 0.7 dynamic-slice_bitcast_fusion
  41.6 0.1 select_reduce_fusion.1
  41.7 0.1 mul.148
  41.8 0.1 add.88
  41.9 0.1 add.89
  42.0 0.1 add.91
  42.1 0.0 copy-done.5
  42.1 0.6 dynamic_slice.15
  43.3 0.1 multiply_reduce_fusion.1
  43.4 0.1 multiply_reduce_fusion
  43.5 0.1 fusion.27
  43.6 0.0 copy-done.2
  43.6 0.1 multiply_convert_fusion.1
  43.7 0.0 copy-done.1
  43.7 0.1 multiply_convert_fusion
  43.8 0.7 concatenate.14.refs_2_
  44.5 0.7 iota_compare_fusion.3
  45.1 0.6 iota_compare_fusion.2
  45.8 0.6 add_convert_fusion
  46.3 1.2 fusion.11.bias_ref
  47.5 0.7 fusion.4.fresh_bias_ref
  48.2 9.1 %all-gather.2.cloned.1.call-done = bf16[16,256,288]{1,2,0:T(8,128)(2,1)} async-done(((bf16[1,256,288]{1,2,0:T(8,128)(2,1)}), bf16[16,256,288]{1,2,0:T(8,128)(2,1)}) %all-gather.2.cloned.1.call-update) | async-done | bytes 2359312 | tf_op jit(solution)/shard_map/all_gather | solution.py:209
  57.4 2.2 select_reduce_fusion
  59.6 0.6 slice_bitcast_fusion.refs_1_
  60.2 0.0 copy-done
  60.2 2.0 convolution_convert_fusion
  62.2 4.1 %copy.41 = bf16[256,4096]{0,1:T(8,128)(2,1)} copy(bf16[256,4096]{1,0:T(8,128)(2,1)} %convolution_convert_fusion) | data formatting | bytes 4194304 | tf_op jit(solution)/shard_map/convert_element_type | solution.py:219
  66.3 4.1 %copy.42 = bf16[256,32,128]{2,0,1:T(8,128)(2,1)} copy(bf16[256,32,128]{0,2,1:T(8,128)(2,1)} %bitcast.21) | data formatting | bytes 4194304 | tf_op jit(solution)/shard_map/reshape | solution.py:220
  70.4 0.0 copy-start.3
  70.4 88.3 %shard_map.119 = (bf16[32,256,128]{2,1,0:T(8,128)(2,1)}, bf16[32,32,256]{2,1,0:T(8,128)(2,1)}, bf16[32,8,1056]{2,1,0:T(8,128)(2,1)}) custom-call(bf16[32,256,128]{2,1,0:T(8,128)(2,1)} %bitcast.20, bf16[32,256]{1,0:T(8,128)(2,1)} %slice_bitcast_fusion.refs_1_, bf16[8,1056]{1,0:T(8,128)(2,1)} %concatenate.14.refs_2_), custom_call_target="tpu_custom_call" | custom-call | tf_op jit(solution)/shard_map/pallas_call | solution.py:93
  158.7 0.8 slice.81
  159.6 1.1 convolution_convert_fusion.3
  160.6 0.7 fusion.30
  161.4 0.0 copy-done.3
  161.4 1.3 fusion.1
  162.6 0.1 fusion.17
  162.8 0.7 copy.46.q_rope_ref
  163.5 0.7 copy.49.q_nope_ref
  164.2 0.7 pad_maximum_fusion.fresh_keys_ref
  164.9 20.5 %shard_map.120 = bf16[256,64]{1,0:T(8,128)(2,1)} custom-call(bf16[256,64]{1,0:T(8,128)(2,1)} %copy.49.q_nope_ref, bf16[256,32]{1,0:T(8,128)(2,1)} %copy.46.q_rope_ref, bf16[8192,128]{1,0:T(8,128)(2,1)} %bitcast.23, bf16[32,32,256]{2,1,0:T(8,128)(2,1)} %get-tuple-element.10.rope_ref, f32[32,256]{1,0:T(8,128)} %fusion.11.bias_ref, ...), custom_call_target="tpu_custom_call" | custom-call | tf_op jit(solution)/shard_map/pallas_call | solution.py:165
  185.5 1.5 fusion
  187.0 1.5 copy.47
  188.5 40.6 %shard_map.121 = bf16[32,80,256]{2,1,0:T(8,128)(2,1)} custom-call(bf16[32,80,256]{2,1,0:T(8,128)(2,1)} %bitcast.22), custom_call_target="tpu_custom_call" | custom-call | tf_op jit(solution)/shard_map/pallas_call | solution.py:93
  229.2 2.1 reduce_sum.62
  (8 shorter events, 0.1 us)
Async XLA Ops:
  6.5 53.6 %copy-start = (bf16[256,4096]{1,0:T(8,128)(2,1)S(1)}, bf16[256,4096]{1,0:T(8,128)(2,1)}, u32[]{:S(2)}) copy-start(bf16[256,4096]{1,0:T(8,128)(2,1)} %param.17) | copy-start | bytes 6291460
  6.5 50.8 %all-gather.2.cloned.1.call-start = ((), (), s32[]{:S(2)}) async-start(), calls=%async_computation | async-start | bytes 2506752 | tf_op jit(solution)/shard_map/all_gather | solution.py:209
  11.1 29.2 %copy-start.4 = (s32[16]{0:T(128)S(1)}, s32[16]{0:T(128)}, u32[]{:S(2)}) copy-start(s32[16]{0:T(128)} %param.20) | copy-start | bytes 196
  11.1 30.9 %copy-start.5 = (s32[16]{0:T(128)S(1)}, s32[16]{0:T(128)}, u32[]{:S(2)}) copy-start(s32[16]{0:T(128)} %param.21) | copy-start | bytes 196
  11.1 32.5 %copy-start.2 = (f32[256]{0:T(256)S(1)}, f32[256]{0:T(256)}, u32[]{:S(2)}) copy-start(f32[256]{0:T(256)} %param.15) | copy-start | bytes 3076
  11.2 32.6 %copy-start.1 = (f32[768]{0:T(1024)S(1)}, f32[768]{0:T(1024)}, u32[]{:S(2)}) copy-start(f32[768]{0:T(1024)} %param.14) | copy-start | bytes 9220
  70.4 91.0 %copy-start.3 = (bf16[768,96]{0,1:T(8,128)(2,1)S(1)}, bf16[768,96]{0,1:T(8,128)(2,1)}, u32[]{:S(2)}) copy-start(bf16[768,96]{0,1:T(8,128)(2,1)} %param.16) | copy-start | bytes 442372
Sparse Core Ops, SparseCore 0:
  9.5 47.8 all-gather.1

commit v7 on v5

v7 whole, which is shorter than its diff:
```python
import functools
import math

import jax
import jax.numpy as jnp
from jax import lax
from jax.experimental import pallas as pl
from jax.experimental.pallas import tpu as pltpu
from jax.sharding import PartitionSpec as P

MESH = pl.DeviceIdType.MESH

NOPE = 64
ROPE = 32
VDIM = 64


epsilon = 1e-05


def rms_scale(values, gain):
    return values * lax.rsqrt(jnp.mean(values * values, axis=-1, keepdims=True) + epsilon) * gain


def angle_tables(positions, width):
    half_dim = width // 2
    frequency = 10000.0 ** (-2.0 * jnp.arange(half_dim, dtype=jnp.float32) / width)
    angles = positions.astype(jnp.float32)[:, None] * frequency[None, :]
    return (jnp.cos(angles), jnp.sin(angles))


def rotary(values, cosine, sine_table):
    half_dim = values.shape[-1] // 2
    first_half = values[..., :half_dim]
    second_half = values[..., half_dim:]
    return jnp.concatenate(
        [
            first_half * cosine - second_half * sine_table,
            second_half * cosine + first_half * sine_table,
        ],
        -1,
    )


PLANE_X = 4


def _group_size(group, n):
    return {"all": n, "x": PLANE_X, "y": n // PLANE_X}[group]


def _group_peer(group, n, me, k):
    if group == "x":
        return (me // PLANE_X) * PLANE_X + lax.rem(me % PLANE_X + k, PLANE_X)
    if group == "y":
        return lax.rem(me // PLANE_X + k, n // PLANE_X) * PLANE_X + me % PLANE_X
    return lax.rem(me + k, n)


def _group_slot(group, device):
    if group == "x":
        return device % PLANE_X
    if group == "y":
        return device // PLANE_X
    return device


def _exchange_kernel(n, plan, *refs):
    count = len(plan)
    sources, targets = refs[:count], refs[count : 2 * count]
    send_sem, recv_sem = refs[2 * count :]
    me = lax.axis_index("col")
    barrier = pltpu.get_barrier_semaphore()
    for k in range(1, n):
        pl.semaphore_signal(
            barrier, inc=1, device_id={"col": lax.rem(me + k, n)}, device_id_type=MESH
        )
    pl.semaphore_wait(barrier, n - 1)

    def remote(a, k, peer, landing):
        group, gather = plan[a]
        x_ref = sources[a]
        return pltpu.make_async_remote_copy(
            src_ref=x_ref if gather else x_ref.at[_group_slot(group, peer)],
            dst_ref=targets[a].at[landing],
            send_sem=send_sem.at[a, k],
            recv_sem=recv_sem.at[a, k],
            device_id={"col": peer},
            device_id_type=MESH,
        )

    sends = []
    for a, (group, gather) in enumerate(plan):
        for k in range(1, _group_size(group, n)):
            copy = remote(a, k, _group_peer(group, n, me, k), _group_slot(group, me))
            copy.start()
            sends.append(copy)
    for a, (group, gather) in enumerate(plan):
        mine = _group_slot(group, me)
        if gather:
            targets[a][mine] = sources[a][...]
        else:
            targets[a][mine] = sources[a][mine]
    for copy in sends:
        copy.wait_send()
    for a, (group, gather) in enumerate(plan):
        size = _group_size(group, n)
        for k in range(1, size):
            source = _group_peer(group, n, me, size - k)
            remote(a, k, source, _group_slot(group, source)).wait_recv()


def exchange(arrays, plan, collective_id):
    n = lax.axis_size("col")
    shapes = [
        jax.ShapeDtypeStruct(
            ((_group_size(group, n),) + x.shape) if gather else x.shape, x.dtype
        )
        for x, (group, gather) in zip(arrays, plan)
    ]
    return pl.pallas_call(
        functools.partial(_exchange_kernel, n, tuple(plan)),
        out_shape=shapes,
        in_specs=[pl.BlockSpec(memory_space=pltpu.VMEM)] * len(arrays),
        out_specs=[pl.BlockSpec(memory_space=pltpu.VMEM)] * len(arrays),
        scratch_shapes=[
            pltpu.SemaphoreType.DMA((len(arrays), n)),
            pltpu.SemaphoreType.DMA((len(arrays), n)),
        ],
        compiler_params=pltpu.CompilerParams(collective_id=collective_id, has_side_effects=True),
    )(*arrays)


def body(
    tokens,
    w_down,
    q_gain,
    kv_gain,
    w_q_up,
    w_kv_up,
    w_out,
    latent_cache,
    cache_len,
    new_len,
    page_table,
    home_slot,
):
    columns = lax.axis_size("col")
    column_id = lax.axis_index("col")
    row_id = lax.axis_index("row")
    lines = columns // PLANE_X
    line_id = column_id // PLANE_X
    lane_id = column_id % PLANE_X
    group_rows = tokens.shape[0]
    own_rows = group_rows // columns
    q_width = q_gain.shape[0]
    kv_width = kv_gain.shape[0]
    slot_index = home_slot[row_id]
    cached_count = cache_len[slot_index]
    live_count = new_len[row_id]
    partial_sums = jnp.dot(tokens, w_down, preferred_element_type=jnp.float32)
    (pieces,) = exchange(
        [partial_sums.astype(jnp.bfloat16).reshape(columns, -1, 128)], [("all", False)], 0
    )
    combined = jnp.sum(pieces.astype(jnp.float32), 0).reshape(own_rows, -1)
    own_position = cached_count + column_id * own_rows + jnp.arange(own_rows, dtype=jnp.int32)
    own_cos, own_sin = angle_tables(own_position, ROPE)
    own_query = rms_scale(combined[:, :q_width], q_gain).astype(jnp.bfloat16)
    own_latent = rms_scale(combined[:, q_width : q_width + kv_width], kv_gain).astype(jnp.bfloat16)
    own_rope = rotary(combined[:, q_width + kv_width :], own_cos, own_sin).astype(jnp.bfloat16)
    own_rows_all = jnp.concatenate([own_query, own_latent, own_rope], 1)
    segment = lax.all_gather(latent_cache, "row", axis=0, tiled=True)
    matches = jnp.arange(segment.shape[0], dtype=jnp.int32) == slot_index
    own_cache = jnp.sum(
        jnp.where(matches[:, None, None], segment.astype(jnp.float32), 0.0), 0
    ).astype(jnp.bfloat16)
    chunk = own_cache.shape[0]
    cache_parts, all_rows = exchange(
        [own_cache.T, own_rows_all], [("x", True), ("all", True)], 2
    )
    all_rows = all_rows.reshape(group_rows, -1)
    query_latent = all_rows[:, :q_width]
    fresh_latents = all_rows[:, q_width:]
    query_cos, query_sin = angle_tables(
        cached_count + jnp.arange(group_rows, dtype=jnp.int32), ROPE
    )
    projected = jnp.dot(query_latent, w_q_up, preferred_element_type=jnp.float32)
    queries = jnp.concatenate(
        [projected[:, :NOPE], rotary(projected[:, NOPE:], query_cos, query_sin)], 1
    ).astype(jnp.bfloat16)
    (head_queries,) = exchange([queries], [("y", True)], 1)
    head_width = NOPE + VDIM
    heads = columns
    line_weight = lax.dynamic_index_in_dim(
        w_kv_up.reshape(kv_width, lines, PLANE_X, head_width), lane_id, axis=2, keepdims=False
    ).reshape(kv_width, lines * head_width)
    span = PLANE_X * chunk
    span_latents = cache_parts[:, :kv_width, :].transpose(0, 2, 1).reshape(span, kv_width)
    span_rope = cache_parts[:, kv_width:, :].transpose(0, 2, 1).reshape(span, ROPE)
    span_lifted = (
        jnp.dot(span_latents, line_weight, preferred_element_type=jnp.float32)
        .astype(jnp.bfloat16)
        .reshape(span, lines, head_width)
    )
    fresh_lifted = (
        jnp.dot(fresh_latents[:, :kv_width], line_weight, preferred_element_type=jnp.float32)
        .astype(jnp.bfloat16)
        .reshape(group_rows, lines, head_width)
    )
    fresh_rope = fresh_latents[:, kv_width:]
    q_nope = head_queries[:, :, :NOPE]
    q_rope = head_queries[:, :, NOPE:]
    score_scale = 1.0 / math.sqrt(NOPE + ROPE)

    def score(lifted, rope):
        return (
            jnp.einsum("hqd,khd->hqk", q_nope, lifted[:, :, :NOPE], preferred_element_type=jnp.float32)
            + jnp.einsum("hqd,kd->hqk", q_rope, rope, preferred_element_type=jnp.float32)
        ) * score_scale

    key_total = columns * chunk
    page_row = page_table[slot_index]
    page_count = page_row.shape[0]
    page_size = key_total // page_count
    offsets = jnp.arange(page_size, dtype=jnp.int32)
    page_ids = jnp.arange(page_count, dtype=jnp.int32)
    logical_page = jnp.sum(
        page_ids[:, None] * (page_row[:, None] == page_ids[None, :]).astype(jnp.int32), 0
    )
    cached_visible = (logical_page[:, None] * page_size + offsets[None, :]).reshape(
        key_total
    ) < cached_count
    span_visible = lax.dynamic_slice_in_dim(cached_visible, line_id * span, span, 0)
    share = group_rows // lines
    query_index = jnp.arange(group_rows, dtype=jnp.int32)[:, None]
    key_index = jnp.arange(group_rows, dtype=jnp.int32)[None, :]
    fresh_visible = (
        (key_index <= query_index) & (key_index < live_count) & (key_index // share == line_id)
    )
    visible = jnp.concatenate(
        [jnp.broadcast_to(span_visible[None, :], (group_rows, span)), fresh_visible], 1
    )
    scores = jnp.concatenate(
        [score(span_lifted, span_rope), score(fresh_lifted, fresh_rope)], 2
    )
    scores = jnp.where(visible[None], scores, -jnp.inf)
    row_peak = jnp.max(scores, 2)
    safe_peak = jnp.where(row_peak == -jnp.inf, 0.0, row_peak)
    exponent = jnp.exp(scores - safe_peak[:, :, None])
    row_total = jnp.sum(exponent, 2)
    values = jnp.concatenate([span_lifted[:, :, NOPE:], fresh_lifted[:, :, NOPE:]], 0)
    summed = jnp.einsum(
        "hqk,khd->hdq", exponent.astype(jnp.bfloat16), values, preferred_element_type=jnp.float32
    )
    stats = jnp.stack([row_peak, row_total], 1)
    summed_parts, stat_parts = exchange([summed, stats], [("y", False), ("y", False)], 4)
    peak = jnp.max(stat_parts[:, 0, :], 0)
    factor = jnp.exp(stat_parts[:, 0, :] - peak[None, :])
    total = jnp.sum(factor * stat_parts[:, 1, :], 0)
    merged = jnp.sum(factor[:, None, :] * summed_parts, 0)
    attended = (merged / total[None, :]).astype(jnp.bfloat16)
    live_rows = jnp.arange(group_rows, dtype=jnp.int32) < live_count
    attended = jnp.where(live_rows[None, :], attended, jnp.zeros_like(attended))
    out_parts = lax.dot_general(
        w_out, attended, (((0,), (0,)), ((), ())), preferred_element_type=jnp.float32
    ).astype(jnp.bfloat16)
    (out_pieces,) = exchange([out_parts.reshape(columns, -1, group_rows)], [("all", False)], 3)
    summed_out = jnp.sum(out_pieces.astype(jnp.float32), 0)
    result = summed_out.T.astype(jnp.bfloat16)
    return result


def solution(mesh):
    return jax.shard_map(
        body,
        mesh=mesh,
        in_specs=(
            P("row", "col"),
            P("col", None),
            P(),
            P(),
            P(None, "col"),
            P(),
            P("col", None),
            P("row", "col", None),
            P(),
            P(),
            P(),
            P(),
        ),
        out_specs=P("row", "col"),
        check_vma=False,
    )
```

time: 239 us -> 230 us (0.962)
  Pallas kernels: 154 us -> 134 us
  other arithmetic: 10.1 us -> 25.2 us
  matrix products: 20 us -> 25.9 us
  local copies, waits for them, and re-layouts: 26 us -> 20.6 us
  waiting for transfers between devices: 11.7 us -> 7.11 us
    pallas_call x3 -> x5, Pallas kernels: 154 us -> 134 us  [exchange(): pl.pallas_call(functools.partial(_exchange_kernel, n, tuple(plan)), out_s...]
    reduce_sum x1 -> x3, other arithmetic: 1.39 us -> 7.4 us  [the longest x1 6.28 us: body(): row_total = jnp.sum(exponent, 2)]
    dot_general x4 -> x8, matrix products: 17.5 us -> 23.4 us  [the longest x2 9.48 us: score(): jnp.einsum('hqd,kd->hqk', q_rope, rope, preferred_element_type=jnp.float32)]
    reduce_max x0 -> x2, other arithmetic: none -> 5.7 us  [the longest x1 5.68 us: body(): row_peak = jnp.max(scores, 2)]
    reshape x2, local copies, waits for them, and re-layouts: 5.87 us -> 1.28 us  [the longest x1 1.24 us: body(): fresh_lifted = jnp.dot(fresh_latents[:, :kv_width], line_weight, preferre...]
    all_gather x1, waiting for transfers between devices: 11 us -> 6.4 us  [body(): segment = lax.all_gather(latent_cache, 'row', axis=0, tiled=True)]
    transpose x1 -> x4, local copies, waits for them, and re-layouts: 0.6 us -> 4.83 us  [the longest x2 3.93 us: body(): cache_parts[:, :kv_width, :].transpose(0, 2, 1).reshape(span, kv_width)]
    convert_element_type x2 -> x1, local copies, waits for them, and re-layouts: 5.56 us -> 1.46 us  [body(): out_parts = lax.dot_general(w_out, attended, (((0,), (0,)), ((), ())), pr...]
  transfers between devices with their start and end apart: 1 -> 1, of which waited for: 1 -> 1; matrix products, arithmetic and copies ran while one was open for 5% -> 7% of each run, Pallas kernels for 11% -> 11%
where the time goes in v7:
time: 230 us; the launch traced here: 229 us
  Pallas kernels  134 us (58%)
  matrix products  25.9 us (11%)
  other arithmetic  25.2 us (11%)
  local copies, waits for them, and re-layouts  20.6 us (9%)
  between operations  16.2 us (7%)
  waiting for transfers between devices  7.11 us (3%)
    pallas_call x5, Pallas kernels, exchange(): pl.pallas_call(functools.partial(_exchange_kernel, n, tuple(plan)), out_s...  134 us
    dot_general x2, matrix products, score(): jnp.einsum('hqd,kd->hqk', q_rope, rope, preferred_element_type=jnp.float32)  9.48 us
    all_gather x1, waiting for transfers between devices, body(): segment = lax.all_gather(latent_cache, 'row', axis=0, tiled=True)  6.4 us
    reduce_sum x1, other arithmetic, body(): row_total = jnp.sum(exponent, 2)  6.28 us
    dot_general x2, matrix products, score(): jnp.einsum('hqd,khd->hqk', q_nope, lifted[:, :, :NOPE], preferred_element...  6.26 us
    reduce_max x1, other arithmetic, body(): row_peak = jnp.max(scores, 2)  5.68 us
  transfers between devices with their start and end apart: 1, of which 1 were waited for; matrix products, arithmetic and copies ran while one was open for 7% of the time, Pallas kernels for 11%

profile of v7, /device:TPU:6, one launch (start us, length us, event | category | flops | bytes accessed | tf_op | source)
XLA Modules:
  0.0 229.1 jit_solution(2791712188716041066)
XLA Ops:
  6.5 0.7 all-gather.2.cloned.1.call-update
  7.3 1.2 dynamic_slice.20
  9.7 1.3 convolution_convert_fusion.1
  11.0 0.0 copy-start.9
  11.0 0.0 copy-start.10
  11.0 0.0 copy-start.7
  11.0 0.0 copy-start.6
  11.0 0.3 copy.99
  11.3 1.6 reshape.137.refs_0_
  12.9 25.3 %shard_map.118 = bf16[32,66,128]{2,1,0:T(8,128)(2,1)} custom-call(bf16[32,66,128]{2,1,0:T(8,128)(2,1)} %reshape.137.refs_0_), custom_call_target="tpu_custom_call" | custom-call | tf_op jit(solution)/shard_map/pallas_call | solution.py:121
  38.2 1.2 convert_reduce_fusion
  39.4 0.1 reshape.138
  39.5 3.5 %copy.101 = bf16[256,4096]{0,1:T(8,128)(2,1)S(1)} copy(bf16[256,4096]{1,0:T(8,128)(2,1)} %param.17) | data formatting | bytes 4194304 | tf_op args[5]
  43.0 0.6 dynamic_slice.19
  44.2 0.6 dynamic_slice.21
  45.4 0.7 dynamic-slice_bitcast_fusion
  46.1 0.1 select_reduce_fusion.1
  46.2 0.7 add_compare_fusion
  46.9 0.1 lt.52
  47.1 0.1 multiply_reduce_fusion.2
  47.2 0.1 multiply_reduce_fusion.1
  47.3 0.1 fusion.43
  47.5 0.1 multiply_convert_fusion.1
  47.5 0.1 multiply_convert_fusion
  47.6 0.7 concatenate.19.refs_1_
  48.3 0.6 iota_compare_fusion.3
  48.9 0.6 add_convert_fusion
  49.5 0.6 fusion.44
  50.2 0.8 pad_add_fusion
  51.0 6.4 %all-gather.2.cloned.1.call-done = bf16[16,256,288]{1,2,0:T(8,128)(2,1)} async-done(((bf16[1,256,288]{1,2,0:T(8,128)(2,1)}), bf16[16,256,288]{1,2,0:T(8,128)(2,1)}) %all-gather.2.cloned.1.call-update) | async-done | bytes 2359312 | tf_op jit(solution)/shard_map/all_gather | solution.py:172
  57.4 2.9 %select_reduce_fusion = bf16[256,288]{0,1:T(8,128)(2,1)} fusion(bf16[16,256,288]{1,2,0:T(8,128)(2,1)} %all-gather.2.cloned.1.call-done, pred[16]{0:T(512)(128)(4,1)S(1)} %iota_compare_fusion.3), kind=kLoop, calls=%fused_computation.8 | loop fusion | flops 3465216 | bytes 2506768 | tf_op jit(solution)/shard_map/reduce_sum | solution.py:174
  60.3 26.0 %shard_map.119 = (bf16[4,288,256]{2,1,0:T(8,128)(2,1)}, bf16[32,8,1056]{2,1,0:T(8,128)(2,1)}) custom-call(bf16[288,256]{1,0:T(8,128)(2,1)} %bitcast.59, bf16[8,1056]{1,0:T(8,128)(2,1)} %concatenate.19.refs_1_), custom_call_target="tpu_custom_call" | custom-call | tf_op jit(solution)/shard_map/pallas_call | solution.py:121
  86.3 1.3 fusion.17
  87.6 1.9 slice_bitcast_fusion
  89.5 0.8 slice_bitcast_fusion.3
  90.3 0.1 copy.128
  90.4 0.1 copy.127
  90.5 0.1 copy.126
  90.7 0.6 fusion.27
  91.2 0.7 pad_maximum_fusion.refs_0_
  92.0 18.7 %shard_map.120 = bf16[8,256,96]{2,1,0:T(8,128)(2,1)} custom-call(bf16[256,96]{1,0:T(8,128)(2,1)} %pad_maximum_fusion.refs_0_), custom_call_target="tpu_custom_call" | custom-call | tf_op jit(solution)/shard_map/pallas_call | solution.py:121
  110.7 1.5 fusion.12
  112.2 2.1 convolution_convert_fusion.3
  114.4 2.0 copy.100
  116.4 1.8 convolution_convert_fusion.2
  118.2 4.5 %fusion.10 = f32[8,256,1024]{2,1,0:T(8,128)} fusion(bf16[1024,8,128]{0,2,1:T(8,128)(2,1)S(1)} %bitcast.50, bf16[8,256,96]{2,1,0:T(8,128)(2,1)S(1)} %copy-done.2), kind=kOutput, calls=%fused_computation.20 | convolution fusion | flops 268435456 | bytes 9961472 | tf_op jit(solution)/shard_map/hqd,khd->hqk/dot_general | solution.py:217
  122.7 1.0 slice.95
  123.7 1.2 copy.124
  124.9 0.7 slice.97
  125.7 1.8 add_multiply_fusion.1
  127.5 0.1 copy.108
  127.6 7.9 %add_multiply_fusion = f32[8,256,1024]{2,1,0:T(8,128)} fusion(f32[8,256,1024]{2,1,0:T(8,128)} %fusion.10, bf16[1024,32,1]{0,1,2:T(8,128)(2,1)S(1)} %reshape.147, bf16[8,256,96]{2,1,0:T(8,128)(2,1)S(1)} %copy-done.2), kind=kOutput, calls=%fused_computation.4 | convolution fusion | flops 138412032 | bytes 17235968 | tf_op jit(solution)/shard_map/hqd,kd->hqk/dot_general | solution.py:218
  135.5 5.7 %fusion.2 = f32[8,256]{1,0:T(8,128)S(1)} fusion(f32[8,256,256]{2,1,0:T(8,128)} %add_multiply_fusion.1, f32[8,256,1024]{2,1,0:T(8,128)} %add_multiply_fusion, pred[256,1280]{1,0:T(8,128)(4,1)S(1)} %copy-done.3), kind=kLoop, calls=%fused_computation.5 | loop fusion | flops 7862272 | bytes 10821632 | tf_op jit(solution)/shard_map/reduce_max | solution.py:247
  141.3 6.3 %fusion = f32[8,256]{1,0:T(8,128)S(1)} fusion(f32[8,256,256]{2,1,0:T(8,128)} %add_multiply_fusion.1, f32[8,256,1024]{2,1,0:T(8,128)} %add_multiply_fusion, f32[8,256]{1,0:T(8,128)S(1)} %compare_select_fusion, pred[256,1280]{1,0:T(8,128)(4,1)S(1)} %copy-done.3), kind=kLoop, calls=%fused_computation.2 | loop fusion | flops 10483712 | bytes 10829824 | tf_op jit(solution)/shard_map/reduce_sum | solution.py:250
  147.6 3.2 %fusion.3.refs_0_ = f32[8,64,256]{2,1,0:T(8,128)} fusion(f32[8,256,256]{2,1,0:T(8,128)S(1)} %copy-done.1, f32[8,256,1024]{2,1,0:T(8,128)S(1)} %bitcast.49, f32[8,256]{1,0:T(8,128)S(1)} %compare_select_fusion, pred[256,1280]{1,0:T(8,128)(4,1)S(1)} %copy-done.3, bf16[256,8,64]{0,2,1:T(8,128)(2,1)S(1)} %copy-done.5, bf16[1024,8,64]{0,2,1:T(8,128)(2,1)S(1)} %copy-done.4), kind=kOutput, calls=%fused_computation.6 | convolution fusion | flops 348651520 | bytes 12656640 | tf_op jit(solution)/shard_map/hqk,khd->hdq/dot_general | solution.py:252
  150.8 0.6 pad_maximum_fusion.1.refs_1_
  151.5 24.2 %shard_map.121 = (f32[8,64,256]{2,1,0:T(8,128)}, f32[8,2,256]{2,1,0:T(2,128)}) custom-call(f32[8,64,256]{2,1,0:T(8,128)} %fusion.3.refs_0_, f32[8,2,256]{2,1,0:T(2,128)} %pad_maximum_fusion.1.refs_1_), custom_call_target="tpu_custom_call" | custom-call | tf_op jit(solution)/shard_map/pallas_call | solution.py:121
  175.7 0.7 copy.116
  176.4 0.7 slice.90
  177.2 1.1 multiply_reduce_fusion
  178.3 0.5 fusion.6
  178.8 1.5 copy.117
  180.3 39.8 %shard_map.122 = bf16[32,80,256]{2,1,0:T(8,128)(2,1)} custom-call(bf16[32,80,256]{2,1,0:T(8,128)(2,1)} %bitcast.52), custom_call_target="tpu_custom_call" | custom-call | tf_op jit(solution)/shard_map/pallas_call | solution.py:121
  220.1 2.1 reduce_sum.92
  (42 shorter events, 0.3 us)
Async XLA Ops:
  6.5 171.7 %copy-start = (bf16[64,2560]{1,0:T(8,128)(2,1)S(1)}, bf16[64,2560]{1,0:T(8,128)(2,1)}, u32[]{:S(2)}) copy-start(bf16[64,2560]{1,0:T(8,128)(2,1)} %param.18) | copy-start | bytes 983044
  6.5 50.9 %all-gather.2.cloned.1.call-start = ((), (), s32[]{:S(2)}) async-start(), calls=%async_computation | async-start | bytes 2506752 | tf_op jit(solution)/shard_map/all_gather | solution.py:172
  11.0 32.0 %copy-start.9 = (s32[16]{0:T(128)S(1)}, s32[16]{0:T(128)}, u32[]{:S(2)}) copy-start(s32[16]{0:T(128)} %param.21) | copy-start | bytes 196
  11.0 33.2 %copy-start.10 = (s32[16]{0:T(128)S(1)}, s32[16]{0:T(128)}, u32[]{:S(2)}) copy-start(s32[16]{0:T(128)} %param.20) | copy-start | bytes 196
  11.0 36.5 %copy-start.7 = (f32[256]{0:T(256)S(1)}, f32[256]{0:T(256)}, u32[]{:S(2)}) copy-start(f32[256]{0:T(256)} %param.15) | copy-start | bytes 3076
  11.0 36.5 %copy-start.6 = (f32[768]{0:T(1024)S(1)}, f32[768]{0:T(1024)}, u32[]{:S(2)}) copy-start(f32[768]{0:T(1024)} %param.14) | copy-start | bytes 9220
  39.5 46.8 %copy-start.8 = (bf16[768,96]{0,1:T(8,128)(2,1)S(1)}, bf16[768,96]{0,1:T(8,128)(2,1)}, u32[]{:S(2)}) copy-start(bf16[768,96]{0,1:T(8,128)(2,1)} %param.16) | copy-start | bytes 442372
  112.2 6.0 %copy-start.2 = (bf16[8,256,96]{2,1,0:T(8,128)(2,1)S(1)}, bf16[8,256,96]{2,1,0:T(8,128)(2,1)}, u32[]{:S(2)}) copy-start(bf16[8,256,96]{2,1,0:T(8,128)(2,1)} %shard_map.120) | copy-start | bytes 1179652
  127.6 8.0 %copy-start.3 = (pred[256,1280]{1,0:T(8,128)(4,1)S(1)}, pred[256,1280]{1,0:T(8,128)(4,1)}, u32[]{:S(2)}) copy-start(pred[256,1280]{1,0:T(8,128)(4,1)} %pad_add_fusion) | copy-start | bytes 983044
  135.5 12.1 %slice-start = ((s8[8388608]{0:T(1024)(128)(4,1)}), s8[4194304]{0:T(1024)(128)(4,1)S(1)}, s32[]{:S(2)}) async-start(s8[8388608]{0:T(1024)(128)(4,1)} %bitcast.48), calls=%async_computation.1 | async-start | bytes 8388608
  141.2 6.4 %slice-start.1 = ((s8[8388608]{0:T(1024)(128)(4,1)}), s8[4194304]{0:T(1024)(128)(4,1)S(1)}, s32[]{:S(2)}) async-start(s8[8388608]{0:T(1024)(128)(4,1)} %bitcast.48), calls=%async_computation.2 | async-start | bytes 8388608
  141.3 6.4 %copy-start.1 = (f32[8,256,256]{2,1,0:T(8,128)S(1)}, f32[8,256,256]{2,1,0:T(8,128)}, u32[]{:S(2)}) copy-start(f32[8,256,256]{2,1,0:T(8,128)} %add_multiply_fusion.1) | copy-start | bytes 6291460
  141.3 6.4 %copy-start.4 = (bf16[1024,8,64]{0,2,1:T(8,128)(2,1)S(1)}, bf16[1024,8,64]{0,2,1:T(8,128)(2,1)}, u32[]{:S(2)}) copy-start(bf16[1024,8,64]{0,2,1:T(8,128)(2,1)} %slice.95) | copy-start | bytes 3145732
  141.3 6.4 %copy-start.5 = (bf16[256,8,64]{0,2,1:T(8,128)(2,1)S(1)}, bf16[256,8,64]{0,2,1:T(8,128)(2,1)}, u32[]{:S(2)}) copy-start(bf16[256,8,64]{0,2,1:T(8,128)(2,1)} %slice.97) | copy-start | bytes 786436
Sparse Core Ops, SparseCore 0:
  9.5 47.8 all-gather.1

commit v8 on v7

--- a/solution.py
+++ b/solution.py
@@ -159,8 +159,10 @@
     cached_count = cache_len[slot_index]
     live_count = new_len[row_id]
     partial_sums = jnp.dot(tokens, w_down, preferred_element_type=jnp.float32)
-    (pieces,) = exchange(
-        [partial_sums.astype(jnp.bfloat16).reshape(columns, -1, 128)], [("all", False)], 0
+    pieces, line_query_weight = exchange(
+        [partial_sums.astype(jnp.bfloat16).reshape(columns, -1, 128), w_q_up.T],
+        [("all", False), ("y", True)],
+        0,
     )
     combined = jnp.sum(pieces.astype(jnp.float32), 0).reshape(own_rows, -1)
     own_position = cached_count + column_id * own_rows + jnp.arange(own_rows, dtype=jnp.int32)
@@ -184,11 +186,16 @@
     query_cos, query_sin = angle_tables(
         cached_count + jnp.arange(group_rows, dtype=jnp.int32), ROPE
     )
-    projected = jnp.dot(query_latent, w_q_up, preferred_element_type=jnp.float32)
-    queries = jnp.concatenate(
-        [projected[:, :NOPE], rotary(projected[:, NOPE:], query_cos, query_sin)], 1
+    projected = jnp.einsum(
+        "qk,hdk->hqd", query_latent, line_query_weight, preferred_element_type=jnp.float32
+    )
+    head_queries = jnp.concatenate(
+        [
+            projected[:, :, :NOPE],
+            rotary(projected[:, :, NOPE:], query_cos[None], query_sin[None]),
+        ],
+        2,
     ).astype(jnp.bfloat16)
-    (head_queries,) = exchange([queries], [("y", True)], 1)
     head_width = NOPE + VDIM
     heads = columns
     line_weight = lax.dynamic_index_in_dim(

time: 230 us -> 212 us (0.922)
  matrix products: 25.9 us -> 15.4 us
  waiting for transfers between devices: 7.11 us -> 0.71 us
    all_gather x1, waiting for transfers between devices: 6.4 us -> 0.01 us  [body(): segment = lax.all_gather(latent_cache, 'row', axis=0, tiled=True)]
    dot_general x2, matrix products: 6.26 us -> 1.76 us  [score(): jnp.einsum('hqd,khd->hqk', q_nope, lifted[:, :, :NOPE], preferred_element...]
    transpose x2, local copies, waits for them, and re-layouts: 3.93 us -> 1.28 us  [body(): cache_parts[:, :kv_width, :].transpose(0, 2, 1).reshape(span, kv_width)]
    dot_general x2, matrix products: 9.48 us -> 7.11 us  [score(): jnp.einsum('hqd,kd->hqk', q_rope, rope, preferred_element_type=jnp.float32)]
    pallas_call x5 -> x4, Pallas kernels: 134 us -> 134 us  [exchange(): pl.pallas_call(functools.partial(_exchange_kernel, n, tuple(plan)), out_s...]
  transfers between devices with their start and end apart: 1 -> 1, of which waited for: 1 -> 0; matrix products, arithmetic and copies ran while one was open for 7% -> 7% of each run, Pallas kernels for 11% -> 24%
where the time goes in v8:
time: 212 us; the launch traced here: 210 us
  Pallas kernels  134 us (63%)
  other arithmetic  23.8 us (11%)
  local copies, waits for them, and re-layouts  19.6 us (9%)
  between operations  16.1 us (8%)
  matrix products  15.4 us (7%)
    pallas_call x4, Pallas kernels, exchange(): pl.pallas_call(functools.partial(_exchange_kernel, n, tuple(plan)), out_s...  134 us
    dot_general x2, matrix products, score(): jnp.einsum('hqd,kd->hqk', q_rope, rope, preferred_element_type=jnp.float32)  7.11 us
    reduce_max x1, other arithmetic, body(): row_peak = jnp.max(scores, 2)  5.68 us
    reduce_sum x1, other arithmetic, body(): row_total = jnp.sum(exponent, 2)  5.51 us
  transfers between devices with their start and end apart: 1, of which 0 were waited for; matrix products, arithmetic and copies ran while one was open for 7% of the time, Pallas kernels for 24%

profile of v8, /device:TPU:6, one launch (start us, length us, event | category | flops | bytes accessed | tf_op | source)
XLA Modules:
  0.0 209.9 jit_solution(5140621683822179754)
XLA Ops:
  6.5 0.7 all-gather.2.cloned.1.call-update
  7.3 1.2 dynamic_slice.20
  9.6 3.3 %copy.55 = bf16[256,4096]{0,1:T(8,128)(2,1)S(1)} copy(bf16[256,4096]{1,0:T(8,128)(2,1)} %param.17) | data formatting | bytes 4194304 | tf_op args[5]
  12.9 0.0 copy-done.9
  12.9 0.0 copy-done.7
  12.9 0.4 convolution_convert_fusion.1
  13.3 0.3 copy.53
  13.6 0.0 copy-start.14
  13.6 0.0 copy-start.15
  13.6 0.0 copy-start.13
  13.6 0.0 copy-start.12
  13.6 1.6 reshape.192.refs_0_
  15.2 49.9 %shard_map.118 = (bf16[32,66,128]{2,1,0:T(8,128)(2,1)}, bf16[8,96,768]{2,1,0:T(8,128)(2,1)}) custom-call(bf16[32,66,128]{2,1,0:T(8,128)(2,1)} %reshape.192.refs_0_, bf16[96,768]{1,0:T(8,128)(2,1)} %bitcast.68), custom_call_target="tpu_custom_call" | custom-call | tf_op jit(solution)/shard_map/pallas_call | solution.py:121
  65.0 1.2 convert_reduce_fusion
  66.2 0.1 reshape.193
  66.9 0.6 dynamic_slice.21
  68.0 0.7 dynamic-slice_bitcast_fusion
  68.7 0.1 select_reduce_fusion.1
  68.8 0.7 add_compare_fusion
  69.5 0.1 lt.52
  69.6 0.0 copy-done.15
  69.6 0.6 dynamic_slice.19
  70.2 0.1 multiply_reduce_fusion.2
  70.3 0.1 multiply_reduce_fusion.1
  70.4 0.1 fusion.29
  70.6 0.1 multiply_convert_fusion.1
  70.6 0.1 multiply_convert_fusion
  70.7 0.7 concatenate.20.refs_1_
  71.4 0.5 iota_compare_fusion.3
  71.9 0.6 add_convert_fusion.1
  72.5 0.6 fusion.30
  73.2 0.7 multiply_cosine_fusion
  73.9 0.9 pad_add_fusion
  74.8 2.9 %select_reduce_fusion = bf16[256,288]{0,1:T(8,128)(2,1)} fusion(bf16[16,256,288]{1,2,0:T(8,128)(2,1)} %all-gather.2.cloned.1.call-done, pred[16]{0:T(512)(128)(4,1)S(1)} %iota_compare_fusion.3), kind=kLoop, calls=%fused_computation.8 | loop fusion | flops 3465216 | bytes 2506768 | tf_op jit(solution)/shard_map/reduce_sum | solution.py:176
  77.7 23.4 %shard_map.119 = (bf16[4,288,256]{2,1,0:T(8,128)(2,1)}, bf16[32,8,1056]{2,1,0:T(8,128)(2,1)}) custom-call(bf16[288,256]{1,0:T(8,128)(2,1)} %bitcast.67, bf16[8,1056]{1,0:T(8,128)(2,1)} %concatenate.20.refs_1_), custom_call_target="tpu_custom_call" | custom-call | tf_op jit(solution)/shard_map/pallas_call | solution.py:121
  101.1 1.1 slice_bitcast_fusion
  102.1 0.8 slice_bitcast_fusion.5
  103.0 0.2 copy.54
  103.2 0.7 convolution_convert_fusion.2
  104.0 0.3 copy-done.6
  104.3 1.2 convolution_convert_fusion.3
  105.5 0.5 convolution_bitcast_fusion
  106.0 0.1 copy.57
  106.1 2.1 copy.68
  108.2 1.3 fusion.10
  109.5 0.5 fusion.12
  110.0 0.2 copy-done.8
  110.2 2.6 %add_multiply_fusion.1 = f32[8,256,256]{2,1,0:T(8,128)} fusion(f32[8,256,256]{2,1,0:T(8,128)S(1)} %fusion.12, bf16[8,256,16]{1,2,0:T(8,128)(2,1)S(1)} %get-tuple-element.18, bf16[8,256,16]{1,2,0:T(8,128)(2,1)S(1)} %get-tuple-element.17, bf16[256,1056]{1,0:T(8,128)(2,1)} %bitcast.64), kind=kOutput, calls=%fused_computation.12 | convolution fusion | flops 34865152 | bytes 4390912 | tf_op jit(solution)/shard_map/hqd,kd->hqk/dot_general | solution.py:225
  112.8 4.5 %add_multiply_fusion = f32[8,256,1024]{2,1,0:T(8,128)} fusion(f32[8,256,1024]{2,1,0:T(8,128)S(1)} %fusion.10, bf16[1024,32,1]{0,1,2:T(8,128)(2,1)S(1)} %reshape.203, bf16[8,256,16]{1,2,0:T(8,128)(2,1)S(1)} %get-tuple-element.18, bf16[8,256,16]{1,2,0:T(8,128)(2,1)S(1)} %get-tuple-element.17), kind=kOutput, calls=%fused_computation.4 | convolution fusion | flops 138674176 | bytes 16973824 | tf_op jit(solution)/shard_map/hqd,kd->hqk/dot_general | solution.py:225
  117.3 5.7 %fusion.2 = f32[8,256]{1,0:T(8,128)S(1)} fusion(f32[8,256,256]{2,1,0:T(8,128)} %add_multiply_fusion.1, f32[8,256,1024]{2,1,0:T(8,128)} %add_multiply_fusion, pred[256,1280]{1,0:T(8,128)(4,1)S(1)} %copy-done.3), kind=kLoop, calls=%fused_computation.5 | loop fusion | flops 7862272 | bytes 10821632 | tf_op jit(solution)/shard_map/reduce_max | solution.py:254
  123.1 0.0 slice-start.1
  123.1 1.5 slice.90
  124.5 1.3 slice.92
  125.8 5.5 %fusion = f32[8,256]{1,0:T(8,128)S(1)} fusion(f32[8,256,256]{2,1,0:T(8,128)S(1)} %copy-done.1, f32[8,256,1024]{2,1,0:T(8,128)} %add_multiply_fusion, f32[8,256]{1,0:T(8,128)S(1)} %compare_select_fusion, pred[256,1280]{1,0:T(8,128)(4,1)S(1)} %copy-done.3), kind=kLoop, calls=%fused_computation.2 | loop fusion | flops 10483712 | bytes 10829824 | tf_op jit(solution)/shard_map/reduce_sum | solution.py:257
  131.3 0.6 pad_maximum_fusion.3.refs_1_
  132.0 3.2 %fusion.3.refs_0_ = f32[8,64,256]{2,1,0:T(8,128)} fusion(f32[8,256,256]{2,1,0:T(8,128)S(1)} %copy-done.1, f32[8,256,1024]{2,1,0:T(8,128)S(1)} %bitcast.54, f32[8,256]{1,0:T(8,128)S(1)} %compare_select_fusion, pred[256,1280]{1,0:T(8,128)(4,1)S(1)} %copy-done.3, bf16[256,8,64]{0,2,1:T(8,128)(2,1)S(1)} %slice.92, bf16[1024,8,64]{0,2,1:T(8,128)(2,1)S(1)} %slice.90), kind=kOutput, calls=%fused_computation.6 | convolution fusion | flops 348651520 | bytes 12656640 | tf_op jit(solution)/shard_map/hqk,khd->hdq/dot_general | solution.py:259
  135.2 22.0 %shard_map.120 = (f32[8,64,256]{2,1,0:T(8,128)}, f32[8,2,256]{2,1,0:T(2,128)}) custom-call(f32[8,64,256]{2,1,0:T(8,128)} %fusion.3.refs_0_, f32[8,2,256]{2,1,0:T(2,128)} %pad_maximum_fusion.3.refs_1_), custom_call_target="tpu_custom_call" | custom-call | tf_op jit(solution)/shard_map/pallas_call | solution.py:121
  157.2 0.7 copy.62
  157.9 0.7 slice.85
  158.7 1.1 multiply_reduce_fusion
  159.8 0.5 fusion.6
  160.3 1.5 copy.63
  161.8 39.2 %shard_map.121 = bf16[32,80,256]{2,1,0:T(8,128)(2,1)} custom-call(bf16[32,80,256]{2,1,0:T(8,128)(2,1)} %bitcast.57), custom_call_target="tpu_custom_call" | custom-call | tf_op jit(solution)/shard_map/pallas_call | solution.py:121
  201.0 2.1 %reduce_sum.92 = bf16[80,256]{1,0:T(8,128)(2,1)} reduce(bf16[32,80,256]{2,1,0:T(8,128)(2,1)} %shard_map.121, bf16[]{:T(256)} %constant.91.clone.1), dimensions={0}, to_apply=%region_10.11 | reduce | flops 634880 | bytes 1351682 | tf_op jit(solution)/shard_map/reduce_sum | solution.py:275
  (46 shorter events, 0.3 us)
Async XLA Ops:
  6.5 153.2 %copy-start = (bf16[64,2560]{1,0:T(8,128)(2,1)S(1)}, bf16[64,2560]{1,0:T(8,128)(2,1)}, u32[]{:S(2)}) copy-start(bf16[64,2560]{1,0:T(8,128)(2,1)} %param.18) | copy-start | bytes 983044
  6.5 6.3 %copy-start.9 = (bf16[256,80]{0,1:T(8,128)(2,1)S(1)}, bf16[256,80]{0,1:T(8,128)(2,1)}, u32[]{:S(2)}) copy-start(bf16[256,80]{0,1:T(8,128)(2,1)} %param.12) | copy-start | bytes 122884
  6.5 6.4 %copy-start.7 = (bf16[80,1056]{1,0:T(8,128)(2,1)S(1)}, bf16[80,1056]{1,0:T(8,128)(2,1)}, u32[]{:S(2)}) copy-start(bf16[80,1056]{1,0:T(8,128)(2,1)} %param.13) | copy-start | bytes 506884
  6.5 68.3 %all-gather.2.cloned.1.call-start = ((), (), s32[]{:S(2)}) async-start(), calls=%async_computation | async-start | bytes 2506752 | tf_op jit(solution)/shard_map/all_gather | solution.py:174
  13.6 53.3 %copy-start.14 = (s32[16]{0:T(128)S(1)}, s32[16]{0:T(128)}, u32[]{:S(2)}) copy-start(s32[16]{0:T(128)} %param.20) | copy-start | bytes 196
  13.6 56.0 %copy-start.15 = (s32[16]{0:T(128)S(1)}, s32[16]{0:T(128)}, u32[]{:S(2)}) copy-start(s32[16]{0:T(128)} %param.21) | copy-start | bytes 196
  13.6 57.0 %copy-start.13 = (f32[256]{0:T(256)S(1)}, f32[256]{0:T(256)}, u32[]{:S(2)}) copy-start(f32[256]{0:T(256)} %param.15) | copy-start | bytes 3076
  13.6 57.0 %copy-start.12 = (f32[768]{0:T(1024)S(1)}, f32[768]{0:T(1024)}, u32[]{:S(2)}) copy-start(f32[768]{0:T(1024)} %param.14) | copy-start | bytes 9220
  73.1 29.0 %copy-start.10 = (pred[256]{0:T(512)(128)(4,1)}, pred[256]{0:T(512)(128)(4,1)S(1)}, u32[]{:S(2)}) copy-start(pred[256]{0:T(512)(128)(4,1)S(1)} %get-tuple-element.24) | copy-start | bytes 772
  103.2 1.1 copy-start.6
  103.2 2.3 %copy-start.5 = (bf16[8,96,768]{2,1,0:T(8,128)(2,1)S(1)}, bf16[8,96,768]{2,1,0:T(8,128)(2,1)}, u32[]{:S(2)}) copy-start(bf16[8,96,768]{2,1,0:T(8,128)(2,1)} %get-tuple-element.14) | copy-start | bytes 3538948
  104.0 5.5 %copy-start.2 = (bf16[1024,1024]{0,1:T(8,128)(2,1)}, bf16[1024,1024]{0,1:T(8,128)(2,1)S(1)}, u32[]{:S(2)}) copy-start(bf16[1024,1024]{0,1:T(8,128)(2,1)S(1)} %convolution_convert_fusion.2) | copy-start | bytes 6291460
  108.2 1.3 copy-start.4
  109.5 0.7 copy-start.8
  112.8 4.5 %copy-start.3 = (pred[256,1280]{1,0:T(8,128)(4,1)S(1)}, pred[256,1280]{1,0:T(8,128)(4,1)}, u32[]{:S(2)}) copy-start(pred[256,1280]{1,0:T(8,128)(4,1)} %pad_add_fusion) | copy-start | bytes 983044
  117.3 14.6 %slice-start = ((s8[8388608]{0:T(1024)(128)(4,1)}), s8[4194304]{0:T(1024)(128)(4,1)S(1)}, s32[]{:S(2)}) async-start(s8[8388608]{0:T(1024)(128)(4,1)} %bitcast.53), calls=%async_computation.1 | async-start | bytes 8388608
  123.0 2.8 %copy-start.1 = (f32[8,256,256]{2,1,0:T(8,128)S(1)}, f32[8,256,256]{2,1,0:T(8,128)}, u32[]{:S(2)}) copy-start(f32[8,256,256]{2,1,0:T(8,128)} %add_multiply_fusion.1) | copy-start | bytes 6291460
  123.1 8.9 %slice-start.1 = ((s8[8388608]{0:T(1024)(128)(4,1)}), s8[4194304]{0:T(1024)(128)(4,1)S(1)}, s32[]{:S(2)}) async-start(s8[8388608]{0:T(1024)(128)(4,1)} %bitcast.53), calls=%async_computation.2 | async-start | bytes 8388608
  132.0 27.8 %copy-start.11 = (pred[256]{0:T(512)(128)(4,1)S(1)}, pred[256]{0:T(512)(128)(4,1)}, u32[]{:S(2)}) copy-start(pred[256]{0:T(512)(128)(4,1)} %copy-done.10) | copy-start | bytes 772
Sparse Core Ops, SparseCore 0:
  9.5 47.9 all-gather.1

commit v9 on v8

--- a/solution.py
+++ b/solution.py
@@ -260,11 +260,13 @@
         "hqk,khd->hdq", exponent.astype(jnp.bfloat16), values, preferred_element_type=jnp.float32
     )
     stats = jnp.stack([row_peak, row_total], 1)
-    summed_parts, stat_parts = exchange([summed, stats], [("y", False), ("y", False)], 4)
+    summed_parts, stat_parts = exchange(
+        [summed.astype(jnp.bfloat16), stats], [("y", False), ("y", False)], 4
+    )
     peak = jnp.max(stat_parts[:, 0, :], 0)
     factor = jnp.exp(stat_parts[:, 0, :] - peak[None, :])
     total = jnp.sum(factor * stat_parts[:, 1, :], 0)
-    merged = jnp.sum(factor[:, None, :] * summed_parts, 0)
+    merged = jnp.sum(factor[:, None, :] * summed_parts.astype(jnp.float32), 0)
     attended = (merged / total[None, :]).astype(jnp.bfloat16)
     live_rows = jnp.arange(group_rows, dtype=jnp.int32) < live_count
     attended = jnp.where(live_rows[None, :], attended, jnp.zeros_like(attended))

time: 212 us -> 206 us (0.972)
  Pallas kernels: 134 us -> 127 us
    pallas_call x4, Pallas kernels: 134 us -> 127 us  [exchange(): pl.pallas_call(functools.partial(_exchange_kernel, n, tuple(plan)), out_s...]
  transfers between devices with their start and end apart: 1 -> 1, of which waited for: 0 -> 0; matrix products, arithmetic and copies ran while one was open for 7% -> 8% of each run, Pallas kernels for 24% -> 25%
where the time goes in v9:
time: 206 us; the launch traced here: 202 us
  Pallas kernels  127 us (62%)
  other arithmetic  23.7 us (12%)
  local copies, waits for them, and re-layouts  19.6 us (10%)
  between operations  16.1 us (8%)
  matrix products  15.3 us (7%)
    pallas_call x4, Pallas kernels, exchange(): pl.pallas_call(functools.partial(_exchange_kernel, n, tuple(plan)), out_s...  127 us
    dot_general x2, matrix products, score(): jnp.einsum('hqd,kd->hqk', q_rope, rope, preferred_element_type=jnp.float32)  7.11 us
    reduce_max x1, other arithmetic, body(): row_peak = jnp.max(scores, 2)  5.68 us
    reduce_sum x1, other arithmetic, body(): row_total = jnp.sum(exponent, 2)  5.51 us
  transfers between devices with their start and end apart: 1, of which 0 were waited for; matrix products, arithmetic and copies ran while one was open for 8% of the time, Pallas kernels for 25%

profile of v9, /device:TPU:6, one launch (start us, length us, event | category | flops | bytes accessed | tf_op | source)
XLA Modules:
  0.0 202.3 jit_solution(17785338352216068808)
XLA Ops:
  6.5 0.7 all-gather.2.cloned.1.call-update
  7.3 1.2 dynamic_slice.20
  9.6 3.3 %copy.55 = bf16[256,4096]{0,1:T(8,128)(2,1)S(1)} copy(bf16[256,4096]{1,0:T(8,128)(2,1)} %param.17) | data formatting | bytes 4194304 | tf_op args[5]
  12.9 0.0 copy-done.9
  12.9 0.0 copy-done.7
  12.9 0.4 convolution_convert_fusion.1
  13.3 0.3 copy.53
  13.6 0.0 copy-start.14
  13.6 0.0 copy-start.15
  13.6 0.0 copy-start.13
  13.6 0.0 copy-start.12
  13.6 1.6 reshape.192.refs_0_
  15.2 49.9 %shard_map.118 = (bf16[32,66,128]{2,1,0:T(8,128)(2,1)}, bf16[8,96,768]{2,1,0:T(8,128)(2,1)}) custom-call(bf16[32,66,128]{2,1,0:T(8,128)(2,1)} %reshape.192.refs_0_, bf16[96,768]{1,0:T(8,128)(2,1)} %bitcast.68), custom_call_target="tpu_custom_call" | custom-call | tf_op jit(solution)/shard_map/pallas_call | solution.py:121
  65.0 1.2 convert_reduce_fusion
  66.2 0.1 reshape.193
  66.9 0.6 dynamic_slice.21
  68.0 0.7 dynamic-slice_bitcast_fusion
  68.7 0.1 select_reduce_fusion.1
  68.8 0.7 add_compare_fusion
  69.5 0.1 lt.52
  69.6 0.0 copy-done.15
  69.6 0.6 dynamic_slice.19
  70.2 0.1 multiply_reduce_fusion.2
  70.3 0.1 multiply_reduce_fusion.1
  70.4 0.1 fusion.34
  70.6 0.1 multiply_convert_fusion.1
  70.6 0.1 multiply_convert_fusion
  70.7 0.7 concatenate.20.refs_1_
  71.4 0.5 iota_compare_fusion.3
  71.9 0.6 add_convert_fusion.1
  72.5 0.6 fusion.35
  73.2 0.7 multiply_cosine_fusion
  73.9 0.9 pad_add_fusion
  74.8 2.9 %select_reduce_fusion = bf16[256,288]{0,1:T(8,128)(2,1)} fusion(bf16[16,256,288]{1,2,0:T(8,128)(2,1)} %all-gather.2.cloned.1.call-done, pred[16]{0:T(512)(128)(4,1)S(1)} %iota_compare_fusion.3), kind=kLoop, calls=%fused_computation.8 | loop fusion | flops 3465216 | bytes 2506768 | tf_op jit(solution)/shard_map/reduce_sum | solution.py:176
  77.7 23.4 %shard_map.119 = (bf16[4,288,256]{2,1,0:T(8,128)(2,1)}, bf16[32,8,1056]{2,1,0:T(8,128)(2,1)}) custom-call(bf16[288,256]{1,0:T(8,128)(2,1)} %bitcast.67, bf16[8,1056]{1,0:T(8,128)(2,1)} %concatenate.20.refs_1_), custom_call_target="tpu_custom_call" | custom-call | tf_op jit(solution)/shard_map/pallas_call | solution.py:121
  101.1 1.1 slice_bitcast_fusion
  102.1 0.8 slice_bitcast_fusion.5
  103.0 0.2 copy.54
  103.2 0.7 convolution_convert_fusion.2
  104.0 0.3 copy-done.6
  104.3 1.2 convolution_convert_fusion.3
  105.5 0.5 convolution_bitcast_fusion
  106.0 0.1 copy.57
  106.1 2.1 %copy.68 = bf16[256,1024]{0,1:T(8,128)(2,1)} copy(bf16[256,1024]{1,0:T(8,128)(2,1)} %convolution_convert_fusion.3) | data formatting | bytes 1048576 | tf_op jit(solution)/shard_map/reshape | solution.py:215
  108.2 1.3 fusion.15
  109.5 0.5 fusion.17
  110.0 0.2 copy-done.8
  110.2 2.6 %add_multiply_fusion.1 = f32[8,256,256]{2,1,0:T(8,128)} fusion(f32[8,256,256]{2,1,0:T(8,128)S(1)} %fusion.17, bf16[8,256,16]{1,2,0:T(8,128)(2,1)S(1)} %get-tuple-element.18, bf16[8,256,16]{1,2,0:T(8,128)(2,1)S(1)} %get-tuple-element.17, bf16[256,1056]{1,0:T(8,128)(2,1)} %bitcast.64), kind=kOutput, calls=%fused_computation.12 | convolution fusion | flops 34865152 | bytes 4390912 | tf_op jit(solution)/shard_map/hqd,kd->hqk/dot_general | solution.py:225
  112.8 4.5 %add_multiply_fusion = f32[8,256,1024]{2,1,0:T(8,128)} fusion(f32[8,256,1024]{2,1,0:T(8,128)S(1)} %fusion.15, bf16[1024,32,1]{0,1,2:T(8,128)(2,1)S(1)} %reshape.203, bf16[8,256,16]{1,2,0:T(8,128)(2,1)S(1)} %get-tuple-element.18, bf16[8,256,16]{1,2,0:T(8,128)(2,1)S(1)} %get-tuple-element.17), kind=kOutput, calls=%fused_computation.4 | convolution fusion | flops 138674176 | bytes 16973824 | tf_op jit(solution)/shard_map/hqd,kd->hqk/dot_general | solution.py:225
  117.3 5.7 %fusion.2 = f32[8,256]{1,0:T(8,128)S(1)} fusion(f32[8,256,256]{2,1,0:T(8,128)} %add_multiply_fusion.1, f32[8,256,1024]{2,1,0:T(8,128)} %add_multiply_fusion, pred[256,1280]{1,0:T(8,128)(4,1)S(1)} %copy-done.3), kind=kLoop, calls=%fused_computation.5 | loop fusion | flops 7862272 | bytes 10821632 | tf_op jit(solution)/shard_map/reduce_max | solution.py:254
  123.1 0.0 slice-start.1
  123.1 1.5 slice.90
  124.5 1.3 slice.92
  125.8 5.5 %fusion = f32[8,256]{1,0:T(8,128)S(1)} fusion(f32[8,256,256]{2,1,0:T(8,128)S(1)} %copy-done.1, f32[8,256,1024]{2,1,0:T(8,128)} %add_multiply_fusion, f32[8,256]{1,0:T(8,128)S(1)} %compare_select_fusion, pred[256,1280]{1,0:T(8,128)(4,1)S(1)} %copy-done.3), kind=kLoop, calls=%fused_computation.2 | loop fusion | flops 10483712 | bytes 10829824 | tf_op jit(solution)/shard_map/reduce_sum | solution.py:257
  131.3 0.6 pad_maximum_fusion.3.refs_1_
  132.0 3.1 %fusion.10.refs_0_ = bf16[8,64,256]{2,1,0:T(8,128)(2,1)} fusion(f32[8,256,256]{2,1,0:T(8,128)S(1)} %copy-done.1, f32[8,256,1024]{2,1,0:T(8,128)S(1)} %bitcast.54, f32[8,256]{1,0:T(8,128)S(1)} %compare_select_fusion, pred[256,1280]{1,0:T(8,128)(4,1)S(1)} %copy-done.3, bf16[256,8,64]{0,2,1:T(8,128)(2,1)S(1)} %slice.92, bf16[1024,8,64]{0,2,1:T(8,128)(2,1)S(1)} %slice.90), kind=kOutput, calls=%fused_computation.20 | convolution fusion | flops 348782592 | bytes 12394496 | tf_op jit(solution)/shard_map/hqk,khd->hdq/dot_general | solution.py:259
  135.1 16.2 %shard_map.120 = (bf16[8,64,256]{2,1,0:T(8,128)(2,1)}, f32[8,2,256]{2,1,0:T(2,128)}) custom-call(bf16[8,64,256]{2,1,0:T(8,128)(2,1)} %fusion.10.refs_0_, f32[8,2,256]{2,1,0:T(2,128)} %pad_maximum_fusion.3.refs_1_), custom_call_target="tpu_custom_call" | custom-call | tf_op jit(solution)/shard_map/pallas_call | solution.py:121
  151.3 0.7 copy.62
  152.0 0.7 slice.85
  152.8 1.0 multiply_reduce_fusion
  153.8 0.5 fusion.6
  154.3 1.5 copy.63
  155.8 37.6 %shard_map.121 = bf16[32,80,256]{2,1,0:T(8,128)(2,1)} custom-call(bf16[32,80,256]{2,1,0:T(8,128)(2,1)} %bitcast.57), custom_call_target="tpu_custom_call" | custom-call | tf_op jit(solution)/shard_map/pallas_call | solution.py:121
  193.3 2.1 %reduce_sum.92 = bf16[80,256]{1,0:T(8,128)(2,1)} reduce(bf16[32,80,256]{2,1,0:T(8,128)(2,1)} %shard_map.121, bf16[]{:T(256)} %constant.91.clone.1), dimensions={0}, to_apply=%region_10.11 | reduce | flops 634880 | bytes 1351682 | tf_op jit(solution)/shard_map/reduce_sum | solution.py:277
  (46 shorter events, 0.3 us)
Async XLA Ops:
  6.5 147.2 %copy-start = (bf16[64,2560]{1,0:T(8,128)(2,1)S(1)}, bf16[64,2560]{1,0:T(8,128)(2,1)}, u32[]{:S(2)}) copy-start(bf16[64,2560]{1,0:T(8,128)(2,1)} %param.18) | copy-start | bytes 983044
  6.5 6.3 %copy-start.9 = (bf16[256,80]{0,1:T(8,128)(2,1)S(1)}, bf16[256,80]{0,1:T(8,128)(2,1)}, u32[]{:S(2)}) copy-start(bf16[256,80]{0,1:T(8,128)(2,1)} %param.12) | copy-start | bytes 122884
  6.5 6.4 %copy-start.7 = (bf16[80,1056]{1,0:T(8,128)(2,1)S(1)}, bf16[80,1056]{1,0:T(8,128)(2,1)}, u32[]{:S(2)}) copy-start(bf16[80,1056]{1,0:T(8,128)(2,1)} %param.13) | copy-start | bytes 506884
  6.5 68.3 %all-gather.2.cloned.1.call-start = ((), (), s32[]{:S(2)}) async-start(), calls=%async_computation | async-start | bytes 2506752 | tf_op jit(solution)/shard_map/all_gather | solution.py:174
  13.6 53.3 %copy-start.14 = (s32[16]{0:T(128)S(1)}, s32[16]{0:T(128)}, u32[]{:S(2)}) copy-start(s32[16]{0:T(128)} %param.20) | copy-start | bytes 196
  13.6 56.0 %copy-start.15 = (s32[16]{0:T(128)S(1)}, s32[16]{0:T(128)}, u32[]{:S(2)}) copy-start(s32[16]{0:T(128)} %param.21) | copy-start | bytes 196
  13.6 57.0 %copy-start.13 = (f32[256]{0:T(256)S(1)}, f32[256]{0:T(256)}, u32[]{:S(2)}) copy-start(f32[256]{0:T(256)} %param.15) | copy-start | bytes 3076
  13.6 57.0 %copy-start.12 = (f32[768]{0:T(1024)S(1)}, f32[768]{0:T(1024)}, u32[]{:S(2)}) copy-start(f32[768]{0:T(1024)} %param.14) | copy-start | bytes 9220
  73.1 29.0 %copy-start.10 = (pred[256]{0:T(512)(128)(4,1)}, pred[256]{0:T(512)(128)(4,1)S(1)}, u32[]{:S(2)}) copy-start(pred[256]{0:T(512)(128)(4,1)S(1)} %get-tuple-element.24) | copy-start | bytes 772
  103.2 1.1 copy-start.6
  103.2 2.3 %copy-start.5 = (bf16[8,96,768]{2,1,0:T(8,128)(2,1)S(1)}, bf16[8,96,768]{2,1,0:T(8,128)(2,1)}, u32[]{:S(2)}) copy-start(bf16[8,96,768]{2,1,0:T(8,128)(2,1)} %get-tuple-element.14) | copy-start | bytes 3538948
  104.0 5.5 %copy-start.2 = (bf16[1024,1024]{0,1:T(8,128)(2,1)}, bf16[1024,1024]{0,1:T(8,128)(2,1)S(1)}, u32[]{:S(2)}) copy-start(bf16[1024,1024]{0,1:T(8,128)(2,1)S(1)} %convolution_convert_fusion.2) | copy-start | bytes 6291460
  108.2 1.3 copy-start.4
  109.5 0.7 copy-start.8
  112.8 4.5 %copy-start.3 = (pred[256,1280]{1,0:T(8,128)(4,1)S(1)}, pred[256,1280]{1,0:T(8,128)(4,1)}, u32[]{:S(2)}) copy-start(pred[256,1280]{1,0:T(8,128)(4,1)} %pad_add_fusion) | copy-start | bytes 983044
  117.3 14.6 %slice-start = ((s8[8388608]{0:T(1024)(128)(4,1)}), s8[4194304]{0:T(1024)(128)(4,1)S(1)}, s32[]{:S(2)}) async-start(s8[8388608]{0:T(1024)(128)(4,1)} %bitcast.53), calls=%async_computation.1 | async-start | bytes 8388608
  123.0 2.8 %copy-start.1 = (f32[8,256,256]{2,1,0:T(8,128)S(1)}, f32[8,256,256]{2,1,0:T(8,128)}, u32[]{:S(2)}) copy-start(f32[8,256,256]{2,1,0:T(8,128)} %add_multiply_fusion.1) | copy-start | bytes 6291460
  123.1 8.9 %slice-start.1 = ((s8[8388608]{0:T(1024)(128)(4,1)}), s8[4194304]{0:T(1024)(128)(4,1)S(1)}, s32[]{:S(2)}) async-start(s8[8388608]{0:T(1024)(128)(4,1)} %bitcast.53), calls=%async_computation.2 | async-start | bytes 8388608
  132.0 21.8 %copy-start.11 = (pred[256]{0:T(512)(128)(4,1)S(1)}, pred[256]{0:T(512)(128)(4,1)}, u32[]{:S(2)}) copy-start(pred[256]{0:T(512)(128)(4,1)} %copy-done.10) | copy-start | bytes 772
Sparse Core Ops, SparseCore 0:
  9.5 47.9 all-gather.1

commit v10 on v9

--- a/solution.py
+++ b/solution.py
@@ -204,27 +204,22 @@
     span = PLANE_X * chunk
     span_latents = cache_parts[:, :kv_width, :].transpose(0, 2, 1).reshape(span, kv_width)
     span_rope = cache_parts[:, kv_width:, :].transpose(0, 2, 1).reshape(span, ROPE)
-    span_lifted = (
-        jnp.dot(span_latents, line_weight, preferred_element_type=jnp.float32)
+    key_latents = jnp.concatenate([span_latents, fresh_latents[:, :kv_width]], 0)
+    key_rope = jnp.concatenate([span_rope, fresh_latents[:, kv_width:]], 0)
+    key_count = key_latents.shape[0]
+    lifted = (
+        jnp.dot(key_latents, line_weight, preferred_element_type=jnp.float32)
         .astype(jnp.bfloat16)
-        .reshape(span, lines, head_width)
-    )
-    fresh_lifted = (
-        jnp.dot(fresh_latents[:, :kv_width], line_weight, preferred_element_type=jnp.float32)
-        .astype(jnp.bfloat16)
-        .reshape(group_rows, lines, head_width)
-    )
-    fresh_rope = fresh_latents[:, kv_width:]
-    q_nope = head_queries[:, :, :NOPE]
-    q_rope = head_queries[:, :, NOPE:]
+        .reshape(key_count, lines, head_width)
+    )
+    keys = jnp.concatenate(
+        [
+            lifted[:, :, :NOPE],
+            jnp.broadcast_to(key_rope[:, None, :], (key_count, lines, ROPE)),
+        ],
+        2,
+    )
     score_scale = 1.0 / math.sqrt(NOPE + ROPE)
-
-    def score(lifted, rope):
-        return (
-            jnp.einsum("hqd,khd->hqk", q_nope, lifted[:, :, :NOPE], preferred_element_type=jnp.float32)
-            + jnp.einsum("hqd,kd->hqk", q_rope, rope, preferred_element_type=jnp.float32)
-        ) * score_scale
-
     key_total = columns * chunk
     page_row = page_table[slot_index]
     page_count = page_row.shape[0]
@@ -247,15 +242,16 @@
     visible = jnp.concatenate(
         [jnp.broadcast_to(span_visible[None, :], (group_rows, span)), fresh_visible], 1
     )
-    scores = jnp.concatenate(
-        [score(span_lifted, span_rope), score(fresh_lifted, fresh_rope)], 2
+    scores = (
+        jnp.einsum("hqd,khd->hqk", head_queries, keys, preferred_element_type=jnp.float32)
+        * score_scale
     )
     scores = jnp.where(visible[None], scores, -jnp.inf)
     row_peak = jnp.max(scores, 2)
     safe_peak = jnp.where(row_peak == -jnp.inf, 0.0, row_peak)
     exponent = jnp.exp(scores - safe_peak[:, :, None])
     row_total = jnp.sum(exponent, 2)
-    values = jnp.concatenate([span_lifted[:, :, NOPE:], fresh_lifted[:, :, NOPE:]], 0)
+    values = lifted[:, :, NOPE:]
     summed = jnp.einsum(
         "hqk,khd->hdq", exponent.astype(jnp.bfloat16), values, preferred_element_type=jnp.float32
     )

time: 206 us -> 189 us (0.917)
  other arithmetic: 23.7 us -> 14.2 us
  matrix products: 15.3 us -> 9.81 us
    dot_general x6 -> x2, matrix products: 10.8 us -> 2.89 us  [the longest x1 2.01 us: body(): jnp.einsum('hqd,khd->hqk', head_queries, keys, preferred_element_type=jnp...]
    reduce_max x1 -> x0, other arithmetic: 5.68 us -> none  [body(): row_peak = jnp.max(scores, 2)]
    reduce_sum x1, other arithmetic: 5.51 us -> 2.75 us  [body(): row_total = jnp.sum(exponent, 2)]
    reshape x1 -> x0, local copies, waits for them, and re-layouts: 2.07 us -> none  [body(): fresh_lifted = jnp.dot(fresh_latents[:, :kv_width], line_weight, preferre...]
    unnamed x37 -> x8, local copies, waits for them, and re-layouts: 3.85 us -> 4.33 us
  transfers between devices with their start and end apart: 1 -> 1, of which waited for: 0 -> 0; matrix products, arithmetic and copies ran while one was open for 8% -> 9% of each run, Pallas kernels for 25% -> 27%
where the time goes in v10:
time: 189 us; the launch traced here: 187 us
  Pallas kernels  128 us (68%)
  local copies, waits for them, and re-layouts  17.9 us (9%)
  between operations  16.3 us (9%)
  other arithmetic  14.2 us (8%)
  matrix products  9.81 us (5%)
    pallas_call x4, Pallas kernels, exchange(): pl.pallas_call(functools.partial(_exchange_kernel, n, tuple(plan)), out_s...  128 us
    unnamed x8, local copies, waits for them, and re-layouts  4.33 us
  transfers between devices with their start and end apart: 1, of which 0 were waited for; matrix products, arithmetic and copies ran while one was open for 9% of the time, Pallas kernels for 27%

profile of v10, /device:TPU:6, one launch (start us, length us, event | category | flops | bytes accessed | tf_op | source)
XLA Modules:
  0.0 186.5 jit_solution(2834766458383018137)
XLA Ops:
  6.5 0.0 copy-start
  6.5 0.0 all-gather.2.cloned.1.call-start
  6.5 0.7 all-gather.2.cloned.1.call-update
  7.3 1.3 dynamic_slice.20
  9.9 1.2 dynamic_slice.19
  11.7 1.3 dynamic_slice.21
  13.7 0.7 dynamic-slice_bitcast_fusion
  14.4 0.1 select_reduce_fusion.1
  14.5 0.8 add_compare_fusion
  15.3 0.1 lt.52
  15.4 1.3 convolution_convert_fusion.2
  16.7 0.3 copy.37
  17.0 1.6 reshape.190.refs_0_
  18.6 49.8 %shard_map.118 = (bf16[32,66,128]{2,1,0:T(8,128)(2,1)}, bf16[8,96,768]{2,1,0:T(8,128)(2,1)}) custom-call(bf16[32,66,128]{2,1,0:T(8,128)(2,1)} %reshape.190.refs_0_, bf16[96,768]{1,0:T(8,128)(2,1)} %bitcast.57), custom_call_target="tpu_custom_call" | custom-call | tf_op jit(solution)/shard_map/pallas_call | solution.py:121
  68.4 0.0 copy-start.2
  68.4 0.0 copy-start.1
  68.4 1.2 convert_reduce_fusion
  69.6 0.1 reshape.191
  69.7 3.5 %copy.39 = bf16[256,4096]{0,1:T(8,128)(2,1)S(1)} copy(bf16[256,4096]{1,0:T(8,128)(2,1)} %param.17) | data formatting | bytes 4194304 | tf_op args[5]
  73.2 0.1 multiply_reduce_fusion.2
  73.3 0.1 multiply_reduce_fusion.1
  73.5 0.1 fusion.39
  73.6 0.0 copy-done.2
  73.6 0.1 multiply_convert_fusion.1
  73.7 0.0 copy-done.1
  73.7 0.1 multiply_convert_fusion
  73.8 0.7 concatenate.22.refs_1_
  74.5 0.6 iota_compare_fusion.3
  75.1 0.7 add_convert_fusion.1
  75.8 0.6 fusion.40
  76.4 0.1 multiply_cosine_fusion
  76.6 0.1 pad_add_fusion
  76.7 0.0 all-gather.2.cloned.1.call-done
  76.7 2.9 %select_reduce_fusion = bf16[256,288]{0,1:T(8,128)(2,1)} fusion(bf16[16,256,288]{1,2,0:T(8,128)(2,1)} %all-gather.2.cloned.1.call-done, pred[16]{0:T(512)(128)(4,1)S(1)} %iota_compare_fusion.3), kind=kLoop, calls=%fused_computation.7 | loop fusion | flops 3465216 | bytes 2506768 | tf_op jit(solution)/shard_map/reduce_sum | solution.py:176
  79.6 23.4 %shard_map.119 = (bf16[4,288,256]{2,1,0:T(8,128)(2,1)}, bf16[32,8,1056]{2,1,0:T(8,128)(2,1)}) custom-call(bf16[288,256]{1,0:T(8,128)(2,1)} %bitcast.55, bf16[8,1056]{1,0:T(8,128)(2,1)} %concatenate.22.refs_1_), custom_call_target="tpu_custom_call" | custom-call | tf_op jit(solution)/shard_map/pallas_call | solution.py:121
  103.0 0.8 slice.86
  103.8 0.9 slice.79
  104.7 0.8 slice_bitcast_fusion.3
  105.6 1.1 slice_bitcast_fusion
  106.7 1.9 convolution_bitcast_fusion
  108.5 0.1 copy.41
  108.6 0.2 copy.38
  108.9 0.9 convolution_convert_fusion.1
  109.8 0.1 slice.85
  110.0 2.0 %fusion = (f32[8,256]{1,0:T(8,128)S(1)}, f32[8,256,1280]{2,1,0:T(8,128)S(1)}) fusion(pred[256,1280]{1,0:T(8,128)(4,1)S(1)} %pad_add_fusion, bf16[1280,8,32]{0,2,1:T(8,128)(2,1)S(1)} %broadcast_in_dim.43, bf16[1280,8,64]{0,2,1:T(8,128)(2,1)S(1)} %slice.85, bf16[8,256,16]{1,2,0:T(8,128)(2,1)S(1)} %get-tuple-element.18, ...), kind=kOutput, calls=%fused_computation.2 | convolution fusion | flops 516290560 | bytes 13180928 | tf_op jit(solution)/shard_map/hqd,khd->hqk/dot_general | solution.py:246
  112.0 3.2 %fusion.12.refs_0_ = bf16[8,64,256]{2,1,0:T(8,128)(2,1)} fusion(f32[8,256,1280]{2,1,0:T(8,128)S(1)} %get-tuple-element.24, f32[8,256]{1,0:T(8,128)S(1)} %compare_select_fusion, pred[256,1280]{1,0:T(8,128)(4,1)S(1)} %pad_add_fusion, bf16[1280,8,128]{0,2,1:T(8,128)(2,1)S(1)} %bitcast.47), kind=kOutput, calls=%fused_computation.19 | convolution fusion | flops 346161152 | bytes 12394496 | tf_op jit(solution)/shard_map/hqk,khd->hdq/dot_general | solution.py:255
  115.2 2.8 %fusion.1 = f32[8,256]{1,0:T(8,128)S(1)} fusion(f32[8,256,1280]{2,1,0:T(8,128)S(1)} %get-tuple-element.24, f32[8,256]{1,0:T(8,128)S(1)} %compare_select_fusion, pred[256,1280]{1,0:T(8,128)(4,1)S(1)} %pad_add_fusion), kind=kLoop, calls=%fused_computation.3 | loop fusion | flops 10483712 | bytes 10829824 | tf_op jit(solution)/shard_map/reduce_sum | solution.py:253
  118.0 0.6 pad_maximum_fusion.1.refs_1_
  118.6 16.2 %shard_map.120 = (bf16[8,64,256]{2,1,0:T(8,128)(2,1)}, f32[8,2,256]{2,1,0:T(2,128)}) custom-call(bf16[8,64,256]{2,1,0:T(8,128)(2,1)} %fusion.12.refs_0_, f32[8,2,256]{2,1,0:T(2,128)} %pad_maximum_fusion.1.refs_1_), custom_call_target="tpu_custom_call" | custom-call | tf_op jit(solution)/shard_map/pallas_call | solution.py:121
  134.8 0.7 slice.74
  135.5 0.7 copy.42
  136.3 1.0 multiply_reduce_fusion
  137.3 0.0 copy-done
  137.3 0.5 fusion.6
  137.9 1.5 copy.43
  139.3 38.2 %shard_map.121 = bf16[32,80,256]{2,1,0:T(8,128)(2,1)} custom-call(bf16[32,80,256]{2,1,0:T(8,128)(2,1)} %bitcast.48), custom_call_target="tpu_custom_call" | custom-call | tf_op jit(solution)/shard_map/pallas_call | solution.py:121
  177.5 2.1 %reduce_sum.92 = bf16[80,256]{1,0:T(8,128)(2,1)} reduce(bf16[32,80,256]{2,1,0:T(8,128)(2,1)} %shard_map.121, bf16[]{:T(256)} %constant.90.clone.1), dimensions={0}, to_apply=%region_10.11 | reduce | flops 634880 | bytes 1351682 | tf_op jit(solution)/shard_map/reduce_sum | solution.py:273
  (20 shorter events, 0.3 us)
Async XLA Ops:
  6.5 130.8 %copy-start = (bf16[64,2560]{1,0:T(8,128)(2,1)S(1)}, bf16[64,2560]{1,0:T(8,128)(2,1)}, u32[]{:S(2)}) copy-start(bf16[64,2560]{1,0:T(8,128)(2,1)} %param.18) | copy-start | bytes 983044
  6.5 70.2 %all-gather.2.cloned.1.call-start = ((), (), s32[]{:S(2)}) async-start(), calls=%async_computation | async-start | bytes 2506752 | tf_op jit(solution)/shard_map/all_gather | solution.py:174
  68.4 5.2 %copy-start.2 = (f32[256]{0:T(256)S(1)}, f32[256]{0:T(256)}, u32[]{:S(2)}) copy-start(f32[256]{0:T(256)} %param.15) | copy-start | bytes 3076
  68.4 5.3 %copy-start.1 = (f32[768]{0:T(1024)S(1)}, f32[768]{0:T(1024)}, u32[]{:S(2)}) copy-start(f32[768]{0:T(1024)} %param.14) | copy-start | bytes 9220
Sparse Core Ops, SparseCore 0:
  9.5 47.9 all-gather.1

commit v11 on v10

--- a/solution.py
+++ b/solution.py
@@ -155,9 +155,10 @@
     own_rows = group_rows // columns
     q_width = q_gain.shape[0]
     kv_width = kv_gain.shape[0]
-    slot_index = home_slot[row_id]
-    cached_count = cache_len[slot_index]
-    live_count = new_len[row_id]
+    request_ids = jnp.arange(home_slot.shape[0], dtype=jnp.int32)
+    slot_index = jnp.sum(jnp.where(request_ids == row_id, home_slot, 0))
+    cached_count = jnp.sum(jnp.where(request_ids == slot_index, cache_len, 0))
+    live_count = jnp.sum(jnp.where(request_ids == row_id, new_len, 0))
     partial_sums = jnp.dot(tokens, w_down, preferred_element_type=jnp.float32)
     pieces, line_query_weight = exchange(
         [partial_sums.astype(jnp.bfloat16).reshape(columns, -1, 128), w_q_up.T],
@@ -198,8 +199,11 @@
     ).astype(jnp.bfloat16)
     head_width = NOPE + VDIM
     heads = columns
-    line_weight = lax.dynamic_index_in_dim(
-        w_kv_up.reshape(kv_width, lines, PLANE_X, head_width), lane_id, axis=2, keepdims=False
+    line_weight = lax.dynamic_slice_in_dim(
+        w_kv_up.reshape(kv_width, lines, PLANE_X * head_width),
+        lane_id * head_width,
+        head_width,
+        2,
     ).reshape(kv_width, lines * head_width)
     span = PLANE_X * chunk
     span_latents = cache_parts[:, :kv_width, :].transpose(0, 2, 1).reshape(span, kv_width)

time: 189 us -> 187 us (0.989)
  local copies, waits for them, and re-layouts: 17.9 us -> 13.1 us
  other arithmetic: 14.2 us -> 17.4 us
    dynamic_slice x4 -> x1, local copies, waits for them, and re-layouts: 3.87 us -> 0.08 us  [body(): lax.dynamic_slice_in_dim(w_kv_up.reshape(kv_width, lines, PLANE_X * head_...]
    reduce_sum x0 -> x2, other arithmetic: none -> 3.18 us  [the longest x1 1.92 us: body(): live_count = jnp.sum(jnp.where(request_ids == row_id, new_len, 0))]
  transfers between devices with their start and end apart: 1 -> 1, of which waited for: 0 -> 0; matrix products, arithmetic and copies ran while one was open for 9% -> 8% of each run, Pallas kernels for 27% -> 27%
where the time goes in v11:
time: 187 us; the launch traced here: 184 us
  Pallas kernels  127 us (68%)
  other arithmetic  17.4 us (9%)
  between operations  16.1 us (9%)
  local copies, waits for them, and re-layouts  13.1 us (7%)
  matrix products  9.83 us (5%)
    pallas_call x4, Pallas kernels, exchange(): pl.pallas_call(functools.partial(_exchange_kernel, n, tuple(plan)), out_s...  127 us
  transfers between devices with their start and end apart: 1, of which 0 were waited for; matrix products, arithmetic and copies ran while one was open for 8% of the time, Pallas kernels for 27%

profile of v11, /device:TPU:6, one launch (start us, length us, event | category | flops | bytes accessed | tf_op | source)
XLA Modules:
  0.0 184.4 jit_solution(415531814044730286)
XLA Ops:
  6.5 0.0 copy-start
  6.5 0.0 all-gather.2.cloned.1.call-start
  6.5 0.7 all-gather.2.cloned.1.call-update
  7.3 1.3 fusion.44
  10.2 1.9 %fusion.43 = (s32[]{:T(128)}, s32[]{:T(128)}) fusion(s32[16]{0:T(128)} %param.21, s32[]{:T(128)S(6)} %axis_index.23, s32[16]{0:T(128)} %param.20, s32[]{:T(128)} %fusion.44), kind=kLoop, calls=%fused_computation.83 | loop fusion | flops 94 | bytes 144 | tf_op jit(solution)/shard_map/reduce_sum | solution.py:161
  12.8 0.7 dynamic-slice_bitcast_fusion
  13.5 0.1 select_reduce_fusion.1
  13.6 0.8 add_compare_fusion
  14.4 0.1 lt.45
  14.5 1.3 convolution_convert_fusion.2
  15.8 0.3 copy.29
  16.1 1.6 reshape.189.refs_0_
  17.6 49.9 %shard_map.118 = (bf16[32,66,128]{2,1,0:T(8,128)(2,1)}, bf16[8,96,768]{2,1,0:T(8,128)(2,1)}) custom-call(bf16[32,66,128]{2,1,0:T(8,128)(2,1)} %reshape.189.refs_0_, bf16[96,768]{1,0:T(8,128)(2,1)} %bitcast.58), custom_call_target="tpu_custom_call" | custom-call | tf_op jit(solution)/shard_map/pallas_call | solution.py:121
  67.5 0.0 copy-start.2
  67.5 0.0 copy-start.1
  67.5 1.2 convert_reduce_fusion
  68.7 0.1 reshape.190
  68.8 2.5 %copy.37 = bf16[32,8,8,512]{3,2,1,0:T(8,128)(2,1)S(1)} copy(bf16[32,8,8,512]{3,1,2,0:T(8,128)(2,1)} %bitcast.50) | data formatting | bytes 4194304
  71.3 0.1 multiply_reduce_fusion.2
  71.4 0.1 multiply_reduce_fusion.1
  71.6 0.1 fusion.41
  71.7 0.0 copy-done.2
  71.7 0.1 multiply_convert_fusion.1
  71.8 0.0 copy-done.1
  71.8 0.1 multiply_convert_fusion
  71.9 0.7 concatenate.22.refs_1_
  72.6 0.5 iota_compare_fusion.3
  73.1 0.6 iota_compare_fusion.2
  73.8 0.7 add_convert_fusion.1
  74.4 0.1 constant_dynamic-slice_fusion
  74.5 0.1 multiply_cosine_fusion
  74.7 0.1 pad_add_fusion
  74.8 0.0 all-gather.2.cloned.1.call-done
  74.8 2.9 %select_reduce_fusion = bf16[256,288]{0,1:T(8,128)(2,1)} fusion(bf16[16,256,288]{1,2,0:T(8,128)(2,1)} %all-gather.2.cloned.1.call-done, pred[16]{0:T(512)(128)(4,1)S(1)} %iota_compare_fusion.3), kind=kLoop, calls=%fused_computation.7 | loop fusion | flops 3465216 | bytes 2506768 | tf_op jit(solution)/shard_map/reduce_sum | solution.py:177
  77.7 23.4 %shard_map.119 = (bf16[4,288,256]{2,1,0:T(8,128)(2,1)}, bf16[32,8,1056]{2,1,0:T(8,128)(2,1)}) custom-call(bf16[288,256]{1,0:T(8,128)(2,1)} %bitcast.56, bf16[8,1056]{1,0:T(8,128)(2,1)} %concatenate.22.refs_1_), custom_call_target="tpu_custom_call" | custom-call | tf_op jit(solution)/shard_map/pallas_call | solution.py:121
  101.1 0.8 slice.86
  102.0 0.9 slice.79
  102.9 0.8 slice_bitcast_fusion.3
  103.7 1.1 slice_bitcast_fusion
  104.8 1.9 %convolution_bitcast_fusion = f32[8,256,96]{1,2,0:T(8,128)S(1)} fusion(bf16[8,96,768]{2,1,0:T(8,128)(2,1)} %get-tuple-element.14, bf16[256,1056]{1,0:T(8,128)(2,1)} %bitcast.55), kind=kOutput, calls=%fused_computation.18 | convolution fusion | flops 301989888 | bytes 2359296 | tf_op jit(solution)/shard_map/qk,hdk->hqd/dot_general | solution.py:190
  106.7 0.1 copy.32
  106.7 0.2 copy.30
  107.0 0.9 convolution_convert_fusion.1
  107.9 0.1 slice.85
  108.1 2.0 %fusion = (f32[8,256]{1,0:T(8,128)S(1)}, f32[8,256,1280]{2,1,0:T(8,128)S(1)}) fusion(pred[256,1280]{1,0:T(8,128)(4,1)S(1)} %pad_add_fusion, bf16[1280,8,32]{0,2,1:T(8,128)(2,1)S(1)} %broadcast_in_dim.51, bf16[1280,8,64]{0,2,1:T(8,128)(2,1)S(1)} %slice.85, bf16[8,256,16]{1,2,0:T(8,128)(2,1)S(1)} %get-tuple-element.18, ...), kind=kOutput, calls=%fused_computation.2 | convolution fusion | flops 516290560 | bytes 13180928 | tf_op jit(solution)/shard_map/hqd,khd->hqk/dot_general | solution.py:250
  110.1 3.2 %fusion.12.refs_0_ = bf16[8,64,256]{2,1,0:T(8,128)(2,1)} fusion(f32[8,256,1280]{2,1,0:T(8,128)S(1)} %get-tuple-element.24, f32[8,256]{1,0:T(8,128)S(1)} %compare_select_fusion, pred[256,1280]{1,0:T(8,128)(4,1)S(1)} %pad_add_fusion, bf16[1280,8,128]{0,2,1:T(8,128)(2,1)S(1)} %bitcast.47), kind=kOutput, calls=%fused_computation.19 | convolution fusion | flops 346161152 | bytes 12394496 | tf_op jit(solution)/shard_map/hqk,khd->hdq/dot_general | solution.py:259
  113.4 2.8 %fusion.1 = f32[8,256]{1,0:T(8,128)S(1)} fusion(f32[8,256,1280]{2,1,0:T(8,128)S(1)} %get-tuple-element.24, f32[8,256]{1,0:T(8,128)S(1)} %compare_select_fusion, pred[256,1280]{1,0:T(8,128)(4,1)S(1)} %pad_add_fusion), kind=kLoop, calls=%fused_computation.3 | loop fusion | flops 10483712 | bytes 10829824 | tf_op jit(solution)/shard_map/reduce_sum | solution.py:257
  116.2 0.6 pad_maximum_fusion.1.refs_1_
  116.8 16.2 %shard_map.120 = (bf16[8,64,256]{2,1,0:T(8,128)(2,1)}, f32[8,2,256]{2,1,0:T(2,128)}) custom-call(bf16[8,64,256]{2,1,0:T(8,128)(2,1)} %fusion.12.refs_0_, f32[8,2,256]{2,1,0:T(2,128)} %pad_maximum_fusion.1.refs_1_), custom_call_target="tpu_custom_call" | custom-call | tf_op jit(solution)/shard_map/pallas_call | solution.py:121
  133.0 0.7 slice.74
  133.7 0.7 copy.33
  134.5 1.0 multiply_reduce_fusion
  135.5 0.0 copy-done
  135.5 0.5 fusion.6
  136.0 1.5 copy.34
  137.5 37.9 %shard_map.121 = bf16[32,80,256]{2,1,0:T(8,128)(2,1)} custom-call(bf16[32,80,256]{2,1,0:T(8,128)(2,1)} %bitcast.48), custom_call_target="tpu_custom_call" | custom-call | tf_op jit(solution)/shard_map/pallas_call | solution.py:121
  175.4 2.1 %reduce_sum.122 = bf16[80,256]{1,0:T(8,128)(2,1)} reduce(bf16[32,80,256]{2,1,0:T(8,128)(2,1)} %shard_map.121, bf16[]{:T(256)} %constant.90.clone.1), dimensions={0}, to_apply=%region_13.14 | reduce | flops 634880 | bytes 1351682 | tf_op jit(solution)/shard_map/reduce_sum | solution.py:277
  (20 shorter events, 0.3 us)
Async XLA Ops:
  6.5 129.0 %copy-start = (bf16[64,2560]{1,0:T(8,128)(2,1)S(1)}, bf16[64,2560]{1,0:T(8,128)(2,1)}, u32[]{:S(2)}) copy-start(bf16[64,2560]{1,0:T(8,128)(2,1)} %param.18) | copy-start | bytes 983044
  6.5 68.3 %all-gather.2.cloned.1.call-start = ((), (), s32[]{:S(2)}) async-start(), calls=%async_computation | async-start | bytes 2506752 | tf_op jit(solution)/shard_map/all_gather | solution.py:175
  67.5 4.2 %copy-start.2 = (f32[256]{0:T(256)S(1)}, f32[256]{0:T(256)}, u32[]{:S(2)}) copy-start(f32[256]{0:T(256)} %param.15) | copy-start | bytes 3076
  67.5 4.3 %copy-start.1 = (f32[768]{0:T(1024)S(1)}, f32[768]{0:T(1024)}, u32[]{:S(2)}) copy-start(f32[768]{0:T(1024)} %param.14) | copy-start | bytes 9220
Sparse Core Ops, SparseCore 0:
  9.5 47.9 all-gather.1

commit v12 on v11

--- a/solution.py
+++ b/solution.py
@@ -155,16 +155,19 @@
     own_rows = group_rows // columns
     q_width = q_gain.shape[0]
     kv_width = kv_gain.shape[0]
-    request_ids = jnp.arange(home_slot.shape[0], dtype=jnp.int32)
-    slot_index = jnp.sum(jnp.where(request_ids == row_id, home_slot, 0))
-    cached_count = jnp.sum(jnp.where(request_ids == slot_index, cache_len, 0))
-    live_count = jnp.sum(jnp.where(request_ids == row_id, new_len, 0))
     partial_sums = jnp.dot(tokens, w_down, preferred_element_type=jnp.float32)
     pieces, line_query_weight = exchange(
         [partial_sums.astype(jnp.bfloat16).reshape(columns, -1, 128), w_q_up.T],
         [("all", False), ("y", True)],
         0,
     )
+    pieces, line_query_weight, home_slot, cache_len, new_len = lax.optimization_barrier(
+        (pieces, line_query_weight, home_slot, cache_len, new_len)
+    )
+    request_ids = jnp.arange(home_slot.shape[0], dtype=jnp.int32)
+    slot_index = jnp.sum(jnp.where(request_ids == row_id, home_slot, 0))
+    cached_count = jnp.sum(jnp.where(request_ids == slot_index, cache_len, 0))
+    live_count = jnp.sum(jnp.where(request_ids == row_id, new_len, 0))
     combined = jnp.sum(pieces.astype(jnp.float32), 0).reshape(own_rows, -1)
     own_position = cached_count + column_id * own_rows + jnp.arange(own_rows, dtype=jnp.int32)
     own_cos, own_sin = angle_tables(own_position, ROPE)

time: 187 us -> 186 us (level)
  no operation moved by 1% of the time
where the time goes in v12:
time: 186 us; the launch traced here: 183 us
  Pallas kernels  127 us (68%)
  other arithmetic  16.3 us (9%)
  between operations  16.3 us (9%)
  local copies, waits for them, and re-layouts  13.1 us (7%)
  matrix products  9.82 us (5%)
    pallas_call x4, Pallas kernels, exchange(): pl.pallas_call(functools.partial(_exchange_kernel, n, tuple(plan)), out_s...  127 us
  transfers between devices with their start and end apart: 1, of which 0 were waited for; matrix products, arithmetic and copies ran while one was open for 8% of the time, Pallas kernels for 27%

profile of v12, /device:TPU:6, one launch (start us, length us, event | category | flops | bytes accessed | tf_op | source)
XLA Modules:
  0.0 183.5 jit_solution(5024362187767048781)
XLA Ops:
  6.5 0.0 copy-start
  6.5 0.0 copy-start.5
  6.5 0.0 copy-start.3
  6.5 0.0 copy-start.4
  6.5 0.0 all-gather.2.cloned.1.call-start
  6.6 0.7 all-gather.2.cloned.1.call-update
  7.3 1.3 convolution_convert_fusion.2
  8.6 0.3 copy.29
  8.9 1.6 reshape.189.refs_0_
  10.5 49.8 %shard_map.118 = (bf16[32,66,128]{2,1,0:T(8,128)(2,1)}, bf16[8,96,768]{2,1,0:T(8,128)(2,1)}) custom-call(bf16[32,66,128]{2,1,0:T(8,128)(2,1)} %reshape.189.refs_0_, bf16[96,768]{1,0:T(8,128)(2,1)} %bitcast.58), custom_call_target="tpu_custom_call" | custom-call | tf_op jit(solution)/shard_map/pallas_call | solution.py:121
  60.3 0.0 copy-start.2
  60.3 0.0 copy-start.1
  60.4 0.0 copy-done.5
  60.4 0.7 fusion.44
  62.9 0.0 copy-done.3
  62.9 0.0 copy-done.4
  63.0 1.3 fusion.43
  64.9 0.7 dynamic-slice_bitcast_fusion
  65.6 0.1 select_reduce_fusion.1
  65.7 0.7 add_compare_fusion
  66.5 0.1 lt.45
  66.6 1.2 convert_reduce_fusion
  67.7 0.1 reshape.190
  67.8 2.5 %copy.37 = bf16[32,8,8,512]{3,2,1,0:T(8,128)(2,1)S(1)} copy(bf16[32,8,8,512]{3,1,2,0:T(8,128)(2,1)} %bitcast.50) | data formatting | bytes 4194304
  70.4 0.1 multiply_reduce_fusion.2
  70.5 0.1 multiply_reduce_fusion.1
  70.6 0.1 fusion.41
  70.7 0.0 copy-done.2
  70.7 0.1 multiply_convert_fusion.1
  70.8 0.0 copy-done.1
  70.8 0.1 multiply_convert_fusion
  70.9 0.7 concatenate.22.refs_1_
  71.6 0.6 iota_compare_fusion.3
  72.2 0.7 iota_compare_fusion.2
  72.9 0.6 add_convert_fusion.1
  73.6 0.1 constant_dynamic-slice_fusion
  73.7 0.1 multiply_cosine_fusion
  73.8 0.1 pad_add_fusion
  74.0 0.0 all-gather.2.cloned.1.call-done
  74.0 2.9 %select_reduce_fusion = bf16[256,288]{0,1:T(8,128)(2,1)} fusion(bf16[16,256,288]{1,2,0:T(8,128)(2,1)} %all-gather.2.cloned.1.call-done, pred[16]{0:T(512)(128)(4,1)S(1)} %iota_compare_fusion.3), kind=kLoop, calls=%fused_computation.7 | loop fusion | flops 3465216 | bytes 2506768 | tf_op jit(solution)/shard_map/reduce_sum | solution.py:180
  76.9 23.4 %shard_map.119 = (bf16[4,288,256]{2,1,0:T(8,128)(2,1)}, bf16[32,8,1056]{2,1,0:T(8,128)(2,1)}) custom-call(bf16[288,256]{1,0:T(8,128)(2,1)} %bitcast.56, bf16[8,1056]{1,0:T(8,128)(2,1)} %concatenate.22.refs_1_), custom_call_target="tpu_custom_call" | custom-call | tf_op jit(solution)/shard_map/pallas_call | solution.py:121
  100.2 0.8 slice.86
  101.1 0.9 slice.79
  102.0 0.8 slice_bitcast_fusion.3
  102.8 1.1 slice_bitcast_fusion
  103.9 1.9 %convolution_bitcast_fusion = f32[8,256,96]{1,2,0:T(8,128)S(1)} fusion(bf16[8,96,768]{2,1,0:T(8,128)(2,1)} %get-tuple-element.24, bf16[256,1056]{1,0:T(8,128)(2,1)} %bitcast.55), kind=kOutput, calls=%fused_computation.18 | convolution fusion | flops 301989888 | bytes 2359296 | tf_op jit(solution)/shard_map/qk,hdk->hqd/dot_general | solution.py:193
  105.8 0.1 copy.32
  105.9 0.2 copy.30
  106.1 0.9 convolution_convert_fusion.1
  107.0 0.1 slice.85
  107.2 2.0 %fusion = (f32[8,256]{1,0:T(8,128)S(1)}, f32[8,256,1280]{2,1,0:T(8,128)S(1)}) fusion(pred[256,1280]{1,0:T(8,128)(4,1)S(1)} %pad_add_fusion, bf16[1280,8,32]{0,2,1:T(8,128)(2,1)S(1)} %broadcast_in_dim.51, bf16[1280,8,64]{0,2,1:T(8,128)(2,1)S(1)} %slice.85, bf16[8,256,16]{1,2,0:T(8,128)(2,1)S(1)} %get-tuple-element.28, ...), kind=kOutput, calls=%fused_computation.2 | convolution fusion | flops 516290560 | bytes 13180928 | tf_op jit(solution)/shard_map/hqd,khd->hqk/dot_general | solution.py:253
  109.3 3.2 %fusion.12.refs_0_ = bf16[8,64,256]{2,1,0:T(8,128)(2,1)} fusion(f32[8,256,1280]{2,1,0:T(8,128)S(1)} %get-tuple-element.34, f32[8,256]{1,0:T(8,128)S(1)} %compare_select_fusion, pred[256,1280]{1,0:T(8,128)(4,1)S(1)} %pad_add_fusion, bf16[1280,8,128]{0,2,1:T(8,128)(2,1)S(1)} %bitcast.47), kind=kOutput, calls=%fused_computation.19 | convolution fusion | flops 346161152 | bytes 12394496 | tf_op jit(solution)/shard_map/hqk,khd->hdq/dot_general | solution.py:262
  112.5 2.8 %fusion.1 = f32[8,256]{1,0:T(8,128)S(1)} fusion(f32[8,256,1280]{2,1,0:T(8,128)S(1)} %get-tuple-element.34, f32[8,256]{1,0:T(8,128)S(1)} %compare_select_fusion, pred[256,1280]{1,0:T(8,128)(4,1)S(1)} %pad_add_fusion), kind=kLoop, calls=%fused_computation.3 | loop fusion | flops 10483712 | bytes 10829824 | tf_op jit(solution)/shard_map/reduce_sum | solution.py:260
  115.3 0.6 pad_maximum_fusion.1.refs_1_
  115.9 16.2 %shard_map.120 = (bf16[8,64,256]{2,1,0:T(8,128)(2,1)}, f32[8,2,256]{2,1,0:T(2,128)}) custom-call(bf16[8,64,256]{2,1,0:T(8,128)(2,1)} %fusion.12.refs_0_, f32[8,2,256]{2,1,0:T(2,128)} %pad_maximum_fusion.1.refs_1_), custom_call_target="tpu_custom_call" | custom-call | tf_op jit(solution)/shard_map/pallas_call | solution.py:121
  132.1 0.7 slice.74
  132.8 0.7 copy.33
  133.6 1.0 multiply_reduce_fusion
  134.6 0.0 copy-done
  134.6 0.5 fusion.6
  135.2 1.5 copy.34
  136.6 37.9 %shard_map.121 = bf16[32,80,256]{2,1,0:T(8,128)(2,1)} custom-call(bf16[32,80,256]{2,1,0:T(8,128)(2,1)} %bitcast.48), custom_call_target="tpu_custom_call" | custom-call | tf_op jit(solution)/shard_map/pallas_call | solution.py:121
  174.5 2.1 %reduce_sum.122 = bf16[80,256]{1,0:T(8,128)(2,1)} reduce(bf16[32,80,256]{2,1,0:T(8,128)(2,1)} %shard_map.121, bf16[]{:T(256)} %constant.90.clone.1), dimensions={0}, to_apply=%region_13.14 | reduce | flops 634880 | bytes 1351682 | tf_op jit(solution)/shard_map/reduce_sum | solution.py:280
  (20 shorter events, 0.3 us)
Async XLA Ops:
  6.5 128.1 %copy-start = (bf16[64,2560]{1,0:T(8,128)(2,1)S(1)}, bf16[64,2560]{1,0:T(8,128)(2,1)}, u32[]{:S(2)}) copy-start(bf16[64,2560]{1,0:T(8,128)(2,1)} %param.18) | copy-start | bytes 983044
  6.5 53.8 %copy-start.5 = (s32[16]{0:T(128)S(1)}, s32[16]{0:T(128)}, u32[]{:S(2)}) copy-start(s32[16]{0:T(128)} %param.23) | copy-start | bytes 196
  6.5 56.4 %copy-start.3 = (s32[16]{0:T(128)S(1)}, s32[16]{0:T(128)}, u32[]{:S(2)}) copy-start(s32[16]{0:T(128)} %param.21) | copy-start | bytes 196
  6.5 56.4 %copy-start.4 = (s32[16]{0:T(128)S(1)}, s32[16]{0:T(128)}, u32[]{:S(2)}) copy-start(s32[16]{0:T(128)} %param.20) | copy-start | bytes 196
  6.5 67.4 %all-gather.2.cloned.1.call-start = ((), (), s32[]{:S(2)}) async-start(), calls=%async_computation | async-start | bytes 2506752 | tf_op jit(solution)/shard_map/all_gather | solution.py:178
  60.3 10.4 %copy-start.2 = (f32[256]{0:T(256)S(1)}, f32[256]{0:T(256)}, u32[]{:S(2)}) copy-start(f32[256]{0:T(256)} %param.15) | copy-start | bytes 3076
  60.3 10.5 %copy-start.1 = (f32[768]{0:T(1024)S(1)}, f32[768]{0:T(1024)}, u32[]{:S(2)}) copy-start(f32[768]{0:T(1024)} %param.14) | copy-start | bytes 9220
Sparse Core Ops, SparseCore 0:
  9.5 47.9 all-gather.1

commit v13 on v12

--- a/solution.py
+++ b/solution.py
@@ -176,10 +176,7 @@
     own_rope = rotary(combined[:, q_width + kv_width :], own_cos, own_sin).astype(jnp.bfloat16)
     own_rows_all = jnp.concatenate([own_query, own_latent, own_rope], 1)
     segment = lax.all_gather(latent_cache, "row", axis=0, tiled=True)
-    matches = jnp.arange(segment.shape[0], dtype=jnp.int32) == slot_index
-    own_cache = jnp.sum(
-        jnp.where(matches[:, None, None], segment.astype(jnp.float32), 0.0), 0
-    ).astype(jnp.bfloat16)
+    own_cache = lax.dynamic_index_in_dim(segment, slot_index, axis=0, keepdims=False)
     chunk = own_cache.shape[0]
     cache_parts, all_rows = exchange(
         [own_cache.T, own_rows_all], [("x", True), ("all", True)], 2

time: 186 us -> 184 us (0.989)
  other arithmetic: 16.3 us -> 12.8 us
    reduce_sum x1 -> x0, other arithmetic: 2.88 us -> none  [body(): jnp.sum(jnp.where(matches[:, None, None], segment.astype(jnp.float32), 0....]
  transfers between devices with their start and end apart: 1 -> 1, of which waited for: 0 -> 0; matrix products, arithmetic and copies ran while one was open for 8% -> 7% of each run, Pallas kernels for 27% -> 27%
where the time goes in v13:
time: 184 us; the launch traced here: 182 us
  Pallas kernels  127 us (69%)
  between operations  16.4 us (9%)
  local copies, waits for them, and re-layouts  14.7 us (8%)
  other arithmetic  12.8 us (7%)
  matrix products  9.84 us (5%)
    pallas_call x4, Pallas kernels, exchange(): pl.pallas_call(functools.partial(_exchange_kernel, n, tuple(plan)), out_s...  127 us
  transfers between devices with their start and end apart: 1, of which 0 were waited for; matrix products, arithmetic and copies ran while one was open for 7% of the time, Pallas kernels for 27%

profile of v13, /device:TPU:6, one launch (start us, length us, event | category | flops | bytes accessed | tf_op | source)
XLA Modules:
  0.0 181.7 jit_solution(17517660105058570434)
XLA Ops:
  6.5 0.0 copy-start
  6.5 0.0 copy-start.5
  6.5 0.0 copy-start.3
  6.5 0.0 copy-start.4
  6.5 0.0 all-gather.2.cloned.1.call-start
  6.6 0.7 all-gather.2.cloned.1.call-update
  7.3 1.3 convolution_convert_fusion.2
  8.6 0.3 copy.29
  8.9 1.6 reshape.185.refs_0_
  10.5 49.8 %shard_map.118 = (bf16[32,66,128]{2,1,0:T(8,128)(2,1)}, bf16[8,96,768]{2,1,0:T(8,128)(2,1)}) custom-call(bf16[32,66,128]{2,1,0:T(8,128)(2,1)} %reshape.185.refs_0_, bf16[96,768]{1,0:T(8,128)(2,1)} %bitcast.58), custom_call_target="tpu_custom_call" | custom-call | tf_op jit(solution)/shard_map/pallas_call | solution.py:121
  60.3 0.0 copy-start.2
  60.3 0.0 copy-start.1
  60.4 0.0 copy-done.5
  60.4 0.6 fusion.45
  62.9 0.0 copy-done.3
  63.0 0.0 copy-done.4
  63.0 1.4 fusion.44
  65.0 0.7 fusion.43
  65.7 0.1 select_reduce_fusion
  65.8 0.8 add_compare_fusion
  66.6 0.1 lt.47
  66.7 1.2 convert_reduce_fusion
  67.9 0.1 reshape.186
  68.0 2.5 %copy.37 = bf16[32,8,8,512]{3,2,1,0:T(8,128)(2,1)S(1)} copy(bf16[32,8,8,512]{3,1,2,0:T(8,128)(2,1)} %bitcast.51) | data formatting | bytes 4194304
  70.5 0.1 multiply_reduce_fusion.2
  70.6 0.1 multiply_reduce_fusion.1
  70.8 0.1 fusion.41
  70.9 0.0 copy-done.2
  70.9 0.1 multiply_convert_fusion.1
  71.0 0.0 copy-done.1
  71.0 0.1 multiply_convert_fusion
  71.0 0.7 concatenate.22.refs_1_
  71.7 0.6 iota_compare_fusion.2
  72.4 0.7 add_convert_fusion.1
  73.1 0.1 constant_dynamic-slice_fusion.1
  73.2 0.1 multiply_cosine_fusion
  73.3 0.1 pad_add_fusion
  73.5 0.0 all-gather.2.cloned.1.call-done
  73.5 1.6 dynamic-slice_bitcast_fusion.refs_0_
  75.1 23.4 %shard_map.119 = (bf16[4,288,256]{2,1,0:T(8,128)(2,1)}, bf16[32,8,1056]{2,1,0:T(8,128)(2,1)}) custom-call(bf16[288,256]{1,0:T(8,128)(2,1)} %dynamic-slice_bitcast_fusion.refs_0_, bf16[8,1056]{1,0:T(8,128)(2,1)} %concatenate.22.refs_1_), custom_call_target="tpu_custom_call" | custom-call | tf_op jit(solution)/shard_map/pallas_call | solution.py:121
  98.4 0.8 slice.86
  99.3 0.9 slice.79
  100.2 0.8 slice_bitcast_fusion.3
  101.0 1.1 slice_bitcast_fusion
  102.1 1.9 %convolution_bitcast_fusion = f32[8,256,96]{1,2,0:T(8,128)S(1)} fusion(bf16[8,96,768]{2,1,0:T(8,128)(2,1)} %get-tuple-element.24, bf16[256,1056]{1,0:T(8,128)(2,1)} %bitcast.56), kind=kOutput, calls=%fused_computation.17 | convolution fusion | flops 301989888 | bytes 2359296 | tf_op jit(solution)/shard_map/qk,hdk->hqd/dot_general | solution.py:190
  104.0 0.1 copy.32
  104.0 0.2 copy.30
  104.3 0.9 convolution_convert_fusion.1
  105.2 0.1 slice.85
  105.4 2.0 %fusion = (f32[8,256]{1,0:T(8,128)S(1)}, f32[8,256,1280]{2,1,0:T(8,128)S(1)}) fusion(pred[256,1280]{1,0:T(8,128)(4,1)S(1)} %pad_add_fusion, bf16[1280,8,32]{0,2,1:T(8,128)(2,1)S(1)} %broadcast_in_dim.36, bf16[1280,8,64]{0,2,1:T(8,128)(2,1)S(1)} %slice.85, bf16[8,256,16]{1,2,0:T(8,128)(2,1)S(1)} %get-tuple-element.28, ...), kind=kOutput, calls=%fused_computation.2 | convolution fusion | flops 516290560 | bytes 13180928 | tf_op jit(solution)/shard_map/hqd,khd->hqk/dot_general | solution.py:250
  107.5 3.2 %fusion.12.refs_0_ = bf16[8,64,256]{2,1,0:T(8,128)(2,1)} fusion(f32[8,256,1280]{2,1,0:T(8,128)S(1)} %get-tuple-element.34, f32[8,256]{1,0:T(8,128)S(1)} %compare_select_fusion, pred[256,1280]{1,0:T(8,128)(4,1)S(1)} %pad_add_fusion, bf16[1280,8,128]{0,2,1:T(8,128)(2,1)S(1)} %bitcast.48), kind=kOutput, calls=%fused_computation.18 | convolution fusion | flops 346161152 | bytes 12394496 | tf_op jit(solution)/shard_map/hqk,khd->hdq/dot_general | solution.py:259
  110.7 2.8 %fusion.1 = f32[8,256]{1,0:T(8,128)S(1)} fusion(f32[8,256,1280]{2,1,0:T(8,128)S(1)} %get-tuple-element.34, f32[8,256]{1,0:T(8,128)S(1)} %compare_select_fusion, pred[256,1280]{1,0:T(8,128)(4,1)S(1)} %pad_add_fusion), kind=kLoop, calls=%fused_computation.3 | loop fusion | flops 10483712 | bytes 10829824 | tf_op jit(solution)/shard_map/reduce_sum | solution.py:257
  113.5 0.6 pad_maximum_fusion.1.refs_1_
  114.1 16.2 %shard_map.120 = (bf16[8,64,256]{2,1,0:T(8,128)(2,1)}, f32[8,2,256]{2,1,0:T(2,128)}) custom-call(bf16[8,64,256]{2,1,0:T(8,128)(2,1)} %fusion.12.refs_0_, f32[8,2,256]{2,1,0:T(2,128)} %pad_maximum_fusion.1.refs_1_), custom_call_target="tpu_custom_call" | custom-call | tf_op jit(solution)/shard_map/pallas_call | solution.py:121
  130.3 0.7 slice.74
  131.0 0.7 copy.33
  131.8 1.0 multiply_reduce_fusion
  132.8 0.0 copy-done
  132.8 0.5 fusion.6
  133.4 1.5 copy.34
  134.8 37.9 %shard_map.121 = bf16[32,80,256]{2,1,0:T(8,128)(2,1)} custom-call(bf16[32,80,256]{2,1,0:T(8,128)(2,1)} %bitcast.49), custom_call_target="tpu_custom_call" | custom-call | tf_op jit(solution)/shard_map/pallas_call | solution.py:121
  172.7 2.1 %reduce_sum.112 = bf16[80,256]{1,0:T(8,128)(2,1)} reduce(bf16[32,80,256]{2,1,0:T(8,128)(2,1)} %shard_map.121, bf16[]{:T(256)} %constant.94.clone.1), dimensions={0}, to_apply=%region_12.13 | reduce | flops 634880 | bytes 1351682 | tf_op jit(solution)/shard_map/reduce_sum | solution.py:277
  (20 shorter events, 0.3 us)
Async XLA Ops:
  6.5 126.3 %copy-start = (bf16[64,2560]{1,0:T(8,128)(2,1)S(1)}, bf16[64,2560]{1,0:T(8,128)(2,1)}, u32[]{:S(2)}) copy-start(bf16[64,2560]{1,0:T(8,128)(2,1)} %param.18) | copy-start | bytes 983044
  6.5 53.8 %copy-start.5 = (s32[16]{0:T(128)S(1)}, s32[16]{0:T(128)}, u32[]{:S(2)}) copy-start(s32[16]{0:T(128)} %param.23) | copy-start | bytes 196
  6.5 56.4 %copy-start.3 = (s32[16]{0:T(128)S(1)}, s32[16]{0:T(128)}, u32[]{:S(2)}) copy-start(s32[16]{0:T(128)} %param.21) | copy-start | bytes 196
  6.5 56.4 %copy-start.4 = (s32[16]{0:T(128)S(1)}, s32[16]{0:T(128)}, u32[]{:S(2)}) copy-start(s32[16]{0:T(128)} %param.20) | copy-start | bytes 196
  6.5 66.9 %all-gather.2.cloned.1.call-start = ((), (), s32[]{:S(2)}) async-start(), calls=%async_computation | async-start | bytes 2506752 | tf_op jit(solution)/shard_map/all_gather | solution.py:178
  60.3 10.6 %copy-start.2 = (f32[256]{0:T(256)S(1)}, f32[256]{0:T(256)}, u32[]{:S(2)}) copy-start(f32[256]{0:T(256)} %param.15) | copy-start | bytes 3076
  60.3 10.6 %copy-start.1 = (f32[768]{0:T(1024)S(1)}, f32[768]{0:T(1024)}, u32[]{:S(2)}) copy-start(f32[768]{0:T(1024)} %param.14) | copy-start | bytes 9220
Sparse Core Ops, SparseCore 0:
  9.5 47.9 all-gather.1

commit v14 on v13

--- a/solution.py
+++ b/solution.py
@@ -179,7 +179,7 @@
     own_cache = lax.dynamic_index_in_dim(segment, slot_index, axis=0, keepdims=False)
     chunk = own_cache.shape[0]
     cache_parts, all_rows = exchange(
-        [own_cache.T, own_rows_all], [("x", True), ("all", True)], 2
+        [own_cache.T, own_rows_all.reshape(-1, 128)], [("x", True), ("all", True)], 2
     )
     all_rows = all_rows.reshape(group_rows, -1)
     query_latent = all_rows[:, :q_width]

time: 184 us -> 185 us (level)
    reshape x0 -> x2, local copies, waits for them, and re-layouts: none -> 2.88 us  [the longest x1 2.17 us: body(): all_rows = all_rows.reshape(group_rows, -1)]
where the time goes in v14:
time: 185 us; the launch traced here: 182 us
  Pallas kernels  127 us (69%)
  between operations  16.4 us (9%)
  local copies, waits for them, and re-layouts  15.2 us (8%)
  other arithmetic  12.7 us (7%)
  matrix products  9.64 us (5%)
    pallas_call x4, Pallas kernels, exchange(): pl.pallas_call(functools.partial(_exchange_kernel, n, tuple(plan)), out_s...  127 us
  transfers between devices with their start and end apart: 1, of which 0 were waited for; matrix products, arithmetic and copies ran while one was open for 7% of the time, Pallas kernels for 27%

profile of v14, /device:TPU:6, one launch (start us, length us, event | category | flops | bytes accessed | tf_op | source)
XLA Modules:
  0.0 182.0 jit_solution(5329818990796003222)
XLA Ops:
  6.5 0.0 copy-start
  6.5 0.0 copy-start.5
  6.5 0.0 copy-start.3
  6.5 0.0 copy-start.4
  6.5 0.0 copy-start.2
  6.5 0.0 copy-start.1
  6.6 0.0 all-gather.2.cloned.1.call-start
  6.6 0.7 all-gather.2.cloned.1.call-update
  7.3 1.3 convolution_convert_fusion.2
  8.6 0.3 copy.29
  8.9 1.6 reshape.188.refs_0_
  10.5 49.8 %shard_map.118 = (bf16[32,66,128]{2,1,0:T(8,128)(2,1)}, bf16[8,96,768]{2,1,0:T(8,128)(2,1)}) custom-call(bf16[32,66,128]{2,1,0:T(8,128)(2,1)} %reshape.188.refs_0_, bf16[96,768]{1,0:T(8,128)(2,1)} %bitcast.54), custom_call_target="tpu_custom_call" | custom-call | tf_op jit(solution)/shard_map/pallas_call | solution.py:121
  60.4 0.0 copy-done.5
  60.4 0.6 fusion.45
  62.9 0.0 copy-done.3
  63.0 0.0 copy-done.4
  63.0 1.4 fusion.44
  65.0 0.7 fusion.43
  65.7 0.1 select_reduce_fusion
  65.8 0.8 add_compare_fusion
  66.6 0.1 lt.47
  66.7 1.2 convert_reduce_fusion
  67.9 0.1 reshape.189
  68.0 0.1 multiply_reduce_fusion.2
  68.1 0.1 multiply_reduce_fusion.1
  68.2 0.1 fusion.41
  68.3 0.0 copy-done.2
  68.4 0.1 multiply_convert_fusion.1
  68.4 0.0 copy-done.1
  68.4 0.1 multiply_convert_fusion
  68.5 0.1 concatenate.22
  68.6 0.7 reshape.190.refs_1_
  69.3 2.5 %copy.37 = bf16[32,8,8,512]{3,2,1,0:T(8,128)(2,1)S(1)} copy(bf16[32,8,8,512]{3,1,2,0:T(8,128)(2,1)} %bitcast.50) | data formatting | bytes 4194304
  71.8 0.6 iota_compare_fusion.2
  72.5 0.7 add_convert_fusion.1
  73.2 0.1 constant_dynamic-slice_fusion.1
  73.3 0.1 multiply_cosine_fusion
  73.5 0.1 pad_add_fusion
  73.6 0.0 all-gather.2.cloned.1.call-done
  73.6 1.6 dynamic-slice_bitcast_fusion.refs_0_
  75.2 23.4 %shard_map.119 = (bf16[4,288,256]{2,1,0:T(8,128)(2,1)}, bf16[32,66,128]{2,1,0:T(8,128)(2,1)}) custom-call(bf16[288,256]{1,0:T(8,128)(2,1)} %dynamic-slice_bitcast_fusion.refs_0_, bf16[66,128]{1,0:T(8,128)(2,1)} %reshape.190.refs_1_), custom_call_target="tpu_custom_call" | custom-call | tf_op jit(solution)/shard_map/pallas_call | solution.py:121
  98.5 2.2 %reshape.192 = bf16[256,1056]{1,0:T(8,128)(2,1)S(1)} reshape(bf16[32,66,128]{2,1,0:T(8,128)(2,1)} %get-tuple-element.23) | data formatting | bytes 1081344 | tf_op jit(solution)/shard_map/reshape | solution.py:184
  100.7 0.8 slice_bitcast_fusion.3
  101.6 1.1 slice_bitcast_fusion
  102.7 1.8 convolution_bitcast_fusion
  104.4 0.1 copy.32
  104.5 0.2 copy.30
  104.8 0.9 convolution_convert_fusion.1
  105.7 0.1 slice.85
  105.9 2.0 %fusion = (f32[8,256]{1,0:T(8,128)S(1)}, f32[8,256,1280]{2,1,0:T(8,128)S(1)}) fusion(pred[256,1280]{1,0:T(8,128)(4,1)S(1)} %pad_add_fusion, bf16[1280,8,32]{0,2,1:T(8,128)(2,1)S(1)} %broadcast_in_dim.36, bf16[1280,8,64]{0,2,1:T(8,128)(2,1)S(1)} %slice.85, bf16[8,256,16]{1,2,0:T(8,128)(2,1)S(1)} %get-tuple-element.28, ...), kind=kOutput, calls=%fused_computation.2 | convolution fusion | flops 516290560 | bytes 13180928 | tf_op jit(solution)/shard_map/hqd,khd->hqk/dot_general | solution.py:250
  107.9 3.1 %fusion.12.refs_0_ = bf16[8,64,256]{2,1,0:T(8,128)(2,1)} fusion(f32[8,256,1280]{2,1,0:T(8,128)S(1)} %get-tuple-element.34, f32[8,256]{1,0:T(8,128)S(1)} %compare_select_fusion, pred[256,1280]{1,0:T(8,128)(4,1)S(1)} %pad_add_fusion, bf16[1280,8,128]{0,2,1:T(8,128)(2,1)S(1)} %bitcast.47), kind=kOutput, calls=%fused_computation.18 | convolution fusion | flops 346161152 | bytes 12394496 | tf_op jit(solution)/shard_map/hqk,khd->hdq/dot_general | solution.py:259
  111.1 2.7 %fusion.1 = f32[8,256]{1,0:T(8,128)S(1)} fusion(f32[8,256,1280]{2,1,0:T(8,128)S(1)} %get-tuple-element.34, f32[8,256]{1,0:T(8,128)S(1)} %compare_select_fusion, pred[256,1280]{1,0:T(8,128)(4,1)S(1)} %pad_add_fusion), kind=kLoop, calls=%fused_computation.3 | loop fusion | flops 10483712 | bytes 10829824 | tf_op jit(solution)/shard_map/reduce_sum | solution.py:257
  113.8 0.6 pad_maximum_fusion.1.refs_1_
  114.4 16.2 %shard_map.120 = (bf16[8,64,256]{2,1,0:T(8,128)(2,1)}, f32[8,2,256]{2,1,0:T(2,128)}) custom-call(bf16[8,64,256]{2,1,0:T(8,128)(2,1)} %fusion.12.refs_0_, f32[8,2,256]{2,1,0:T(2,128)} %pad_maximum_fusion.1.refs_1_), custom_call_target="tpu_custom_call" | custom-call | tf_op jit(solution)/shard_map/pallas_call | solution.py:121
  130.6 0.7 slice.74
  131.3 0.7 copy.33
  132.1 1.0 multiply_reduce_fusion
  133.1 0.0 copy-done
  133.1 0.5 fusion.6
  133.6 1.5 copy.34
  135.1 37.9 %shard_map.121 = bf16[32,80,256]{2,1,0:T(8,128)(2,1)} custom-call(bf16[32,80,256]{2,1,0:T(8,128)(2,1)} %bitcast.48), custom_call_target="tpu_custom_call" | custom-call | tf_op jit(solution)/shard_map/pallas_call | solution.py:121
  173.0 2.1 %reduce_sum.112 = bf16[80,256]{1,0:T(8,128)(2,1)} reduce(bf16[32,80,256]{2,1,0:T(8,128)(2,1)} %shard_map.121, bf16[]{:T(256)} %constant.94.clone.1), dimensions={0}, to_apply=%region_12.13 | reduce | flops 634880 | bytes 1351682 | tf_op jit(solution)/shard_map/reduce_sum | solution.py:277
  (22 shorter events, 0.3 us)
Async XLA Ops:
  6.5 126.6 %copy-start = (bf16[64,2560]{1,0:T(8,128)(2,1)S(1)}, bf16[64,2560]{1,0:T(8,128)(2,1)}, u32[]{:S(2)}) copy-start(bf16[64,2560]{1,0:T(8,128)(2,1)} %param.18) | copy-start | bytes 983044
  6.5 53.8 %copy-start.5 = (s32[16]{0:T(128)S(1)}, s32[16]{0:T(128)}, u32[]{:S(2)}) copy-start(s32[16]{0:T(128)} %param.23) | copy-start | bytes 196
  6.5 56.4 %copy-start.3 = (s32[16]{0:T(128)S(1)}, s32[16]{0:T(128)}, u32[]{:S(2)}) copy-start(s32[16]{0:T(128)} %param.21) | copy-start | bytes 196
  6.5 56.4 %copy-start.4 = (s32[16]{0:T(128)S(1)}, s32[16]{0:T(128)}, u32[]{:S(2)}) copy-start(s32[16]{0:T(128)} %param.20) | copy-start | bytes 196
  6.5 61.8 %copy-start.2 = (f32[256]{0:T(256)S(1)}, f32[256]{0:T(256)}, u32[]{:S(2)}) copy-start(f32[256]{0:T(256)} %param.15) | copy-start | bytes 3076
  6.5 61.9 %copy-start.1 = (f32[768]{0:T(1024)S(1)}, f32[768]{0:T(1024)}, u32[]{:S(2)}) copy-start(f32[768]{0:T(1024)} %param.14) | copy-start | bytes 9220
  6.6 67.0 %all-gather.2.cloned.1.call-start = ((), (), s32[]{:S(2)}) async-start(), calls=%async_computation | async-start | bytes 2506752 | tf_op jit(solution)/shard_map/all_gather | solution.py:178
Sparse Core Ops, SparseCore 0:
  9.5 47.9 all-gather.1

commit v15 on v14

--- a/solution.py
+++ b/solution.py
@@ -71,11 +71,18 @@
     send_sem, recv_sem = refs[2 * count :]
     me = lax.axis_index("col")
     barrier = pltpu.get_barrier_semaphore()
-    for k in range(1, n):
-        pl.semaphore_signal(
-            barrier, inc=1, device_id={"col": lax.rem(me + k, n)}, device_id_type=MESH
-        )
-    pl.semaphore_wait(barrier, n - 1)
+    groups = sorted({group for group, _ in plan})
+    if "all" in groups:
+        groups = ["all"]
+    greeted = 0
+    for group in groups:
+        for k in range(1, _group_size(group, n)):
+            pl.semaphore_signal(
+                barrier, inc=1, device_id={"col": _group_peer(group, n, me, k)},
+                device_id_type=MESH,
+            )
+            greeted += 1
+    pl.semaphore_wait(barrier, greeted)
 
     def remote(a, k, peer, landing):
         group, gather = plan[a]

time: 185 us -> 184 us (level)
  transfers between devices with their start and end apart: 1 -> 1, of which waited for: 0 -> 0; matrix products, arithmetic and copies ran while one was open for 7% -> 7% of each run, Pallas kernels for 27% -> 28%
where the time goes in v15:
time: 184 us; the launch traced here: 181 us
  Pallas kernels  126 us (68%)
  between operations  16.4 us (9%)
  local copies, waits for them, and re-layouts  15.2 us (8%)
  other arithmetic  12.7 us (7%)
  matrix products  9.63 us (5%)
    pallas_call x4, Pallas kernels, exchange(): pl.pallas_call(functools.partial(_exchange_kernel, n, tuple(plan)), out_s...  126 us
  transfers between devices with their start and end apart: 1, of which 0 were waited for; matrix products, arithmetic and copies ran while one was open for 7% of the time, Pallas kernels for 28%

profile of v15, /device:TPU:6, one launch (start us, length us, event | category | flops | bytes accessed | tf_op | source)
XLA Modules:
  0.0 181.2 jit_solution(3124927073331506795)
XLA Ops:
  6.5 0.0 copy-start
  6.5 0.0 copy-start.5
  6.5 0.0 copy-start.3
  6.5 0.0 copy-start.4
  6.5 0.0 copy-start.2
  6.5 0.0 copy-start.1
  6.6 0.0 all-gather.2.cloned.1.call-start
  6.6 0.7 all-gather.2.cloned.1.call-update
  7.3 1.3 convolution_convert_fusion.2
  8.6 0.3 copy.29
  8.9 1.6 reshape.188.refs_0_
  10.5 49.8 %shard_map.118 = (bf16[32,66,128]{2,1,0:T(8,128)(2,1)}, bf16[8,96,768]{2,1,0:T(8,128)(2,1)}) custom-call(bf16[32,66,128]{2,1,0:T(8,128)(2,1)} %reshape.188.refs_0_, bf16[96,768]{1,0:T(8,128)(2,1)} %bitcast.54), custom_call_target="tpu_custom_call" | custom-call | tf_op jit(solution)/shard_map/pallas_call | solution.py:128
  60.4 0.0 copy-done.5
  60.4 0.6 fusion.45
  62.9 0.0 copy-done.3
  63.0 0.0 copy-done.4
  63.0 1.4 fusion.44
  65.0 0.7 fusion.43
  65.7 0.1 select_reduce_fusion
  65.8 0.8 add_compare_fusion
  66.6 0.1 lt.47
  66.7 1.2 convert_reduce_fusion
  67.9 0.1 reshape.189
  68.0 0.1 multiply_reduce_fusion.2
  68.1 0.1 multiply_reduce_fusion.1
  68.2 0.1 fusion.41
  68.3 0.0 copy-done.2
  68.4 0.1 multiply_convert_fusion.1
  68.4 0.0 copy-done.1
  68.4 0.1 multiply_convert_fusion
  68.5 0.1 concatenate.22
  68.6 0.7 reshape.190.refs_1_
  69.3 2.5 %copy.37 = bf16[32,8,8,512]{3,2,1,0:T(8,128)(2,1)S(1)} copy(bf16[32,8,8,512]{3,1,2,0:T(8,128)(2,1)} %bitcast.50) | data formatting | bytes 4194304
  71.8 0.6 iota_compare_fusion.2
  72.5 0.7 add_convert_fusion.1
  73.2 0.1 constant_dynamic-slice_fusion.1
  73.3 0.1 multiply_cosine_fusion
  73.5 0.1 pad_add_fusion
  73.6 0.0 all-gather.2.cloned.1.call-done
  73.6 1.6 dynamic-slice_bitcast_fusion.refs_0_
  75.2 23.4 %shard_map.119 = (bf16[4,288,256]{2,1,0:T(8,128)(2,1)}, bf16[32,66,128]{2,1,0:T(8,128)(2,1)}) custom-call(bf16[288,256]{1,0:T(8,128)(2,1)} %dynamic-slice_bitcast_fusion.refs_0_, bf16[66,128]{1,0:T(8,128)(2,1)} %reshape.190.refs_1_), custom_call_target="tpu_custom_call" | custom-call | tf_op jit(solution)/shard_map/pallas_call | solution.py:128
  98.5 2.2 %reshape.192 = bf16[256,1056]{1,0:T(8,128)(2,1)S(1)} reshape(bf16[32,66,128]{2,1,0:T(8,128)(2,1)} %get-tuple-element.23) | data formatting | bytes 1081344 | tf_op jit(solution)/shard_map/reshape | solution.py:191
  100.7 0.8 slice_bitcast_fusion.3
  101.6 1.1 slice_bitcast_fusion
  102.7 1.8 convolution_bitcast_fusion
  104.4 0.1 copy.32
  104.5 0.2 copy.30
  104.8 0.9 convolution_convert_fusion.1
  105.7 0.1 slice.85
  105.9 2.0 %fusion = (f32[8,256]{1,0:T(8,128)S(1)}, f32[8,256,1280]{2,1,0:T(8,128)S(1)}) fusion(pred[256,1280]{1,0:T(8,128)(4,1)S(1)} %pad_add_fusion, bf16[1280,8,32]{0,2,1:T(8,128)(2,1)S(1)} %broadcast_in_dim.36, bf16[1280,8,64]{0,2,1:T(8,128)(2,1)S(1)} %slice.85, bf16[8,256,16]{1,2,0:T(8,128)(2,1)S(1)} %get-tuple-element.28, ...), kind=kOutput, calls=%fused_computation.2 | convolution fusion | flops 516290560 | bytes 13180928 | tf_op jit(solution)/shard_map/hqd,khd->hqk/dot_general | solution.py:257
  107.9 3.1 %fusion.12.refs_0_ = bf16[8,64,256]{2,1,0:T(8,128)(2,1)} fusion(f32[8,256,1280]{2,1,0:T(8,128)S(1)} %get-tuple-element.34, f32[8,256]{1,0:T(8,128)S(1)} %compare_select_fusion, pred[256,1280]{1,0:T(8,128)(4,1)S(1)} %pad_add_fusion, bf16[1280,8,128]{0,2,1:T(8,128)(2,1)S(1)} %bitcast.47), kind=kOutput, calls=%fused_computation.18 | convolution fusion | flops 346161152 | bytes 12394496 | tf_op jit(solution)/shard_map/hqk,khd->hdq/dot_general | solution.py:266
  111.1 2.7 %fusion.1 = f32[8,256]{1,0:T(8,128)S(1)} fusion(f32[8,256,1280]{2,1,0:T(8,128)S(1)} %get-tuple-element.34, f32[8,256]{1,0:T(8,128)S(1)} %compare_select_fusion, pred[256,1280]{1,0:T(8,128)(4,1)S(1)} %pad_add_fusion), kind=kLoop, calls=%fused_computation.3 | loop fusion | flops 10483712 | bytes 10829824 | tf_op jit(solution)/shard_map/reduce_sum | solution.py:264
  113.8 0.6 pad_maximum_fusion.1.refs_1_
  114.4 15.4 %shard_map.120 = (bf16[8,64,256]{2,1,0:T(8,128)(2,1)}, f32[8,2,256]{2,1,0:T(2,128)}) custom-call(bf16[8,64,256]{2,1,0:T(8,128)(2,1)} %fusion.12.refs_0_, f32[8,2,256]{2,1,0:T(2,128)} %pad_maximum_fusion.1.refs_1_), custom_call_target="tpu_custom_call" | custom-call | tf_op jit(solution)/shard_map/pallas_call | solution.py:128
  129.8 0.7 slice.74
  130.5 0.7 copy.33
  131.3 1.0 multiply_reduce_fusion
  132.3 0.0 copy-done
  132.3 0.5 fusion.6
  132.9 1.5 copy.34
  134.3 37.9 %shard_map.121 = bf16[32,80,256]{2,1,0:T(8,128)(2,1)} custom-call(bf16[32,80,256]{2,1,0:T(8,128)(2,1)} %bitcast.48), custom_call_target="tpu_custom_call" | custom-call | tf_op jit(solution)/shard_map/pallas_call | solution.py:128
  172.2 2.1 %reduce_sum.112 = bf16[80,256]{1,0:T(8,128)(2,1)} reduce(bf16[32,80,256]{2,1,0:T(8,128)(2,1)} %shard_map.121, bf16[]{:T(256)} %constant.94.clone.1), dimensions={0}, to_apply=%region_12.13 | reduce | flops 634880 | bytes 1351682 | tf_op jit(solution)/shard_map/reduce_sum | solution.py:284
  (22 shorter events, 0.3 us)
Async XLA Ops:
  6.5 125.8 %copy-start = (bf16[64,2560]{1,0:T(8,128)(2,1)S(1)}, bf16[64,2560]{1,0:T(8,128)(2,1)}, u32[]{:S(2)}) copy-start(bf16[64,2560]{1,0:T(8,128)(2,1)} %param.18) | copy-start | bytes 983044
  6.5 53.8 %copy-start.5 = (s32[16]{0:T(128)S(1)}, s32[16]{0:T(128)}, u32[]{:S(2)}) copy-start(s32[16]{0:T(128)} %param.23) | copy-start | bytes 196
  6.5 56.4 %copy-start.3 = (s32[16]{0:T(128)S(1)}, s32[16]{0:T(128)}, u32[]{:S(2)}) copy-start(s32[16]{0:T(128)} %param.21) | copy-start | bytes 196
  6.5 56.4 %copy-start.4 = (s32[16]{0:T(128)S(1)}, s32[16]{0:T(128)}, u32[]{:S(2)}) copy-start(s32[16]{0:T(128)} %param.20) | copy-start | bytes 196
  6.5 61.8 %copy-start.2 = (f32[256]{0:T(256)S(1)}, f32[256]{0:T(256)}, u32[]{:S(2)}) copy-start(f32[256]{0:T(256)} %param.15) | copy-start | bytes 3076
  6.5 61.9 %copy-start.1 = (f32[768]{0:T(1024)S(1)}, f32[768]{0:T(1024)}, u32[]{:S(2)}) copy-start(f32[768]{0:T(1024)} %param.14) | copy-start | bytes 9220
  6.6 67.0 %all-gather.2.cloned.1.call-start = ((), (), s32[]{:S(2)}) async-start(), calls=%async_computation | async-start | bytes 2506752 | tf_op jit(solution)/shard_map/all_gather | solution.py:185
Sparse Core Ops, SparseCore 0:
  9.5 47.9 all-gather.1

commit v16 on v15

--- a/solution.py
+++ b/solution.py
@@ -280,8 +280,15 @@
     out_parts = lax.dot_general(
         w_out, attended, (((0,), (0,)), ((), ())), preferred_element_type=jnp.float32
     ).astype(jnp.bfloat16)
-    (out_pieces,) = exchange([out_parts.reshape(columns, -1, group_rows)], [("all", False)], 3)
-    summed_out = jnp.sum(out_pieces.astype(jnp.float32), 0)
+    feature_block = out_parts.shape[0] // columns
+    (lane_pieces,) = exchange(
+        [out_parts.reshape(lines, PLANE_X, feature_block, group_rows).transpose(1, 0, 2, 3)],
+        [("x", False)],
+        3,
+    )
+    lane_sums = jnp.sum(lane_pieces.astype(jnp.float32), 0).astype(jnp.bfloat16)
+    (line_pieces,) = exchange([lane_sums], [("y", False)], 5)
+    summed_out = jnp.sum(line_pieces.astype(jnp.float32), 0)
     result = summed_out.T.astype(jnp.bfloat16)
     return result
 

time: 184 us -> 183 us (level)
  Pallas kernels: 126 us -> 123 us
  other arithmetic: 12.7 us -> 14.6 us
    pallas_call x4 -> x5, Pallas kernels: 126 us -> 123 us  [exchange(): pl.pallas_call(functools.partial(_exchange_kernel, n, tuple(plan)), out_s...]
    reduce_sum x1 -> x2, other arithmetic: 2.13 us -> 3.99 us  [the longest x1 2.34 us: body(): lane_sums = jnp.sum(lane_pieces.astype(jnp.float32), 0).astype(jnp.bfloat16)]
  transfers between devices with their start and end apart: 1 -> 1, of which waited for: 0 -> 0; matrix products, arithmetic and copies ran while one was open for 7% -> 8% of each run, Pallas kernels for 28% -> 28%
where the time goes in v16:
time: 183 us; the launch traced here: 180 us
  Pallas kernels  123 us (67%)
  between operations  16.4 us (9%)
  local copies, waits for them, and re-layouts  15.6 us (9%)
  other arithmetic  14.6 us (8%)
  matrix products  9.75 us (5%)
    pallas_call x5, Pallas kernels, exchange(): pl.pallas_call(functools.partial(_exchange_kernel, n, tuple(plan)), out_s...  123 us
  transfers between devices with their start and end apart: 1, of which 0 were waited for; matrix products, arithmetic and copies ran while one was open for 8% of the time, Pallas kernels for 28%

profile of v16, /device:TPU:6, one launch (start us, length us, event | category | flops | bytes accessed | tf_op | source)
XLA Modules:
  0.0 180.2 jit_solution(9742008789058531163)
XLA Ops:
  6.5 0.0 copy-start
  6.5 0.0 copy-start.5
  6.5 0.0 copy-start.3
  6.5 0.0 copy-start.4
  6.5 0.0 copy-start.1
  6.6 0.0 all-gather.2.cloned.1.call-start
  6.6 0.7 all-gather.2.cloned.1.call-update
  7.3 1.3 convolution_convert_fusion.2
  8.6 0.3 copy.30
  8.9 1.6 reshape.188.refs_0_
  10.5 49.8 %shard_map.118 = (bf16[32,66,128]{2,1,0:T(8,128)(2,1)}, bf16[8,96,768]{2,1,0:T(8,128)(2,1)}) custom-call(bf16[32,66,128]{2,1,0:T(8,128)(2,1)} %reshape.188.refs_0_, bf16[96,768]{1,0:T(8,128)(2,1)} %bitcast.58), custom_call_target="tpu_custom_call" | custom-call | tf_op jit(solution)/shard_map/pallas_call | solution.py:128
  60.4 0.0 copy-done.5
  60.4 0.6 fusion.45
  62.9 0.0 copy-done.3
  63.0 0.0 copy-done.4
  63.0 1.4 fusion.44
  65.0 0.7 fusion.43
  65.7 0.1 select_reduce_fusion
  65.8 0.8 add_compare_fusion
  66.6 0.1 lt.47
  66.7 1.2 convert_reduce_fusion
  67.9 0.1 reshape.189
  68.0 0.1 multiply_reduce_fusion.2
  68.1 0.1 multiply_reduce_fusion.1
  68.2 0.1 fusion.41
  68.3 0.0 copy-done.2
  68.4 0.1 multiply_convert_fusion.1
  68.4 0.0 copy-done.1
  68.4 0.1 multiply_convert_fusion
  68.5 0.1 concatenate.22
  68.6 0.7 reshape.190.refs_1_
  69.3 2.5 %copy.39 = bf16[32,8,8,512]{3,2,1,0:T(8,128)(2,1)S(1)} copy(bf16[32,8,8,512]{3,1,2,0:T(8,128)(2,1)} %bitcast.54) | data formatting | bytes 4194304
  71.8 0.6 iota_compare_fusion.2
  72.5 0.7 add_convert_fusion.1
  73.2 0.1 constant_dynamic-slice_fusion.1
  73.3 0.1 multiply_cosine_fusion
  73.5 0.1 pad_add_fusion
  73.6 0.0 all-gather.2.cloned.1.call-done
  73.6 1.6 dynamic-slice_bitcast_fusion.refs_0_
  75.2 23.4 %shard_map.119 = (bf16[4,288,256]{2,1,0:T(8,128)(2,1)}, bf16[32,66,128]{2,1,0:T(8,128)(2,1)}) custom-call(bf16[288,256]{1,0:T(8,128)(2,1)} %dynamic-slice_bitcast_fusion.refs_0_, bf16[66,128]{1,0:T(8,128)(2,1)} %reshape.190.refs_1_), custom_call_target="tpu_custom_call" | custom-call | tf_op jit(solution)/shard_map/pallas_call | solution.py:128
  98.5 2.2 %reshape.192 = bf16[256,1056]{1,0:T(8,128)(2,1)S(1)} reshape(bf16[32,66,128]{2,1,0:T(8,128)(2,1)} %get-tuple-element.23) | data formatting | bytes 1081344 | tf_op jit(solution)/shard_map/reshape | solution.py:191
  100.7 0.8 slice_bitcast_fusion.3
  101.6 1.1 slice_bitcast_fusion
  102.7 1.8 convolution_bitcast_fusion
  104.5 0.1 copy.33
  104.5 0.2 copy.31
  104.8 0.9 convolution_convert_fusion.1
  105.7 0.1 slice.85
  105.9 2.0 %fusion = (f32[8,256]{1,0:T(8,128)S(1)}, f32[8,256,1280]{2,1,0:T(8,128)S(1)}) fusion(pred[256,1280]{1,0:T(8,128)(4,1)S(1)} %pad_add_fusion, bf16[1280,8,32]{0,2,1:T(8,128)(2,1)S(1)} %broadcast_in_dim.36, bf16[1280,8,64]{0,2,1:T(8,128)(2,1)S(1)} %slice.85, bf16[8,256,16]{1,2,0:T(8,128)(2,1)S(1)} %get-tuple-element.28, ...), kind=kOutput, calls=%fused_computation.2 | convolution fusion | flops 516290560 | bytes 13180928 | tf_op jit(solution)/shard_map/hqd,khd->hqk/dot_general | solution.py:257
  107.9 3.2 %fusion.12.refs_0_ = bf16[8,64,256]{2,1,0:T(8,128)(2,1)} fusion(f32[8,256,1280]{2,1,0:T(8,128)S(1)} %get-tuple-element.34, f32[8,256]{1,0:T(8,128)S(1)} %compare_select_fusion, pred[256,1280]{1,0:T(8,128)(4,1)S(1)} %pad_add_fusion, bf16[1280,8,128]{0,2,1:T(8,128)(2,1)S(1)} %bitcast.50), kind=kOutput, calls=%fused_computation.19 | convolution fusion | flops 346161152 | bytes 12394496 | tf_op jit(solution)/shard_map/hqk,khd->hdq/dot_general | solution.py:266
  111.2 2.8 %fusion.1 = f32[8,256]{1,0:T(8,128)S(1)} fusion(f32[8,256,1280]{2,1,0:T(8,128)S(1)} %get-tuple-element.34, f32[8,256]{1,0:T(8,128)S(1)} %compare_select_fusion, pred[256,1280]{1,0:T(8,128)(4,1)S(1)} %pad_add_fusion), kind=kLoop, calls=%fused_computation.3 | loop fusion | flops 10483712 | bytes 10829824 | tf_op jit(solution)/shard_map/reduce_sum | solution.py:264
  114.0 0.6 pad_maximum_fusion.1.refs_1_
  114.6 15.4 %shard_map.120 = (bf16[8,64,256]{2,1,0:T(8,128)(2,1)}, f32[8,2,256]{2,1,0:T(2,128)}) custom-call(bf16[8,64,256]{2,1,0:T(8,128)(2,1)} %fusion.12.refs_0_, f32[8,2,256]{2,1,0:T(2,128)} %pad_maximum_fusion.1.refs_1_), custom_call_target="tpu_custom_call" | custom-call | tf_op jit(solution)/shard_map/pallas_call | solution.py:128
  130.0 0.7 slice.74
  130.7 0.7 copy.34
  131.5 1.0 multiply_reduce_fusion
  132.5 0.0 copy-done
  132.6 0.5 fusion.6
  133.1 0.6 copy.35
  133.7 1.2 copy.47
  134.9 18.8 %shard_map.121 = bf16[4,8,80,256]{3,2,1,0:T(8,128)(2,1)} custom-call(bf16[4,8,80,256]{3,2,1,0:T(8,128)(2,1)} %bitcast.52), custom_call_target="tpu_custom_call" | custom-call | tf_op jit(solution)/shard_map/pallas_call | solution.py:128
  153.7 2.3 %reduce_sum.124.refs_0_ = bf16[8,80,256]{2,1,0:T(8,128)(2,1)} reduce(bf16[4,8,80,256]{3,2,1,0:T(8,128)(2,1)} %shard_map.121, bf16[]{:T(256)} %constant.95.clone.1), dimensions={0}, to_apply=%region_12.13 | reduce | flops 491520 | bytes 1638402 | tf_op jit(solution)/shard_map/reduce_sum | solution.py:289
  156.1 15.7 %shard_map.122 = bf16[8,80,256]{2,1,0:T(8,128)(2,1)} custom-call(bf16[8,80,256]{2,1,0:T(8,128)(2,1)} %reduce_sum.124.refs_0_), custom_call_target="tpu_custom_call" | custom-call | tf_op jit(solution)/shard_map/pallas_call | solution.py:128
  171.7 1.6 reduce_sum.125
  (23 shorter events, 0.3 us)
Async XLA Ops:
  6.5 126.0 %copy-start = (bf16[64,2560]{1,0:T(8,128)(2,1)S(1)}, bf16[64,2560]{1,0:T(8,128)(2,1)}, u32[]{:S(2)}) copy-start(bf16[64,2560]{1,0:T(8,128)(2,1)} %param.18) | copy-start | bytes 983044
  6.5 53.8 %copy-start.5 = (s32[16]{0:T(128)S(1)}, s32[16]{0:T(128)}, u32[]{:S(2)}) copy-start(s32[16]{0:T(128)} %param.23) | copy-start | bytes 196
  6.5 56.4 %copy-start.3 = (s32[16]{0:T(128)S(1)}, s32[16]{0:T(128)}, u32[]{:S(2)}) copy-start(s32[16]{0:T(128)} %param.21) | copy-start | bytes 196
  6.5 56.4 %copy-start.4 = (s32[16]{0:T(128)S(1)}, s32[16]{0:T(128)}, u32[]{:S(2)}) copy-start(s32[16]{0:T(128)} %param.20) | copy-start | bytes 196
  6.5 61.8 %copy-start.2 = (f32[256]{0:T(256)S(1)}, f32[256]{0:T(256)}, u32[]{:S(2)}) copy-start(f32[256]{0:T(256)} %param.15) | copy-start | bytes 3076
  6.5 61.9 %copy-start.1 = (f32[768]{0:T(1024)S(1)}, f32[768]{0:T(1024)}, u32[]{:S(2)}) copy-start(f32[768]{0:T(1024)} %param.14) | copy-start | bytes 9220
  6.6 67.0 %all-gather.2.cloned.1.call-start = ((), (), s32[]{:S(2)}) async-start(), calls=%async_computation | async-start | bytes 2506752 | tf_op jit(solution)/shard_map/all_gather | solution.py:185
Sparse Core Ops, SparseCore 0:
  9.5 47.9 all-gather.1

commit v17 on v16

--- a/solution.py
+++ b/solution.py
@@ -67,11 +67,13 @@
 
 def _exchange_kernel(n, plan, *refs):
     count = len(plan)
-    sources, targets = refs[:count], refs[count : 2 * count]
-    send_sem, recv_sem = refs[2 * count :]
+    sources, results = refs[:count], refs[count : 2 * count]
+    send_sem, recv_sem = refs[2 * count : 2 * count + 2]
+    landings = iter(refs[2 * count + 2 :])
+    targets = [next(landings) if summed else results[a] for a, (_, _, summed) in enumerate(plan)]
     me = lax.axis_index("col")
     barrier = pltpu.get_barrier_semaphore()
-    groups = sorted({group for group, _ in plan})
+    groups = sorted({group for group, _, _ in plan})
     if "all" in groups:
         groups = ["all"]
     greeted = 0
@@ -85,7 +87,7 @@
     pl.semaphore_wait(barrier, greeted)
 
     def remote(a, k, peer, landing):
-        group, gather = plan[a]
+        group, gather, _ = plan[a]
         x_ref = sources[a]
         return pltpu.make_async_remote_copy(
             src_ref=x_ref if gather else x_ref.at[_group_slot(group, peer)],
@@ -97,12 +99,12 @@
         )
 
     sends = []
-    for a, (group, gather) in enumerate(plan):
+    for a, (group, gather, _) in enumerate(plan):
         for k in range(1, _group_size(group, n)):
             copy = remote(a, k, _group_peer(group, n, me, k), _group_slot(group, me))
             copy.start()
             sends.append(copy)
-    for a, (group, gather) in enumerate(plan):
+    for a, (group, gather, _) in enumerate(plan):
         mine = _group_slot(group, me)
         if gather:
             targets[a][mine] = sources[a][...]
@@ -110,30 +112,42 @@
             targets[a][mine] = sources[a][mine]
     for copy in sends:
         copy.wait_send()
-    for a, (group, gather) in enumerate(plan):
+    for a, (group, gather, summed) in enumerate(plan):
         size = _group_size(group, n)
         for k in range(1, size):
             source = _group_peer(group, n, me, size - k)
             remote(a, k, source, _group_slot(group, source)).wait_recv()
+        if summed:
+            total = targets[a][0].astype(jnp.float32)
+            for j in range(1, size):
+                total = total + targets[a][j].astype(jnp.float32)
+            results[a][...] = total.astype(results[a].dtype)
 
 
 def exchange(arrays, plan, collective_id):
     n = lax.axis_size("col")
-    shapes = [
-        jax.ShapeDtypeStruct(
-            ((_group_size(group, n),) + x.shape) if gather else x.shape, x.dtype
-        )
-        for x, (group, gather) in zip(arrays, plan)
-    ]
+    plan = tuple((entry + (None,))[:3] for entry in plan)
+    shapes = []
+    landings = []
+    for x, (group, gather, summed) in zip(arrays, plan):
+        if summed:
+            shapes.append(jax.ShapeDtypeStruct(x.shape[1:], summed))
+            landings.append(pltpu.VMEM(x.shape, x.dtype))
+        else:
+            size = _group_size(group, n)
+            shapes.append(
+                jax.ShapeDtypeStruct(((size,) + x.shape) if gather else x.shape, x.dtype)
+            )
     return pl.pallas_call(
-        functools.partial(_exchange_kernel, n, tuple(plan)),
+        functools.partial(_exchange_kernel, n, plan),
         out_shape=shapes,
         in_specs=[pl.BlockSpec(memory_space=pltpu.VMEM)] * len(arrays),
         out_specs=[pl.BlockSpec(memory_space=pltpu.VMEM)] * len(arrays),
         scratch_shapes=[
             pltpu.SemaphoreType.DMA((len(arrays), n)),
             pltpu.SemaphoreType.DMA((len(arrays), n)),
-        ],
+        ]
+        + landings,
         compiler_params=pltpu.CompilerParams(collective_id=collective_id, has_side_effects=True),
     )(*arrays)
 
@@ -165,7 +179,7 @@
     partial_sums = jnp.dot(tokens, w_down, preferred_element_type=jnp.float32)
     pieces, line_query_weight = exchange(
         [partial_sums.astype(jnp.bfloat16).reshape(columns, -1, 128), w_q_up.T],
-        [("all", False), ("y", True)],
+        [("all", False, jnp.float32), ("y", True)],
         0,
     )
     pieces, line_query_weight, home_slot, cache_len, new_len = lax.optimization_barrier(
@@ -175,7 +189,7 @@
     slot_index = jnp.sum(jnp.where(request_ids == row_id, home_slot, 0))
     cached_count = jnp.sum(jnp.where(request_ids == slot_index, cache_len, 0))
     live_count = jnp.sum(jnp.where(request_ids == row_id, new_len, 0))
-    combined = jnp.sum(pieces.astype(jnp.float32), 0).reshape(own_rows, -1)
+    combined = pieces.reshape(own_rows, -1)
     own_position = cached_count + column_id * own_rows + jnp.arange(own_rows, dtype=jnp.int32)
     own_cos, own_sin = angle_tables(own_position, ROPE)
     own_query = rms_scale(combined[:, :q_width], q_gain).astype(jnp.bfloat16)
@@ -283,13 +297,11 @@
     feature_block = out_parts.shape[0] // columns
     (lane_pieces,) = exchange(
         [out_parts.reshape(lines, PLANE_X, feature_block, group_rows).transpose(1, 0, 2, 3)],
-        [("x", False)],
+        [("x", False, jnp.bfloat16)],
         3,
     )
-    lane_sums = jnp.sum(lane_pieces.astype(jnp.float32), 0).astype(jnp.bfloat16)
-    (line_pieces,) = exchange([lane_sums], [("y", False)], 5)
-    summed_out = jnp.sum(line_pieces.astype(jnp.float32), 0)
-    result = summed_out.T.astype(jnp.bfloat16)
+    (summed_out,) = exchange([lane_pieces], [("y", False, jnp.bfloat16)], 5)
+    result = summed_out.T
     return result
 
 

time: 183 us -> 179 us (0.978)
  other arithmetic: 14.6 us -> 9.02 us
  local copies, waits for them, and re-layouts: 15.6 us -> 17.7 us
    reduce_sum x3 -> x0, other arithmetic: 5.16 us -> none  [the longest x1 2.34 us: body(): lane_sums = jnp.sum(lane_pieces.astype(jnp.float32), 0).astype(jnp.bfloat16)]
    unnamed x14 -> x15, local copies, waits for them, and re-layouts: 3.36 us -> 4.76 us
  transfers between devices with their start and end apart: 1 -> 1, of which waited for: 0 -> 0; matrix products, arithmetic and copies ran while one was open for 8% -> 7% of each run, Pallas kernels for 28% -> 28%
where the time goes in v17:
time: 179 us; the launch traced here: 176 us
  Pallas kernels  123 us (69%)
  local copies, waits for them, and re-layouts  17.7 us (10%)
  between operations  16.3 us (9%)
  matrix products  9.64 us (5%)
  other arithmetic  9.02 us (5%)
    pallas_call x5, Pallas kernels, exchange(): pl.pallas_call(functools.partial(_exchange_kernel, n, plan), out_shape=sh...  123 us
    unnamed x15, local copies, waits for them, and re-layouts  4.76 us
  transfers between devices with their start and end apart: 1, of which 0 were waited for; matrix products, arithmetic and copies ran while one was open for 7% of the time, Pallas kernels for 28%

profile of v17, /device:TPU:6, one launch (start us, length us, event | category | flops | bytes accessed | tf_op | source)
XLA Modules:
  0.0 176.1 jit_solution(8812494359084590090)
XLA Ops:
  6.5 0.0 copy-start
  6.5 0.0 copy-start.5
  6.5 0.0 copy-start.3
  6.5 0.0 copy-start.4
  6.5 0.0 copy-start.2
  6.5 0.0 copy-start.1
  6.6 0.0 all-gather.2.cloned.1.call-start
  6.6 0.7 all-gather.2.cloned.1.call-update
  7.3 1.3 convolution_convert_fusion.2
  8.6 0.3 copy.30
  8.9 1.6 reshape.188.refs_0_
  10.5 49.7 %shard_map.118 = (f32[66,128]{1,0:T(8,128)}, bf16[8,96,768]{2,1,0:T(8,128)(2,1)}) custom-call(bf16[32,66,128]{2,1,0:T(8,128)(2,1)} %reshape.188.refs_0_, bf16[96,768]{1,0:T(8,128)(2,1)} %bitcast.59), custom_call_target="tpu_custom_call" | custom-call | tf_op jit(solution)/shard_map/pallas_call | solution.py:141
  60.2 0.0 copy-done.5
  60.2 0.6 fusion.45
  62.8 0.0 copy-done.3
  62.8 0.0 copy-done.4
  62.8 1.3 fusion.44
  64.6 0.7 fusion.43
  65.3 0.1 select_reduce_fusion
  65.4 0.7 add_compare_fusion
  66.1 0.1 lt.47
  66.2 0.8 reshape.189
  67.1 0.1 multiply_reduce_fusion.2
  67.2 0.1 multiply_reduce_fusion.1
  67.3 0.1 fusion.41
  67.5 0.0 copy-done.2
  67.5 0.1 multiply_convert_fusion.1
  67.5 0.0 copy-done.1
  67.5 0.1 multiply_convert_fusion
  67.6 0.1 concatenate.22
  67.7 0.7 reshape.190.refs_1_
  68.4 2.5 %copy.39 = bf16[32,8,8,512]{3,2,1,0:T(8,128)(2,1)S(1)} copy(bf16[32,8,8,512]{3,1,2,0:T(8,128)(2,1)} %bitcast.54) | data formatting | bytes 4194304
  71.0 0.6 iota_compare_fusion.2
  71.5 0.6 add_convert_fusion.1
  72.1 0.1 constant_dynamic-slice_fusion.1
  72.2 0.1 multiply_cosine_fusion
  72.4 0.1 pad_add_fusion
  72.5 0.0 all-gather.2.cloned.1.call-done
  72.5 1.6 dynamic-slice_bitcast_fusion.refs_0_
  74.1 23.4 %shard_map.119 = (bf16[4,288,256]{2,1,0:T(8,128)(2,1)}, bf16[32,66,128]{2,1,0:T(8,128)(2,1)}) custom-call(bf16[288,256]{1,0:T(8,128)(2,1)} %dynamic-slice_bitcast_fusion.refs_0_, bf16[66,128]{1,0:T(8,128)(2,1)} %reshape.190.refs_1_), custom_call_target="tpu_custom_call" | custom-call | tf_op jit(solution)/shard_map/pallas_call | solution.py:141
  97.5 2.2 %reshape.192 = bf16[256,1056]{1,0:T(8,128)(2,1)S(1)} reshape(bf16[32,66,128]{2,1,0:T(8,128)(2,1)} %get-tuple-element.23) | data formatting | bytes 1081344 | tf_op jit(solution)/shard_map/reshape | solution.py:205
  99.7 0.8 slice_bitcast_fusion.3
  100.5 1.1 slice_bitcast_fusion
  101.6 1.8 %convolution_bitcast_fusion = f32[8,256,96]{1,2,0:T(8,128)S(1)} fusion(bf16[8,96,768]{2,1,0:T(8,128)(2,1)} %get-tuple-element.24, bf16[256,1056]{1,0:T(8,128)(2,1)S(1)} %reshape.192), kind=kOutput, calls=%fused_computation.18 | convolution fusion | flops 301989888 | bytes 2359296 | tf_op jit(solution)/shard_map/qk,hdk->hqd/dot_general | solution.py:211
  103.4 0.1 copy.33
  103.5 0.2 copy.31
  103.7 0.9 convolution_convert_fusion.1
  104.6 0.1 slice.85
  104.8 2.0 %fusion = (f32[8,256]{1,0:T(8,128)S(1)}, f32[8,256,1280]{2,1,0:T(8,128)S(1)}) fusion(pred[256,1280]{1,0:T(8,128)(4,1)S(1)} %pad_add_fusion, bf16[1280,8,32]{0,2,1:T(8,128)(2,1)S(1)} %broadcast_in_dim.36, bf16[1280,8,64]{0,2,1:T(8,128)(2,1)S(1)} %slice.85, bf16[8,256,16]{1,2,0:T(8,128)(2,1)S(1)} %get-tuple-element.28, ...), kind=kOutput, calls=%fused_computation.2 | convolution fusion | flops 516290560 | bytes 13180928 | tf_op jit(solution)/shard_map/hqd,khd->hqk/dot_general | solution.py:271
  106.8 3.1 %fusion.12.refs_0_ = bf16[8,64,256]{2,1,0:T(8,128)(2,1)} fusion(f32[8,256,1280]{2,1,0:T(8,128)S(1)} %get-tuple-element.34, f32[8,256]{1,0:T(8,128)S(1)} %compare_select_fusion, pred[256,1280]{1,0:T(8,128)(4,1)S(1)} %pad_add_fusion, bf16[1280,8,128]{0,2,1:T(8,128)(2,1)S(1)} %bitcast.50), kind=kOutput, calls=%fused_computation.19 | convolution fusion | flops 346161152 | bytes 12394496 | tf_op jit(solution)/shard_map/hqk,khd->hdq/dot_general | solution.py:280
  110.0 2.7 %fusion.1 = f32[8,256]{1,0:T(8,128)S(1)} fusion(f32[8,256,1280]{2,1,0:T(8,128)S(1)} %get-tuple-element.34, f32[8,256]{1,0:T(8,128)S(1)} %compare_select_fusion, pred[256,1280]{1,0:T(8,128)(4,1)S(1)} %pad_add_fusion), kind=kLoop, calls=%fused_computation.3 | loop fusion | flops 10483712 | bytes 10829824 | tf_op jit(solution)/shard_map/reduce_sum | solution.py:278
  112.7 0.6 pad_maximum_fusion.1.refs_1_
  113.3 15.4 %shard_map.120 = (bf16[8,64,256]{2,1,0:T(8,128)(2,1)}, f32[8,2,256]{2,1,0:T(2,128)}) custom-call(bf16[8,64,256]{2,1,0:T(8,128)(2,1)} %fusion.12.refs_0_, f32[8,2,256]{2,1,0:T(2,128)} %pad_maximum_fusion.1.refs_1_), custom_call_target="tpu_custom_call" | custom-call | tf_op jit(solution)/shard_map/pallas_call | solution.py:141
  128.7 0.7 slice.74
  129.5 0.7 copy.34
  130.3 1.0 multiply_reduce_fusion
  131.3 0.0 copy-done
  131.3 0.5 fusion.6
  131.8 0.6 copy.35
  132.4 1.2 copy.47
  133.6 18.7 %shard_map.121.refs_0_ = bf16[8,80,256]{2,1,0:T(8,128)(2,1)} custom-call(bf16[4,8,80,256]{3,2,1,0:T(8,128)(2,1)} %bitcast.52), custom_call_target="tpu_custom_call" | custom-call | tf_op jit(solution)/shard_map/pallas_call | solution.py:141
  152.3 15.6 %shard_map.122 = bf16[80,256]{1,0:T(8,128)(2,1)} custom-call(bf16[8,80,256]{2,1,0:T(8,128)(2,1)} %shard_map.121.refs_0_), custom_call_target="tpu_custom_call" | custom-call | tf_op jit(solution)/shard_map/pallas_call | solution.py:141
  167.9 1.4 copy.49
  (22 shorter events, 0.3 us)
Async XLA Ops:
  6.5 124.7 %copy-start = (bf16[64,2560]{1,0:T(8,128)(2,1)S(1)}, bf16[64,2560]{1,0:T(8,128)(2,1)}, u32[]{:S(2)}) copy-start(bf16[64,2560]{1,0:T(8,128)(2,1)} %param.18) | copy-start | bytes 983044
  6.5 53.7 %copy-start.5 = (s32[16]{0:T(128)S(1)}, s32[16]{0:T(128)}, u32[]{:S(2)}) copy-start(s32[16]{0:T(128)} %param.23) | copy-start | bytes 196
  6.5 56.2 %copy-start.3 = (s32[16]{0:T(128)S(1)}, s32[16]{0:T(128)}, u32[]{:S(2)}) copy-start(s32[16]{0:T(128)} %param.21) | copy-start | bytes 196
  6.5 56.2 %copy-start.4 = (s32[16]{0:T(128)S(1)}, s32[16]{0:T(128)}, u32[]{:S(2)}) copy-start(s32[16]{0:T(128)} %param.20) | copy-start | bytes 196
  6.5 60.9 %copy-start.2 = (f32[256]{0:T(256)S(1)}, f32[256]{0:T(256)}, u32[]{:S(2)}) copy-start(f32[256]{0:T(256)} %param.15) | copy-start | bytes 3076
  6.5 61.0 %copy-start.1 = (f32[768]{0:T(1024)S(1)}, f32[768]{0:T(1024)}, u32[]{:S(2)}) copy-start(f32[768]{0:T(1024)} %param.14) | copy-start | bytes 9220
  6.6 66.0 %all-gather.2.cloned.1.call-start = ((), (), s32[]{:S(2)}) async-start(), calls=%async_computation | async-start | bytes 2506752 | tf_op jit(solution)/shard_map/all_gather | solution.py:199
Sparse Core Ops, SparseCore 0:
  9.5 47.9 all-gather.1

commit v18 on v17

--- a/solution.py
+++ b/solution.py
@@ -70,10 +70,10 @@
     sources, results = refs[:count], refs[count : 2 * count]
     send_sem, recv_sem = refs[2 * count : 2 * count + 2]
     landings = iter(refs[2 * count + 2 :])
-    targets = [next(landings) if summed else results[a] for a, (_, _, summed) in enumerate(plan)]
+    targets = [next(landings) if plan[a][2] else results[a] for a in range(count)]
     me = lax.axis_index("col")
     barrier = pltpu.get_barrier_semaphore()
-    groups = sorted({group for group, _, _ in plan})
+    groups = sorted({entry[0] for entry in plan})
     if "all" in groups:
         groups = ["all"]
     greeted = 0
@@ -87,10 +87,11 @@
     pl.semaphore_wait(barrier, greeted)
 
     def remote(a, k, peer, landing):
-        group, gather, _ = plan[a]
+        group, gather, _, axis = plan[a]
         x_ref = sources[a]
+        slot = _group_slot(group, peer)
         return pltpu.make_async_remote_copy(
-            src_ref=x_ref if gather else x_ref.at[_group_slot(group, peer)],
+            src_ref=x_ref if gather else (x_ref.at[slot] if axis == 0 else x_ref.at[:, slot]),
             dst_ref=targets[a].at[landing],
             send_sem=send_sem.at[a, k],
             recv_sem=recv_sem.at[a, k],
@@ -99,20 +100,22 @@
         )
 
     sends = []
-    for a, (group, gather, _) in enumerate(plan):
+    for a, (group, gather, _, _) in enumerate(plan):
         for k in range(1, _group_size(group, n)):
             copy = remote(a, k, _group_peer(group, n, me, k), _group_slot(group, me))
             copy.start()
             sends.append(copy)
-    for a, (group, gather, _) in enumerate(plan):
+    for a, (group, gather, _, axis) in enumerate(plan):
         mine = _group_slot(group, me)
         if gather:
             targets[a][mine] = sources[a][...]
+        elif axis == 0:
+            targets[a][mine] = sources[a][mine]
         else:
-            targets[a][mine] = sources[a][mine]
+            targets[a][mine] = sources[a][:, mine]
     for copy in sends:
         copy.wait_send()
-    for a, (group, gather, summed) in enumerate(plan):
+    for a, (group, gather, summed, _) in enumerate(plan):
         size = _group_size(group, n)
         for k in range(1, size):
             source = _group_peer(group, n, me, size - k)
@@ -126,13 +129,15 @@
 
 def exchange(arrays, plan, collective_id):
     n = lax.axis_size("col")
-    plan = tuple((entry + (None,))[:3] for entry in plan)
+    plan = tuple(tuple(entry) + (None, 0)[len(entry) - 2 :] for entry in plan)
     shapes = []
     landings = []
-    for x, (group, gather, summed) in zip(arrays, plan):
+    for x, (group, gather, summed, axis) in zip(arrays, plan):
         if summed:
-            shapes.append(jax.ShapeDtypeStruct(x.shape[1:], summed))
-            landings.append(pltpu.VMEM(x.shape, x.dtype))
+            chunk_shape = x.shape[:axis] + x.shape[axis + 1 :]
+            size = x.shape[axis]
+            shapes.append(jax.ShapeDtypeStruct(chunk_shape, summed))
+            landings.append(pltpu.VMEM((size,) + chunk_shape, x.dtype))
         else:
             size = _group_size(group, n)
             shapes.append(
@@ -296,8 +301,8 @@
     ).astype(jnp.bfloat16)
     feature_block = out_parts.shape[0] // columns
     (lane_pieces,) = exchange(
-        [out_parts.reshape(lines, PLANE_X, feature_block, group_rows).transpose(1, 0, 2, 3)],
-        [("x", False, jnp.bfloat16)],
+        [out_parts.reshape(lines, PLANE_X, feature_block, group_rows)],
+        [("x", False, jnp.bfloat16, 1)],
         3,
     )
     (summed_out,) = exchange([lane_pieces], [("y", False, jnp.bfloat16)], 5)

time: 179 us -> 179 us (level)
  no operation moved by 1% of the time
where the time goes in v18:
time: 179 us; the launch traced here: 176 us
  Pallas kernels  123 us (69%)
  local copies, waits for them, and re-layouts  17.4 us (10%)
  between operations  16.3 us (9%)
  matrix products  9.64 us (5%)
  other arithmetic  9.02 us (5%)
    pallas_call x5, Pallas kernels, exchange(): pl.pallas_call(functools.partial(_exchange_kernel, n, plan), out_shape=sh...  123 us
    unnamed x15, local copies, waits for them, and re-layouts  4.76 us
  transfers between devices with their start and end apart: 1, of which 0 were waited for; matrix products, arithmetic and copies ran while one was open for 7% of the time, Pallas kernels for 28%

profile of v18, /device:TPU:6, one launch (start us, length us, event | category | flops | bytes accessed | tf_op | source)
XLA Modules:
  0.0 175.8 jit_solution(15632272033303850392)
XLA Ops:
  6.5 0.0 copy-start
  6.5 0.0 copy-start.5
  6.5 0.0 copy-start.3
  6.5 0.0 copy-start.4
  6.5 0.0 copy-start.2
  6.5 0.0 copy-start.1
  6.6 0.0 all-gather.2.cloned.1.call-start
  6.6 0.7 all-gather.2.cloned.1.call-update
  7.3 1.3 convolution_convert_fusion.2
  8.6 0.3 copy.29
  8.9 1.6 reshape.188.refs_0_
  10.5 49.7 %shard_map.118 = (f32[66,128]{1,0:T(8,128)}, bf16[8,96,768]{2,1,0:T(8,128)(2,1)}) custom-call(bf16[32,66,128]{2,1,0:T(8,128)(2,1)} %reshape.188.refs_0_, bf16[96,768]{1,0:T(8,128)(2,1)} %bitcast.55), custom_call_target="tpu_custom_call" | custom-call | tf_op jit(solution)/shard_map/pallas_call | solution.py:146
  60.2 0.0 copy-done.5
  60.2 0.6 fusion.45
  62.8 0.0 copy-done.3
  62.8 0.0 copy-done.4
  62.8 1.3 fusion.44
  64.6 0.7 fusion.43
  65.3 0.1 select_reduce_fusion
  65.4 0.7 add_compare_fusion
  66.1 0.1 lt.47
  66.2 0.8 reshape.189
  67.1 0.1 multiply_reduce_fusion.2
  67.2 0.1 multiply_reduce_fusion.1
  67.3 0.1 fusion.41
  67.5 0.0 copy-done.2
  67.5 0.1 multiply_convert_fusion.1
  67.5 0.0 copy-done.1
  67.5 0.1 multiply_convert_fusion
  67.6 0.1 concatenate.22
  67.7 0.7 reshape.190.refs_1_
  68.4 2.5 %copy.37 = bf16[32,8,8,512]{3,2,1,0:T(8,128)(2,1)S(1)} copy(bf16[32,8,8,512]{3,1,2,0:T(8,128)(2,1)} %bitcast.50) | data formatting | bytes 4194304
  71.0 0.6 iota_compare_fusion.2
  71.5 0.6 add_convert_fusion.1
  72.1 0.1 constant_dynamic-slice_fusion.1
  72.2 0.1 multiply_cosine_fusion
  72.4 0.1 pad_add_fusion
  72.5 0.0 all-gather.2.cloned.1.call-done
  72.5 1.6 dynamic-slice_bitcast_fusion.refs_0_
  74.1 23.4 %shard_map.119 = (bf16[4,288,256]{2,1,0:T(8,128)(2,1)}, bf16[32,66,128]{2,1,0:T(8,128)(2,1)}) custom-call(bf16[288,256]{1,0:T(8,128)(2,1)} %dynamic-slice_bitcast_fusion.refs_0_, bf16[66,128]{1,0:T(8,128)(2,1)} %reshape.190.refs_1_), custom_call_target="tpu_custom_call" | custom-call | tf_op jit(solution)/shard_map/pallas_call | solution.py:146
  97.5 2.2 %reshape.192 = bf16[256,1056]{1,0:T(8,128)(2,1)S(1)} reshape(bf16[32,66,128]{2,1,0:T(8,128)(2,1)} %get-tuple-element.23) | data formatting | bytes 1081344 | tf_op jit(solution)/shard_map/reshape | solution.py:210
  99.7 0.8 slice_bitcast_fusion.3
  100.5 1.1 slice_bitcast_fusion
  101.6 1.8 %convolution_bitcast_fusion = f32[8,256,96]{1,2,0:T(8,128)S(1)} fusion(bf16[8,96,768]{2,1,0:T(8,128)(2,1)} %get-tuple-element.24, bf16[256,1056]{1,0:T(8,128)(2,1)S(1)} %reshape.192), kind=kOutput, calls=%fused_computation.17 | convolution fusion | flops 301989888 | bytes 2359296 | tf_op jit(solution)/shard_map/qk,hdk->hqd/dot_general | solution.py:216
  103.4 0.1 copy.32
  103.5 0.2 copy.30
  103.7 0.9 convolution_convert_fusion.1
  104.6 0.1 slice.85
  104.8 2.0 %fusion = (f32[8,256]{1,0:T(8,128)S(1)}, f32[8,256,1280]{2,1,0:T(8,128)S(1)}) fusion(pred[256,1280]{1,0:T(8,128)(4,1)S(1)} %pad_add_fusion, bf16[1280,8,32]{0,2,1:T(8,128)(2,1)S(1)} %broadcast_in_dim.36, bf16[1280,8,64]{0,2,1:T(8,128)(2,1)S(1)} %slice.85, bf16[8,256,16]{1,2,0:T(8,128)(2,1)S(1)} %get-tuple-element.28, ...), kind=kOutput, calls=%fused_computation.2 | convolution fusion | flops 516290560 | bytes 13180928 | tf_op jit(solution)/shard_map/hqd,khd->hqk/dot_general | solution.py:276
  106.8 3.1 %fusion.12.refs_0_ = bf16[8,64,256]{2,1,0:T(8,128)(2,1)} fusion(f32[8,256,1280]{2,1,0:T(8,128)S(1)} %get-tuple-element.34, f32[8,256]{1,0:T(8,128)S(1)} %compare_select_fusion, pred[256,1280]{1,0:T(8,128)(4,1)S(1)} %pad_add_fusion, bf16[1280,8,128]{0,2,1:T(8,128)(2,1)S(1)} %bitcast.47), kind=kOutput, calls=%fused_computation.18 | convolution fusion | flops 346161152 | bytes 12394496 | tf_op jit(solution)/shard_map/hqk,khd->hdq/dot_general | solution.py:285
  110.0 2.7 %fusion.1 = f32[8,256]{1,0:T(8,128)S(1)} fusion(f32[8,256,1280]{2,1,0:T(8,128)S(1)} %get-tuple-element.34, f32[8,256]{1,0:T(8,128)S(1)} %compare_select_fusion, pred[256,1280]{1,0:T(8,128)(4,1)S(1)} %pad_add_fusion), kind=kLoop, calls=%fused_computation.3 | loop fusion | flops 10483712 | bytes 10829824 | tf_op jit(solution)/shard_map/reduce_sum | solution.py:283
  112.7 0.6 pad_maximum_fusion.1.refs_1_
  113.3 15.4 %shard_map.120 = (bf16[8,64,256]{2,1,0:T(8,128)(2,1)}, f32[8,2,256]{2,1,0:T(2,128)}) custom-call(bf16[8,64,256]{2,1,0:T(8,128)(2,1)} %fusion.12.refs_0_, f32[8,2,256]{2,1,0:T(2,128)} %pad_maximum_fusion.1.refs_1_), custom_call_target="tpu_custom_call" | custom-call | tf_op jit(solution)/shard_map/pallas_call | solution.py:146
  128.7 0.7 slice.74
  129.5 0.7 copy.33
  130.3 1.0 multiply_reduce_fusion
  131.3 0.0 copy-done
  131.3 0.5 fusion.6
  131.8 1.5 copy.34
  133.3 18.7 %shard_map.121.refs_0_ = bf16[8,80,256]{2,1,0:T(8,128)(2,1)} custom-call(bf16[8,4,80,256]{3,2,1,0:T(8,128)(2,1)} %bitcast.48), custom_call_target="tpu_custom_call" | custom-call | tf_op jit(solution)/shard_map/pallas_call | solution.py:146
  151.9 15.6 %shard_map.122 = bf16[80,256]{1,0:T(8,128)(2,1)} custom-call(bf16[8,80,256]{2,1,0:T(8,128)(2,1)} %shard_map.121.refs_0_), custom_call_target="tpu_custom_call" | custom-call | tf_op jit(solution)/shard_map/pallas_call | solution.py:146
  167.5 1.4 copy.45
  (22 shorter events, 0.3 us)
Async XLA Ops:
  6.5 124.7 %copy-start = (bf16[64,2560]{1,0:T(8,128)(2,1)S(1)}, bf16[64,2560]{1,0:T(8,128)(2,1)}, u32[]{:S(2)}) copy-start(bf16[64,2560]{1,0:T(8,128)(2,1)} %param.18) | copy-start | bytes 983044
  6.5 53.7 %copy-start.5 = (s32[16]{0:T(128)S(1)}, s32[16]{0:T(128)}, u32[]{:S(2)}) copy-start(s32[16]{0:T(128)} %param.23) | copy-start | bytes 196
  6.5 56.2 %copy-start.3 = (s32[16]{0:T(128)S(1)}, s32[16]{0:T(128)}, u32[]{:S(2)}) copy-start(s32[16]{0:T(128)} %param.21) | copy-start | bytes 196
  6.5 56.2 %copy-start.4 = (s32[16]{0:T(128)S(1)}, s32[16]{0:T(128)}, u32[]{:S(2)}) copy-start(s32[16]{0:T(128)} %param.20) | copy-start | bytes 196
  6.5 60.9 %copy-start.2 = (f32[256]{0:T(256)S(1)}, f32[256]{0:T(256)}, u32[]{:S(2)}) copy-start(f32[256]{0:T(256)} %param.15) | copy-start | bytes 3076
  6.5 61.0 %copy-start.1 = (f32[768]{0:T(1024)S(1)}, f32[768]{0:T(1024)}, u32[]{:S(2)}) copy-start(f32[768]{0:T(1024)} %param.14) | copy-start | bytes 9220
  6.6 66.0 %all-gather.2.cloned.1.call-start = ((), (), s32[]{:S(2)}) async-start(), calls=%async_computation | async-start | bytes 2506752 | tf_op jit(solution)/shard_map/all_gather | solution.py:204
Sparse Core Ops, SparseCore 0:
  9.5 47.9 all-gather.1

commit v19 on v18

--- a/solution.py
+++ b/solution.py
@@ -120,11 +120,26 @@
         for k in range(1, size):
             source = _group_peer(group, n, me, size - k)
             remote(a, k, source, _group_slot(group, source)).wait_recv()
+        if summed == "merge":
+            continue
         if summed:
             total = targets[a][0].astype(jnp.float32)
             for j in range(1, size):
                 total = total + targets[a][j].astype(jnp.float32)
             results[a][...] = total.astype(results[a].dtype)
+    if plan[0][2] == "merge":
+        parts, stats = targets[0], targets[1]
+        size = parts.shape[0]
+        peak = stats[0][0:1, :]
+        for j in range(1, size):
+            peak = jnp.maximum(peak, stats[j][0:1, :])
+        total = jnp.zeros_like(peak)
+        merged = jnp.zeros(parts.shape[1:], jnp.float32)
+        for j in range(size):
+            factor = jnp.exp(stats[j][0:1, :] - peak)
+            total = total + factor * stats[j][1:2, :]
+            merged = merged + factor * parts[j].astype(jnp.float32)
+        results[0][...] = (merged / total).astype(results[0].dtype)
 
 
 def exchange(arrays, plan, collective_id):
@@ -136,7 +151,9 @@
         if summed:
             chunk_shape = x.shape[:axis] + x.shape[axis + 1 :]
             size = x.shape[axis]
-            shapes.append(jax.ShapeDtypeStruct(chunk_shape, summed))
+            shapes.append(
+                jax.ShapeDtypeStruct(chunk_shape, jnp.bfloat16 if summed == "merge" else summed)
+            )
             landings.append(pltpu.VMEM((size,) + chunk_shape, x.dtype))
         else:
             size = _group_size(group, n)
@@ -286,14 +303,11 @@
         "hqk,khd->hdq", exponent.astype(jnp.bfloat16), values, preferred_element_type=jnp.float32
     )
     stats = jnp.stack([row_peak, row_total], 1)
-    summed_parts, stat_parts = exchange(
-        [summed.astype(jnp.bfloat16), stats], [("y", False), ("y", False)], 4
-    )
-    peak = jnp.max(stat_parts[:, 0, :], 0)
-    factor = jnp.exp(stat_parts[:, 0, :] - peak[None, :])
-    total = jnp.sum(factor * stat_parts[:, 1, :], 0)
-    merged = jnp.sum(factor[:, None, :] * summed_parts.astype(jnp.float32), 0)
-    attended = (merged / total[None, :]).astype(jnp.bfloat16)
+    attended, _ = exchange(
+        [summed.astype(jnp.bfloat16), stats],
+        [("y", False, "merge"), ("y", False, jnp.float32)],
+        4,
+    )
     live_rows = jnp.arange(group_rows, dtype=jnp.int32) < live_count
     attended = jnp.where(live_rows[None, :], attended, jnp.zeros_like(attended))
     out_parts = lax.dot_general(

time: 179 us -> 177 us (0.989)
  transfers between devices with their start and end apart: 1 -> 1, of which waited for: 0 -> 0; matrix products, arithmetic and copies ran while one was open for 7% -> 7% of each run, Pallas kernels for 28% -> 29%
where the time goes in v19:
time: 177 us; the launch traced here: 174 us
  Pallas kernels  123 us (69%)
  between operations  16.3 us (9%)
  local copies, waits for them, and re-layouts  15.9 us (9%)
  matrix products  10.4 us (6%)
  other arithmetic  7.95 us (4%)
    pallas_call x5, Pallas kernels, exchange(): pl.pallas_call(functools.partial(_exchange_kernel, n, plan), out_shape=sh...  123 us
    unnamed x15, local copies, waits for them, and re-layouts  4.76 us
  transfers between devices with their start and end apart: 1, of which 0 were waited for; matrix products, arithmetic and copies ran while one was open for 7% of the time, Pallas kernels for 29%

profile of v19, /device:TPU:6, one launch (start us, length us, event | category | flops | bytes accessed | tf_op | source)
XLA Modules:
  0.0 174.0 jit_solution(7625863028987632418)
XLA Ops:
  6.5 0.0 copy-start
  6.5 0.0 copy-start.5
  6.5 0.0 copy-start.3
  6.5 0.0 copy-start.4
  6.5 0.0 copy-start.2
  6.5 0.0 copy-start.1
  6.6 0.0 all-gather.2.cloned.1.call-start
  6.6 0.7 all-gather.2.cloned.1.call-update
  7.3 1.3 convolution_convert_fusion.2
  8.6 0.3 copy.26
  8.9 1.6 reshape.181.refs_0_
  10.5 49.7 %shard_map.118 = (f32[66,128]{1,0:T(8,128)}, bf16[8,96,768]{2,1,0:T(8,128)(2,1)}) custom-call(bf16[32,66,128]{2,1,0:T(8,128)(2,1)} %reshape.181.refs_0_, bf16[96,768]{1,0:T(8,128)(2,1)} %bitcast.43), custom_call_target="tpu_custom_call" | custom-call | tf_op jit(solution)/shard_map/pallas_call | solution.py:163
  60.2 0.0 copy-done.5
  60.2 0.6 fusion.43
  62.8 0.0 copy-done.3
  62.8 0.0 copy-done.4
  62.8 1.3 fusion.42
  64.6 0.7 fusion.41
  65.3 0.1 select_reduce_fusion
  65.4 0.7 add_compare_fusion
  66.1 0.1 lt.47
  66.2 0.8 reshape.182
  67.1 0.1 multiply_reduce_fusion.1
  67.2 0.1 multiply_reduce_fusion
  67.3 0.1 fusion.39
  67.5 0.0 copy-done.2
  67.5 0.1 multiply_convert_fusion.1
  67.5 0.0 copy-done.1
  67.5 0.1 multiply_convert_fusion
  67.6 0.1 concatenate.22
  67.7 0.7 reshape.183.refs_1_
  68.4 2.5 %copy.32 = bf16[32,8,8,512]{3,2,1,0:T(8,128)(2,1)S(1)} copy(bf16[32,8,8,512]{3,1,2,0:T(8,128)(2,1)} %bitcast.38) | data formatting | bytes 4194304
  71.0 0.6 iota_compare_fusion.2
  71.5 0.6 add_convert_fusion.1
  72.1 0.1 constant_dynamic-slice_fusion.1
  72.2 0.1 multiply_cosine_fusion
  72.4 0.1 pad_add_fusion
  72.5 0.0 all-gather.2.cloned.1.call-done
  72.5 1.6 dynamic-slice_bitcast_fusion.refs_0_
  74.1 23.4 %shard_map.119 = (bf16[4,288,256]{2,1,0:T(8,128)(2,1)}, bf16[32,66,128]{2,1,0:T(8,128)(2,1)}) custom-call(bf16[288,256]{1,0:T(8,128)(2,1)} %dynamic-slice_bitcast_fusion.refs_0_, bf16[66,128]{1,0:T(8,128)(2,1)} %reshape.183.refs_1_), custom_call_target="tpu_custom_call" | custom-call | tf_op jit(solution)/shard_map/pallas_call | solution.py:163
  97.5 2.2 %reshape.185 = bf16[256,1056]{1,0:T(8,128)(2,1)S(1)} reshape(bf16[32,66,128]{2,1,0:T(8,128)(2,1)} %get-tuple-element.22) | data formatting | bytes 1081344 | tf_op jit(solution)/shard_map/reshape | solution.py:227
  99.7 0.8 slice_bitcast_fusion.3
  100.5 1.1 slice_bitcast_fusion
  101.6 1.8 %convolution_bitcast_fusion = f32[8,256,96]{1,2,0:T(8,128)S(1)} fusion(bf16[8,96,768]{2,1,0:T(8,128)(2,1)} %get-tuple-element.23, bf16[256,1056]{1,0:T(8,128)(2,1)S(1)} %reshape.185), kind=kOutput, calls=%fused_computation.17 | convolution fusion | flops 301989888 | bytes 2359296 | tf_op jit(solution)/shard_map/qk,hdk->hqd/dot_general | solution.py:233
  103.4 0.1 copy.29
  103.5 0.2 copy.27
  103.7 0.9 convolution_convert_fusion.1
  104.6 0.1 slice.76
  104.8 2.0 %fusion = (f32[8,256]{1,0:T(8,128)S(1)}, f32[8,256,1280]{2,1,0:T(8,128)S(1)}) fusion(pred[256,1280]{1,0:T(8,128)(4,1)S(1)} %pad_add_fusion, bf16[1280,8,32]{0,2,1:T(8,128)(2,1)S(1)} %broadcast_in_dim.36, bf16[1280,8,64]{0,2,1:T(8,128)(2,1)S(1)} %slice.76, bf16[8,256,16]{1,2,0:T(8,128)(2,1)S(1)} %get-tuple-element.26, ...), kind=kOutput, calls=%fused_computation.2 | convolution fusion | flops 516290560 | bytes 13180928 | tf_op jit(solution)/shard_map/hqd,khd->hqk/dot_general | solution.py:293
  106.8 3.1 %fusion.12.refs_0_ = bf16[8,64,256]{2,1,0:T(8,128)(2,1)} fusion(f32[8,256,1280]{2,1,0:T(8,128)S(1)} %get-tuple-element.32, f32[8,256]{1,0:T(8,128)S(1)} %compare_select_fusion, pred[256,1280]{1,0:T(8,128)(4,1)S(1)} %pad_add_fusion, bf16[1280,8,128]{0,2,1:T(8,128)(2,1)S(1)} %bitcast.35), kind=kOutput, calls=%fused_computation.18 | convolution fusion | flops 346161152 | bytes 12394496 | tf_op jit(solution)/shard_map/hqk,khd->hdq/dot_general | solution.py:302
  110.0 2.7 %fusion.1 = f32[8,256]{1,0:T(8,128)S(1)} fusion(f32[8,256,1280]{2,1,0:T(8,128)S(1)} %get-tuple-element.32, f32[8,256]{1,0:T(8,128)S(1)} %compare_select_fusion, pred[256,1280]{1,0:T(8,128)(4,1)S(1)} %pad_add_fusion), kind=kLoop, calls=%fused_computation.3 | loop fusion | flops 10483712 | bytes 10829824 | tf_op jit(solution)/shard_map/reduce_sum | solution.py:300
  112.7 0.6 pad_maximum_fusion.1.refs_1_
  113.3 15.4 %shard_map.120 = (bf16[64,256]{1,0:T(8,128)(2,1)}, f32[2,256]{1,0:T(2,128)}) custom-call(bf16[8,64,256]{2,1,0:T(8,128)(2,1)} %fusion.12.refs_0_, f32[8,2,256]{2,1,0:T(2,128)} %pad_maximum_fusion.1.refs_1_), custom_call_target="tpu_custom_call" | custom-call | tf_op jit(solution)/shard_map/pallas_call | solution.py:163
  128.7 0.0 copy-done
  128.7 1.3 fusion.6
  130.0 1.5 copy.30
  131.5 18.7 %shard_map.121.refs_0_ = bf16[8,80,256]{2,1,0:T(8,128)(2,1)} custom-call(bf16[8,4,80,256]{3,2,1,0:T(8,128)(2,1)} %bitcast.36), custom_call_target="tpu_custom_call" | custom-call | tf_op jit(solution)/shard_map/pallas_call | solution.py:163
  150.1 15.6 %shard_map.122 = bf16[80,256]{1,0:T(8,128)(2,1)} custom-call(bf16[8,80,256]{2,1,0:T(8,128)(2,1)} %shard_map.121.refs_0_), custom_call_target="tpu_custom_call" | custom-call | tf_op jit(solution)/shard_map/pallas_call | solution.py:163
  165.7 1.4 copy.39
  (19 shorter events, 0.3 us)
Async XLA Ops:
  6.5 122.2 %copy-start = (bf16[64,2560]{1,0:T(8,128)(2,1)S(1)}, bf16[64,2560]{1,0:T(8,128)(2,1)}, u32[]{:S(2)}) copy-start(bf16[64,2560]{1,0:T(8,128)(2,1)} %param.18) | copy-start | bytes 983044
  6.5 53.7 %copy-start.5 = (s32[16]{0:T(128)S(1)}, s32[16]{0:T(128)}, u32[]{:S(2)}) copy-start(s32[16]{0:T(128)} %param.23) | copy-start | bytes 196
  6.5 56.2 %copy-start.3 = (s32[16]{0:T(128)S(1)}, s32[16]{0:T(128)}, u32[]{:S(2)}) copy-start(s32[16]{0:T(128)} %param.21) | copy-start | bytes 196
  6.5 56.2 %copy-start.4 = (s32[16]{0:T(128)S(1)}, s32[16]{0:T(128)}, u32[]{:S(2)}) copy-start(s32[16]{0:T(128)} %param.20) | copy-start | bytes 196
  6.5 60.9 %copy-start.2 = (f32[256]{0:T(256)S(1)}, f32[256]{0:T(256)}, u32[]{:S(2)}) copy-start(f32[256]{0:T(256)} %param.15) | copy-start | bytes 3076
  6.5 61.0 %copy-start.1 = (f32[768]{0:T(1024)S(1)}, f32[768]{0:T(1024)}, u32[]{:S(2)}) copy-start(f32[768]{0:T(1024)} %param.14) | copy-start | bytes 9220
  6.6 66.0 %all-gather.2.cloned.1.call-start = ((), (), s32[]{:S(2)}) async-start(), calls=%async_computation | async-start | bytes 2506752 | tf_op jit(solution)/shard_map/all_gather | solution.py:221
Sparse Core Ops, SparseCore 0:
  9.5 47.9 all-gather.1

commit v20 on v19

--- a/solution.py
+++ b/solution.py
@@ -126,6 +126,8 @@
             total = targets[a][0].astype(jnp.float32)
             for j in range(1, size):
                 total = total + targets[a][j].astype(jnp.float32)
+            if summed == "flip":
+                total = total.T
             results[a][...] = total.astype(results[a].dtype)
     if plan[0][2] == "merge":
         parts, stats = targets[0], targets[1]
@@ -152,7 +154,10 @@
             chunk_shape = x.shape[:axis] + x.shape[axis + 1 :]
             size = x.shape[axis]
             shapes.append(
-                jax.ShapeDtypeStruct(chunk_shape, jnp.bfloat16 if summed == "merge" else summed)
+                jax.ShapeDtypeStruct(
+                    chunk_shape[::-1] if summed == "flip" else chunk_shape,
+                    jnp.bfloat16 if summed in ("merge", "flip") else summed,
+                )
             )
             landings.append(pltpu.VMEM((size,) + chunk_shape, x.dtype))
         else:
@@ -319,8 +324,7 @@
         [("x", False, jnp.bfloat16, 1)],
         3,
     )
-    (summed_out,) = exchange([lane_pieces], [("y", False, jnp.bfloat16)], 5)
-    result = summed_out.T
+    (result,) = exchange([lane_pieces], [("y", False, "flip")], 5)
     return result
 
 

time: 177 us -> 177 us (level)
    unnamed x15 -> x14, local copies, waits for them, and re-layouts: 4.76 us -> 3.36 us
where the time goes in v20:
time: 177 us; the launch traced here: 174 us
  Pallas kernels  123 us (69%)
  between operations  16.3 us (9%)
  local copies, waits for them, and re-layouts  16.1 us (9%)
  matrix products  10.4 us (6%)
  other arithmetic  7.95 us (4%)
    pallas_call x5, Pallas kernels, exchange(): pl.pallas_call(functools.partial(_exchange_kernel, n, plan), out_shape=sh...  123 us
  transfers between devices with their start and end apart: 1, of which 0 were waited for; matrix products, arithmetic and copies ran while one was open for 7% of the time, Pallas kernels for 29%

profile of v20, /device:TPU:6, one launch (start us, length us, event | category | flops | bytes accessed | tf_op | source)
XLA Modules:
  0.0 174.2 jit_solution(13058532358766812958)
XLA Ops:
  6.5 0.0 copy-start
  6.5 0.0 copy-start.5
  6.5 0.0 copy-start.3
  6.5 0.0 copy-start.4
  6.5 0.0 copy-start.2
  6.5 0.0 copy-start.1
  6.6 0.0 all-gather.2.cloned.1.call-start
  6.6 0.7 all-gather.2.cloned.1.call-update
  7.3 1.3 convolution_convert_fusion.2
  8.6 0.3 copy.29
  8.9 1.6 reshape.181.refs_0_
  10.5 49.7 %shard_map.118 = (f32[66,128]{1,0:T(8,128)}, bf16[8,96,768]{2,1,0:T(8,128)(2,1)}) custom-call(bf16[32,66,128]{2,1,0:T(8,128)(2,1)} %reshape.181.refs_0_, bf16[96,768]{1,0:T(8,128)(2,1)} %bitcast.41), custom_call_target="tpu_custom_call" | custom-call | tf_op jit(solution)/shard_map/pallas_call | solution.py:168
  60.2 0.0 copy-done.5
  60.2 0.6 fusion.43
  62.8 0.0 copy-done.3
  62.8 0.0 copy-done.4
  62.8 1.3 fusion.42
  64.6 0.7 fusion.41
  65.3 0.1 select_reduce_fusion
  65.4 0.7 add_compare_fusion
  66.1 0.1 lt.47
  66.2 0.8 reshape.182
  67.1 0.1 multiply_reduce_fusion.1
  67.2 0.1 multiply_reduce_fusion
  67.3 0.1 fusion.39
  67.5 0.0 copy-done.2
  67.5 0.1 multiply_convert_fusion.1
  67.5 0.0 copy-done.1
  67.5 0.1 multiply_convert_fusion
  67.6 0.1 concatenate.22
  67.7 0.7 reshape.183.refs_1_
  68.4 2.5 %copy.36 = bf16[32,8,8,512]{3,2,1,0:T(8,128)(2,1)S(1)} copy(bf16[32,8,8,512]{3,1,2,0:T(8,128)(2,1)} %bitcast.37) | data formatting | bytes 4194304
  71.0 0.6 iota_compare_fusion.2
  71.5 0.6 add_convert_fusion.1
  72.1 0.1 constant_dynamic-slice_fusion.1
  72.2 0.1 multiply_cosine_fusion
  72.4 0.1 pad_add_fusion
  72.5 0.0 all-gather.2.cloned.1.call-done
  72.5 1.6 dynamic-slice_bitcast_fusion.refs_0_
  74.1 23.4 %shard_map.119 = (bf16[4,288,256]{2,1,0:T(8,128)(2,1)}, bf16[32,66,128]{2,1,0:T(8,128)(2,1)}) custom-call(bf16[288,256]{1,0:T(8,128)(2,1)} %dynamic-slice_bitcast_fusion.refs_0_, bf16[66,128]{1,0:T(8,128)(2,1)} %reshape.183.refs_1_), custom_call_target="tpu_custom_call" | custom-call | tf_op jit(solution)/shard_map/pallas_call | solution.py:168
  97.5 2.2 %reshape.185 = bf16[256,1056]{1,0:T(8,128)(2,1)S(1)} reshape(bf16[32,66,128]{2,1,0:T(8,128)(2,1)} %get-tuple-element.22) | data formatting | bytes 1081344 | tf_op jit(solution)/shard_map/reshape | solution.py:232
  99.7 0.8 slice_bitcast_fusion.3
  100.5 1.1 slice_bitcast_fusion
  101.6 1.8 %convolution_bitcast_fusion = f32[8,256,96]{1,2,0:T(8,128)S(1)} fusion(bf16[8,96,768]{2,1,0:T(8,128)(2,1)} %get-tuple-element.23, bf16[256,1056]{1,0:T(8,128)(2,1)S(1)} %reshape.185), kind=kOutput, calls=%fused_computation.17 | convolution fusion | flops 301989888 | bytes 2359296 | tf_op jit(solution)/shard_map/qk,hdk->hqd/dot_general | solution.py:238
  103.4 0.1 copy.32
  103.5 0.2 copy.30
  103.7 0.9 convolution_convert_fusion.1
  104.6 0.1 slice.76
  104.8 2.0 %fusion = (f32[8,256]{1,0:T(8,128)S(1)}, f32[8,256,1280]{2,1,0:T(8,128)S(1)}) fusion(pred[256,1280]{1,0:T(8,128)(4,1)S(1)} %pad_add_fusion, bf16[1280,8,32]{0,2,1:T(8,128)(2,1)S(1)} %broadcast_in_dim.36, bf16[1280,8,64]{0,2,1:T(8,128)(2,1)S(1)} %slice.76, bf16[8,256,16]{1,2,0:T(8,128)(2,1)S(1)} %get-tuple-element.26, ...), kind=kOutput, calls=%fused_computation.2 | convolution fusion | flops 516290560 | bytes 13180928 | tf_op jit(solution)/shard_map/hqd,khd->hqk/dot_general | solution.py:298
  106.8 3.1 %fusion.12.refs_0_ = bf16[8,64,256]{2,1,0:T(8,128)(2,1)} fusion(f32[8,256,1280]{2,1,0:T(8,128)S(1)} %get-tuple-element.32, f32[8,256]{1,0:T(8,128)S(1)} %compare_select_fusion, pred[256,1280]{1,0:T(8,128)(4,1)S(1)} %pad_add_fusion, bf16[1280,8,128]{0,2,1:T(8,128)(2,1)S(1)} %bitcast.34), kind=kOutput, calls=%fused_computation.18 | convolution fusion | flops 346161152 | bytes 12394496 | tf_op jit(solution)/shard_map/hqk,khd->hdq/dot_general | solution.py:307
  110.0 2.7 %fusion.1 = f32[8,256]{1,0:T(8,128)S(1)} fusion(f32[8,256,1280]{2,1,0:T(8,128)S(1)} %get-tuple-element.32, f32[8,256]{1,0:T(8,128)S(1)} %compare_select_fusion, pred[256,1280]{1,0:T(8,128)(4,1)S(1)} %pad_add_fusion), kind=kLoop, calls=%fused_computation.3 | loop fusion | flops 10483712 | bytes 10829824 | tf_op jit(solution)/shard_map/reduce_sum | solution.py:305
  112.7 0.6 pad_maximum_fusion.1.refs_1_
  113.3 15.4 %shard_map.120 = (bf16[64,256]{1,0:T(8,128)(2,1)}, f32[2,256]{1,0:T(2,128)}) custom-call(bf16[8,64,256]{2,1,0:T(8,128)(2,1)} %fusion.12.refs_0_, f32[8,2,256]{2,1,0:T(2,128)} %pad_maximum_fusion.1.refs_1_), custom_call_target="tpu_custom_call" | custom-call | tf_op jit(solution)/shard_map/pallas_call | solution.py:168
  128.7 0.0 copy-done
  128.7 1.3 fusion.6
  130.0 1.5 copy.33
  131.5 18.7 %shard_map.121.refs_0_ = bf16[8,80,256]{2,1,0:T(8,128)(2,1)} custom-call(bf16[8,4,80,256]{3,2,1,0:T(8,128)(2,1)} %bitcast.35), custom_call_target="tpu_custom_call" | custom-call | tf_op jit(solution)/shard_map/pallas_call | solution.py:168
  150.1 15.7 %shard_map.122 = bf16[256,80]{1,0:T(8,128)(2,1)} custom-call(bf16[8,80,256]{2,1,0:T(8,128)(2,1)} %shard_map.121.refs_0_), custom_call_target="tpu_custom_call" | custom-call | tf_op jit(solution)/shard_map/pallas_call | solution.py:168
  165.8 1.5 copy.34
  (19 shorter events, 0.3 us)
Async XLA Ops:
  6.5 122.2 %copy-start = (bf16[64,2560]{1,0:T(8,128)(2,1)S(1)}, bf16[64,2560]{1,0:T(8,128)(2,1)}, u32[]{:S(2)}) copy-start(bf16[64,2560]{1,0:T(8,128)(2,1)} %param.18) | copy-start | bytes 983044
  6.5 53.7 %copy-start.5 = (s32[16]{0:T(128)S(1)}, s32[16]{0:T(128)}, u32[]{:S(2)}) copy-start(s32[16]{0:T(128)} %param.23) | copy-start | bytes 196
  6.5 56.2 %copy-start.3 = (s32[16]{0:T(128)S(1)}, s32[16]{0:T(128)}, u32[]{:S(2)}) copy-start(s32[16]{0:T(128)} %param.21) | copy-start | bytes 196
  6.5 56.2 %copy-start.4 = (s32[16]{0:T(128)S(1)}, s32[16]{0:T(128)}, u32[]{:S(2)}) copy-start(s32[16]{0:T(128)} %param.20) | copy-start | bytes 196
  6.5 60.9 %copy-start.2 = (f32[256]{0:T(256)S(1)}, f32[256]{0:T(256)}, u32[]{:S(2)}) copy-start(f32[256]{0:T(256)} %param.15) | copy-start | bytes 3076
  6.5 61.0 %copy-start.1 = (f32[768]{0:T(1024)S(1)}, f32[768]{0:T(1024)}, u32[]{:S(2)}) copy-start(f32[768]{0:T(1024)} %param.14) | copy-start | bytes 9220
  6.6 66.0 %all-gather.2.cloned.1.call-start = ((), (), s32[]{:S(2)}) async-start(), calls=%async_computation | async-start | bytes 2506752 | tf_op jit(solution)/shard_map/all_gather | solution.py:226
Sparse Core Ops, SparseCore 0:
  9.5 47.9 all-gather.1
